TPU v7x, 32 devices: a whole 2x2x4 slice. The times are simulated.
32 devices in a mesh: grp: 2 (over core), dp: 8 (over z, x), seq: 2 (over y).
Axes of the slice: x: 2, y: 2, z: 4, core: 2. Of those that a mesh axis runs over, the one named last changes fastest.
Arguments:
- tokens: bfloat16 [16, 2048, 1024], P(('grp', 'dp'), 'seq'), may hold values from -6 to 6
- cotangent: bfloat16 [16, 2048, 1024], P(('grp', 'dp'), 'seq'), may hold values from -6 to 6
- segments: int32 [16, 2048], P(('grp', 'dp')), may hold values from 0 to 3, never falling along the last dimension, each value on 1 to 1024 neighbouring positions
- weight_qkv: float32 [1024, 3072], P(('dp', 'seq')), may hold values from -0.1875 to 0.1875
- weight_out: float32 [1024, 1024], P(('dp', 'seq')), may hold values from -3 to 3
- weight_ffn: float32 [2, 1024, 4096], P(None, ('dp', 'seq')), may hold values from -0.1875 to 0.1875
- vectors: float32 [12288], P(('dp', 'seq')), may hold values from -1.5 to 1.5
- first_qkv: float32 [2, 1024, 3072], P('grp', ('dp', 'seq')), may hold values from -32 to 32
- first_out: float32 [2, 1024, 1024], P('grp', ('dp', 'seq')), may hold values from -32 to 32
- first_ffn: float32 [2, 2, 1024, 4096], P('grp', None, ('dp', 'seq')), may hold values from -32 to 32
- first_vec: float32 [2, 12288], P('grp', ('dp', 'seq')), may hold values from -32 to 32
- second_qkv: float32 [2, 1024, 3072], P('grp', ('dp', 'seq')), may hold values from 16.384 to 163.84
- second_out: float32 [2, 1024, 1024], P('grp', ('dp', 'seq')), may hold values from 0.8192 to 8.192
- second_ffn: float32 [2, 2, 1024, 4096], P('grp', None, ('dp', 'seq')), may hold values from 16.384 to 163.84
- second_vec: float32 [2, 12288], P('grp', ('dp', 'seq')), may hold values from 16.384 to 163.84
- outer_qkv: float32 [1024, 3072], P(('dp', 'seq')), may hold values from -0.0625 to 0.0625
- outer_out: float32 [1024, 1024], P(('dp', 'seq')), may hold values from -0.625 to 0.625
- outer_ffn: float32 [2, 1024, 4096], P(None, ('dp', 'seq')), may hold values from -0.03125 to 0.03125
- outer_vec: float32 [12288], P(('dp', 'seq')), may hold values from -0.625 to 0.625
Outputs:
- result: bfloat16 [16, 2048, 1024], P(('grp', 'dp'), 'seq')
- input_grad: float32 [16, 2048, 1024], P(('grp', 'dp'), 'seq')
- grad_qkv: float32 [2, 1024, 3072], P('grp', ('dp', 'seq'))
- grad_out: float32 [2, 1024, 1024], P('grp', ('dp', 'seq'))
- grad_ffn: float32 [2, 2, 1024, 4096], P('grp', None, ('dp', 'seq'))
- grad_vec: float32 [2, 12288], P('grp', ('dp', 'seq'))
- new_first_qkv: float32 [2, 1024, 3072], P('grp', ('dp', 'seq'))
- new_first_out: float32 [2, 1024, 1024], P('grp', ('dp', 'seq'))
- new_first_ffn: float32 [2, 2, 1024, 4096], P('grp', None, ('dp', 'seq'))
- new_first_vec: float32 [2, 12288], P('grp', ('dp', 'seq'))
- new_second_qkv: float32 [2, 1024, 3072], P('grp', ('dp', 'seq'))
- new_second_out: float32 [2, 1024, 1024], P('grp', ('dp', 'seq'))
- new_second_ffn: float32 [2, 2, 1024, 4096], P('grp', None, ('dp', 'seq'))
- new_second_vec: float32 [2, 12288], P('grp', ('dp', 'seq'))
- delta_qkv: float32 [1024, 3072], P(('dp', 'seq'))
- delta_out: float32 [1024, 1024], P(('dp', 'seq'))
- delta_ffn: float32 [2, 1024, 4096], P(None, ('dp', 'seq'))
- delta_vec: float32 [12288], P(('dp', 'seq'))
- momentum_qkv: float32 [1024, 3072], P(('dp', 'seq'))
- momentum_out: float32 [1024, 1024], P(('dp', 'seq'))
- momentum_ffn: float32 [2, 1024, 4096], P(None, ('dp', 'seq'))
- momentum_vec: float32 [12288], P(('dp', 'seq'))
- master_qkv: float32 [1024, 3072], P(('dp', 'seq'))
- master_out: float32 [1024, 1024], P(('dp', 'seq'))
- master_ffn: float32 [2, 1024, 4096], P(None, ('dp', 'seq'))
- master_vec: float32 [12288], P(('dp', 'seq'))
Inputs may be any that keep to these rules, and one draw needn't show every extreme that they name: `segments`: along each sequence the ids never fall; every id appears, each in a run of 1 to 1024 positions.
All inputs are finite; a program needn't handle non-finite values.
Results may differ from a plain program's by a relative error of at most 0.023.
The roundings to bfloat16 on the way count: a program that leaves them out, or rounds other values in their place, can miss the bound.
Values may be sent and summed in bfloat16 or wider, within the bound.
A program may use at most 256 MiB of HBM per device.

v0:
```python
from functools import partial

import jax
import jax.numpy as jnp
from jax import lax
from jax.sharding import PartitionSpec as P

HD = 64
W = 512
QB = 512


beta_one = 0.9
beta_two = 0.95
adam_eps = 1e-08
weight_decay = 0.1
bias_one = 1.0 - 0.9**10
bias_two = 1.0 - 0.95**10
step_rates = (0.01, 0.1, 0.005, 0.2)
outer_rate = 0.7
outer_beta = 0.9
norm_eps = 1e-05
score_fill = -1e30


def partner(x, axis, stride):
    return lax.ppermute(x, axis, [(i, i ^ 1 << stride) for i in range(lax.axis_size(axis))])


def layer_norm(residue, norm_gain, norm_shift):
    average = jnp.mean(residue, axis=-1, keepdims=True)
    centred = residue - average
    variance = jnp.mean(centred * centred, axis=-1, keepdims=True)
    return centred * lax.rsqrt(variance + norm_eps) * norm_gain + norm_shift


def head_scores(block_query, block_keys, allowed):
    query_heads = block_query.reshape(block_query.shape[0], -1, HD)
    key_heads = block_keys.reshape(block_keys.shape[0], -1, HD)
    scores = jnp.einsum(
        "qhd,khd->hqk", query_heads, key_heads, preferred_element_type=jnp.float32
    ) * HD ** (-0.5)
    return (jnp.where(allowed[None], scores, score_fill), query_heads, key_heads)


def adam_step(master, gradient, first, second, step_rate):
    first_new = beta_one * first + (1.0 - beta_one) * gradient
    second_new = beta_two * second + (1.0 - beta_two) * gradient * gradient
    direction = first_new / bias_one / (jnp.sqrt(second_new / bias_two) + adam_eps)
    return (master - step_rate * (direction + weight_decay * master), first_new, second_new)


def on_device(
    tokens,
    cotangent,
    segments,
    weight_qkv,
    weight_out,
    weight_ffn,
    vectors,
    first_qkv,
    first_out,
    first_ffn,
    first_vec,
    second_qkv,
    second_out,
    second_ffn,
    second_vec,
    outer_qkv,
    outer_out,
    outer_ffn,
    outer_vec,
):
    masters = (weight_qkv, weight_out, weight_ffn, vectors)
    lowered = [master.astype(jnp.bfloat16) for master in masters]
    gathered = (
        lax.all_gather(lowered[0], ("dp", "seq"), axis=0, tiled=True),
        lax.all_gather(lowered[1], ("dp", "seq"), axis=0, tiled=True),
        lax.all_gather(lowered[2], ("dp", "seq"), axis=1, tiled=True),
        lax.all_gather(lowered[3], ("dp", "seq"), axis=0, tiled=True),
    )
    full_qkv, full_out, full_ffn, full_vec = gathered
    width = full_out.shape[0]
    vector_values = full_vec.astype(jnp.float32)
    pieces = [vector_values[position * width : (position + 1) * width] for position in range(8)]
    (
        bias_query,
        bias_value,
        bias_output,
        bias_second,
        gain_first,
        shift_first,
        gain_second,
        shift_second,
    ) = pieces
    bias_hidden = vector_values[8 * width :]
    token_rows = tokens[0]
    local_rows = token_rows.shape[0]
    side = lax.axis_index("seq")
    is_first = side == 0
    joined_bias = jnp.concatenate([bias_query, jnp.zeros_like(bias_query), bias_value])
    projected = (
        jnp.dot(token_rows, full_qkv, preferred_element_type=jnp.float32) + joined_bias
    ).astype(jnp.bfloat16)
    queries = projected[:, :width]
    keys_local = projected[:, width : 2 * width]
    values_local = projected[:, 2 * width :]
    send_keys = jnp.where(is_first, keys_local[local_rows - W :], keys_local[:W])
    send_values = jnp.where(is_first, values_local[local_rows - W :], values_local[:W])
    got_keys, got_values = partner((send_keys, send_values), "seq", 0)
    empty_rows = jnp.zeros_like(send_keys)
    keys_wide = jnp.concatenate(
        [
            jnp.where(is_first, empty_rows, got_keys),
            keys_local,
            jnp.where(is_first, got_keys, empty_rows),
        ],
        axis=0,
    )
    values_wide = jnp.concatenate(
        [
            jnp.where(is_first, empty_rows, got_values),
            values_local,
            jnp.where(is_first, got_values, empty_rows),
        ],
        axis=0,
    )
    segment_row = segments[0]
    filler = jnp.full((W,), -1, jnp.int32)
    segment_padded = jnp.concatenate([filler, segment_row, filler])
    segment_query = lax.dynamic_slice_in_dim(segment_row, side * local_rows, local_rows, 0)
    segment_keys = lax.dynamic_slice_in_dim(
        segment_padded, side * local_rows, local_rows + 2 * W, 0
    )
    span = QB + 2 * W
    distance = jnp.arange(span, dtype=jnp.int32)[None, :] - jnp.arange(QB, dtype=jnp.int32)[:, None]
    band = (distance >= 0) & (distance <= 2 * W)
    offsets = jnp.arange(local_rows // QB, dtype=jnp.int32) * QB
    groups = width // 128
    columns = jnp.arange(groups, dtype=jnp.int32) * 128

    def block_allowed(offset):
        near_query = lax.dynamic_slice_in_dim(segment_query, offset, QB, 0)
        near_keys = lax.dynamic_slice_in_dim(segment_keys, offset, span, 0)
        return band & (near_query[:, None] == near_keys[None, :])

    def group_forward(column):
        query_group = lax.dynamic_slice_in_dim(queries, column, 128, 1)
        key_group = lax.dynamic_slice_in_dim(keys_wide, column, 128, 1)
        value_group = lax.dynamic_slice_in_dim(values_wide, column, 128, 1)

        def block_forward(offset):
            scores, query_heads, key_heads = head_scores(
                lax.dynamic_slice_in_dim(query_group, offset, QB, 0),
                lax.dynamic_slice_in_dim(key_group, offset, span, 0),
                block_allowed(offset),
            )
            maximum = jnp.max(scores, axis=-1, keepdims=True)
            exponent = jnp.exp(scores - maximum)
            denominator = jnp.sum(exponent, axis=-1, keepdims=True)
            weights = (exponent / denominator).astype(jnp.bfloat16)
            value_heads = lax.dynamic_slice_in_dim(value_group, offset, span, 0).reshape(
                span, -1, HD
            )
            mixed = jnp.einsum(
                "hqk,khd->qhd", weights, value_heads, preferred_element_type=jnp.float32
            )
            return (
                mixed.reshape(QB, 128).astype(jnp.bfloat16),
                (maximum + jnp.log(denominator))[..., 0],
            )

        return lax.map(block_forward, offsets)

    mixed_groups, logsum = lax.map(group_forward, columns)
    attended = jnp.transpose(mixed_groups.reshape(groups, local_rows, 128), (1, 0, 2)).reshape(
        local_rows, width
    )
    branch = jnp.dot(attended, full_out, preferred_element_type=jnp.float32) + bias_output
    residue_first = token_rows.astype(jnp.float32) + branch
    hidden_in, first_pullback = jax.vjp(layer_norm, residue_first, gain_first, shift_first)
    hidden_low = hidden_in.astype(jnp.bfloat16)
    inner = jnp.dot(hidden_low, full_ffn[0], preferred_element_type=jnp.float32) + bias_hidden
    activated, gelu_pullback = jax.vjp(partial(jax.nn.gelu, approximate=False), inner)
    activated_low = activated.astype(jnp.bfloat16)
    second_branch = (
        lax.dot_general(
            activated_low, full_ffn[1], (((1,), (1,)), ((), ())), preferred_element_type=jnp.float32
        )
        + bias_second
    )
    residue_second = hidden_in + second_branch
    result, second_pullback = jax.vjp(layer_norm, residue_second, gain_second, shift_second)
    upstream = cotangent[0].astype(jnp.float32)
    residue_second_grad, gain_second_grad, shift_second_grad = second_pullback(upstream)
    branch_two_low = residue_second_grad.astype(jnp.bfloat16)
    bias_second_grad = jnp.sum(branch_two_low.astype(jnp.float32), axis=0)
    down_grad = lax.dot_general(
        branch_two_low, activated_low, (((0,), (0,)), ((), ())), preferred_element_type=jnp.float32
    )
    activated_grad = jnp.dot(branch_two_low, full_ffn[1], preferred_element_type=jnp.float32)
    (inner_grad,) = gelu_pullback(activated_grad)
    inner_low = inner_grad.astype(jnp.bfloat16)
    bias_hidden_grad = jnp.sum(inner_low.astype(jnp.float32), axis=0)
    up_grad = lax.dot_general(
        hidden_low, inner_low, (((0,), (0,)), ((), ())), preferred_element_type=jnp.float32
    )
    hidden_grad = residue_second_grad + lax.dot_general(
        inner_low, full_ffn[0], (((1,), (1,)), ((), ())), preferred_element_type=jnp.float32
    )
    residue_first_grad, gain_first_grad, shift_first_grad = first_pullback(hidden_grad)
    branch_low = residue_first_grad.astype(jnp.bfloat16)
    bias_output_grad = jnp.sum(branch_low.astype(jnp.float32), axis=0)
    out_weight_grad = lax.dot_general(
        attended, branch_low, (((0,), (0,)), ((), ())), preferred_element_type=jnp.float32
    )
    mixed_grad = lax.dot_general(
        branch_low, full_out, (((1,), (1,)), ((), ())), preferred_element_type=jnp.float32
    ).astype(jnp.bfloat16)

    def group_backward(group_item):
        column, logsum_group = group_item
        query_group = lax.dynamic_slice_in_dim(queries, column, 128, 1)
        key_group = lax.dynamic_slice_in_dim(keys_wide, column, 128, 1)
        value_group = lax.dynamic_slice_in_dim(values_wide, column, 128, 1)
        outgrad_group = lax.dynamic_slice_in_dim(mixed_grad, column, 128, 1)

        def block_backward(carried, block_item):
            offset, logsum_block = block_item
            key_running, value_running = carried
            scores, query_heads, key_heads = head_scores(
                lax.dynamic_slice_in_dim(query_group, offset, QB, 0),
                lax.dynamic_slice_in_dim(key_group, offset, span, 0),
                block_allowed(offset),
            )
            probs = jnp.exp(scores - logsum_block[..., None])
            value_heads = lax.dynamic_slice_in_dim(value_group, offset, span, 0).reshape(
                span, -1, HD
            )
            outgrad_heads = lax.dynamic_slice_in_dim(outgrad_group, offset, QB, 0).reshape(
                QB, -1, HD
            )
            prob_grad = jnp.einsum(
                "qhd,khd->hqk", outgrad_heads, value_heads, preferred_element_type=jnp.float32
            )
            row_inner = jnp.sum(probs * prob_grad, axis=-1, keepdims=True)
            score_grad = (probs * (prob_grad - row_inner)).astype(jnp.bfloat16)
            query_grad = jnp.einsum(
                "hqk,khd->qhd", score_grad, key_heads, preferred_element_type=jnp.float32
            ).reshape(QB, 128) * HD ** (-0.5)
            key_grad = jnp.einsum(
                "hqk,qhd->khd", score_grad, query_heads, preferred_element_type=jnp.float32
            ).reshape(span, 128) * HD ** (-0.5)
            value_grad = jnp.einsum(
                "hqk,qhd->khd",
                probs.astype(jnp.bfloat16),
                outgrad_heads,
                preferred_element_type=jnp.float32,
            ).reshape(span, 128)
            key_running = lax.dynamic_update_slice_in_dim(
                key_running,
                lax.dynamic_slice_in_dim(key_running, offset, span, 0) + key_grad,
                offset,
                0,
            )
            value_running = lax.dynamic_update_slice_in_dim(
                value_running,
                lax.dynamic_slice_in_dim(value_running, offset, span, 0) + value_grad,
                offset,
                0,
            )
            return ((key_running, value_running), query_grad)

        start_totals = (
            jnp.zeros((local_rows + 2 * W, 128), jnp.float32),
            jnp.zeros((local_rows + 2 * W, 128), jnp.float32),
        )
        (key_running, value_running), query_blocks = lax.scan(
            block_backward, start_totals, (offsets, logsum_group)
        )
        return (query_blocks, key_running, value_running)

    query_parts, key_parts, value_parts = lax.map(group_backward, (columns, logsum))
    query_grad_all = jnp.transpose(query_parts.reshape(groups, local_rows, 128), (1, 0, 2)).reshape(
        local_rows, width
    )
    key_wide_grad = jnp.transpose(key_parts, (1, 0, 2)).reshape(local_rows + 2 * W, width)
    value_wide_grad = jnp.transpose(value_parts, (1, 0, 2)).reshape(local_rows + 2 * W, width)
    send_key_grad = jnp.where(is_first, key_wide_grad[W + local_rows :], key_wide_grad[:W])
    send_value_grad = jnp.where(is_first, value_wide_grad[W + local_rows :], value_wide_grad[:W])
    back_keys, back_values = (
        partner(send_key_grad.astype(jnp.bfloat16), "seq", 0).astype(send_key_grad.dtype),
        partner(send_value_grad.astype(jnp.bfloat16), "seq", 0).astype(send_value_grad.dtype),
    )
    spacer = jnp.zeros((local_rows - W, width), jnp.float32)
    key_grad_all = key_wide_grad[W : W + local_rows] + jnp.where(
        is_first,
        jnp.concatenate([spacer, back_keys], axis=0),
        jnp.concatenate([back_keys, spacer], axis=0),
    )
    value_grad_all = value_wide_grad[W : W + local_rows] + jnp.where(
        is_first,
        jnp.concatenate([spacer, back_values], axis=0),
        jnp.concatenate([back_values, spacer], axis=0),
    )
    projected_grad = jnp.concatenate([query_grad_all, key_grad_all, value_grad_all], axis=1).astype(
        jnp.bfloat16
    )
    qkv_weight_grad = lax.dot_general(
        token_rows, projected_grad, (((0,), (0,)), ((), ())), preferred_element_type=jnp.float32
    )
    projected_sums = jnp.sum(projected_grad.astype(jnp.float32), axis=0)
    input_grad = residue_first_grad + lax.dot_general(
        projected_grad, full_qkv, (((1,), (1,)), ((), ())), preferred_element_type=jnp.float32
    )
    vector_grad = jnp.concatenate(
        [
            projected_sums[:width],
            projected_sums[2 * width :],
            bias_output_grad,
            bias_second_grad,
            gain_first_grad,
            shift_first_grad,
            gain_second_grad,
            shift_second_grad,
            bias_hidden_grad,
        ]
    )
    ffn_grad = jnp.stack([up_grad, down_grad])
    summed = (
        lax.psum_scatter(qkv_weight_grad, ("dp", "seq"), scatter_dimension=0, tiled=True),
        lax.psum_scatter(out_weight_grad, ("dp", "seq"), scatter_dimension=0, tiled=True),
        lax.psum_scatter(ffn_grad, ("dp", "seq"), scatter_dimension=1, tiled=True),
        lax.psum_scatter(vector_grad, ("dp", "seq"), scatter_dimension=0, tiled=True),
    )
    firsts = (first_qkv[0], first_out[0], first_ffn[0], first_vec[0])
    seconds = (second_qkv[0], second_out[0], second_ffn[0], second_vec[0])
    outers = (outer_qkv, outer_out, outer_ffn, outer_vec)
    stepped = [
        adam_step(
            masters[member], summed[member], firsts[member], seconds[member], step_rates[member]
        )
        for member in range(4)
    ]
    changes = [masters[member] - stepped[member][0] for member in range(4)]
    added = (
        lax.psum(changes[0].astype(jnp.bfloat16), "grp").astype(jnp.float32),
        lax.psum(changes[1].astype(jnp.bfloat16), "grp").astype(jnp.float32),
        lax.psum(changes[2].astype(jnp.bfloat16), "grp").astype(jnp.float32),
        lax.psum(changes[3].astype(jnp.bfloat16), "grp").astype(jnp.float32),
    )
    replicas = lax.axis_size("grp")
    deltas = [added[member] / replicas for member in range(4)]
    momenta = [outer_beta * outers[member] + deltas[member] for member in range(4)]
    renewed = [
        masters[member] - outer_rate * (deltas[member] + outer_beta * momenta[member])
        for member in range(4)
    ]
    return (
        result.astype(jnp.bfloat16)[None],
        input_grad[None],
        summed[0][None],
        summed[1][None],
        summed[2][None],
        summed[3][None],
        stepped[0][1][None],
        stepped[1][1][None],
        stepped[2][1][None],
        stepped[3][1][None],
        stepped[0][2][None],
        stepped[1][2][None],
        stepped[2][2][None],
        stepped[3][2][None],
        deltas[0],
        deltas[1],
        deltas[2],
        deltas[3],
        momenta[0],
        momenta[1],
        momenta[2],
        momenta[3],
        renewed[0],
        renewed[1],
        renewed[2],
        renewed[3],
    )


def solution(mesh):
    return jax.shard_map(
        on_device,
        mesh=mesh,
        in_specs=(
            P(("grp", "dp"), "seq", None),
            P(("grp", "dp"), "seq", None),
            P(("grp", "dp"), None),
            P(("dp", "seq"), None),
            P(("dp", "seq"), None),
            P(None, ("dp", "seq"), None),
            P(("dp", "seq")),
            P("grp", ("dp", "seq"), None),
            P("grp", ("dp", "seq"), None),
            P("grp", None, ("dp", "seq"), None),
            P("grp", ("dp", "seq")),
            P("grp", ("dp", "seq"), None),
            P("grp", ("dp", "seq"), None),
            P("grp", None, ("dp", "seq"), None),
            P("grp", ("dp", "seq")),
            P(("dp", "seq"), None),
            P(("dp", "seq"), None),
            P(None, ("dp", "seq"), None),
            P(("dp", "seq")),
        ),
        out_specs=(
            P(("grp", "dp"), "seq", None),
            P(("grp", "dp"), "seq", None),
            P("grp", ("dp", "seq"), None),
            P("grp", ("dp", "seq"), None),
            P("grp", None, ("dp", "seq"), None),
            P("grp", ("dp", "seq")),
            P("grp", ("dp", "seq"), None),
            P("grp", ("dp", "seq"), None),
            P("grp", None, ("dp", "seq"), None),
            P("grp", ("dp", "seq")),
            P("grp", ("dp", "seq"), None),
            P("grp", ("dp", "seq"), None),
            P("grp", None, ("dp", "seq"), None),
            P("grp", ("dp", "seq")),
            P(("dp", "seq"), None),
            P(("dp", "seq"), None),
            P(None, ("dp", "seq"), None),
            P(("dp", "seq")),
            P(("dp", "seq"), None),
            P(("dp", "seq"), None),
            P(None, ("dp", "seq"), None),
            P(("dp", "seq")),
            P(("dp", "seq"), None),
            P(("dp", "seq"), None),
            P(None, ("dp", "seq"), None),
            P(("dp", "seq")),
        ),
        check_vma=False,
    )
```

profile of v0, /device:TPU:0, one launch (start us, length us, event | category | flops | bytes accessed | tf_op | source)
XLA Modules:
  0.0 2311.8 jit_solution(17575086352308015595)
XLA Ops:
  11.6 43.3 %all-gather = bf16[16,1,768]{2,1,0:T(2,128)(2,1)S(1)} all-gather(bf16[1,1,768]{2,1,0:T(2,128)(2,1)S(1)} %reshape.308), channel_id=1, replica_groups=mesh['grp'=2,'dp'=8,'seq'=2] {'dp','seq'}, dimensions={0}, use_global_device_ids=true | all-gather | bytes 26112 | tf_op jit(solution)/shard_map/all_gather | solution.py:80
  55.6 52.3 %all-gather.5.cloned.1.call-done = bf16[1024,3072]{1,0:T(8,128)(2,1)} async-done(((bf16[64,3072]{1,0:T(8,128)(2,1)}), bf16[1024,3072]{1,0:T(8,128)(2,1)}) %all-gather.5.cloned.1.call-update) | async-done | bytes 6291472 | tf_op jit(solution)/shard_map/all_gather | solution.py:77
  107.9 9.4 add_convert_fusion.1
  132.5 5.7 fusion.70
  140.8 9.0 collective-permute-done
  151.2 26.1 %collective-permute-done.1 = bf16[512,1024]{1,0:T(8,128)(2,1)} collective-permute-done((bf16[512,1024]{1,0:T(8,128)(2,1)}, bf16[512,1024]{1,0:T(8,128)(2,1)}, u32[]{:S(2)}, u32[]{:S(2)}) %collective-permute-start.1) | collective-permute-done | bytes 1048608 | tf_op jit(solution)/shard_map/ppermute | solution.py:27
  182.6 6.6 copy.132
  189.2 6.6 copy.133
  195.8 224.0 %while.57 = (s32[]{:T(128)}, bf16[8,2,512,128]{3,2,1,0:T(8,128)(2,1)}, f32[8,2,2,512]{3,2,1,0:T(2,128)}, s32[8]{0:T(128)S(1)}, bf16[1024,1024]{0,1:T(8,128)(2,1)...) while((s32[]{:T(128)}, ...), condition=%wide.region_5.6_spmd.clone, body=%wide.region_0.5_spmd.clone.sunk | while | flops 426310656 | bytes 30483016 | solution.py:175
  201.2 21.1 while.60
  229.1 21.1 while.60
  257.1 21.1 while.60
  285.1 21.1 while.60
  313.1 21.1 while.60
  341.2 21.1 while.60
  369.2 21.1 while.60
  397.1 21.1 while.60
  424.4 4.8 fusion.72
  432.2 48.0 %multiply_convert_fusion.1 = (bf16[1024,4096]{1,0:T(8,128)(2,1)}, f32[1024,4096]{1,0:T(8,128)}, f32[1024,4096]{1,0:T(8,128)}) fusion(f32[4096]{0:T(1024)S(1)} %copy-done.59, bf16[2,1024,4096]{2,1,0:T(8,128)(2,1)} %all-gather.9.cloned.1.call-done, bf16[1024,1024]{0,1:T(8,128)(2,1)S(1)} %fusion.65.clone.5), kind=kOutput, calls=%fused_computation.63 | convolution fusion | flops 8866758656 | bytes 52445184 | tf_op jit(solution)/shard_map/dot_general | solution.py:183
  480.2 14.5 fusion.73
  503.1 25.5 %convert_reduce_fusion = (f32[4096]{0:T(1024)}, bf16[1024,4096]{1,0:T(8,128)(2,1)}) fusion(f32[1024,4096]{1,0:T(8,128)} %get-tuple-element.644, bf16[1024,1024]{0,1:T(8,128)(2,1)} %get-tuple-element.638, bf16[2,1024,4096]{2,1,0:T(8,128)(2,1)} %all-gather.9.cloned.1.call-done, f32[1024,4096]{1,0:T(8,128)} %get-tuple-element.691, f32[4096]{0:T(1024)S(1)} %copy-done.59), kind=kOutput, calls=%fused_computation.61 | convolution fusion | flops 8661233664 | bytes 52461568 | tf_op jit(solution)/shard_map/dot_general | solution.py:201
  528.7 18.0 multiply_reduce_fusion.1
  557.6 5.3 convolution_convert_fusion
  562.9 649.8 %while.59 = (s32[]{:T(128)}, bf16[8,2,512,128]{3,2,1,0:T(8,128)(2,1)}, f32[8,2048,128]{1,2,0:T(8,128)}, f32[8,2048,128]{1,2,0:T(8,128)}, f32[8,2,2,512]{3,2,1,0:...) while((s32[]{:T(128)}, ...), condition=%wide.region_18.19_spmd.clone, body=%wide.region_14.18_spmd.clone.sunk | while | flops 1026227200 | bytes 83686184 | solution.py:283
  578.7 61.0 %while.61 = (s32[]{:T(128)}, f32[2048,128]{0,1:T(8,128)}, f32[2048,128]{0,1:T(8,128)}, bf16[2,512,128]{1,2,0:T(8,128)(2,1)}, s32[2]{0:T(128)}, /*index=5*/bf16[1...) while((s32[]{:T(128)}, f32[2048,128]{0,1:T(8,128)}, ...), condition=%wide.region_17.17_spmd, body=%wide.region_15.16_spmd.sunk | while | flops 1023081472 | bytes 72397168 | solution.py:278
  598.6 4.6 dynamic_update_slice.64
  603.3 4.7 dynamic_update_slice.65
  659.9 61.0 %while.61 = (s32[]{:T(128)}, f32[2048,128]{0,1:T(8,128)}, f32[2048,128]{0,1:T(8,128)}, bf16[2,512,128]{1,2,0:T(8,128)(2,1)}, s32[2]{0:T(128)}, /*index=5*/bf16[1...) while((s32[]{:T(128)}, f32[2048,128]{0,1:T(8,128)}, ...), condition=%wide.region_17.17_spmd, body=%wide.region_15.16_spmd.sunk | while | flops 1023081472 | bytes 72397168 | solution.py:278
  679.9 4.6 dynamic_update_slice.64
  684.5 4.7 dynamic_update_slice.65
  741.1 61.0 %while.61 = (s32[]{:T(128)}, f32[2048,128]{0,1:T(8,128)}, f32[2048,128]{0,1:T(8,128)}, bf16[2,512,128]{1,2,0:T(8,128)(2,1)}, s32[2]{0:T(128)}, /*index=5*/bf16[1...) while((s32[]{:T(128)}, f32[2048,128]{0,1:T(8,128)}, ...), condition=%wide.region_17.17_spmd, body=%wide.region_15.16_spmd.sunk | while | flops 1023081472 | bytes 72397168 | solution.py:278
  761.0 4.6 dynamic_update_slice.64
  765.6 4.7 dynamic_update_slice.65
  822.2 61.0 %while.61 = (s32[]{:T(128)}, f32[2048,128]{0,1:T(8,128)}, f32[2048,128]{0,1:T(8,128)}, bf16[2,512,128]{1,2,0:T(8,128)(2,1)}, s32[2]{0:T(128)}, /*index=5*/bf16[1...) while((s32[]{:T(128)}, f32[2048,128]{0,1:T(8,128)}, ...), condition=%wide.region_17.17_spmd, body=%wide.region_15.16_spmd.sunk | while | flops 1023081472 | bytes 72397168 | solution.py:278
  842.2 4.6 dynamic_update_slice.64
  846.8 4.7 dynamic_update_slice.65
  903.4 61.0 %while.61 = (s32[]{:T(128)}, f32[2048,128]{0,1:T(8,128)}, f32[2048,128]{0,1:T(8,128)}, bf16[2,512,128]{1,2,0:T(8,128)(2,1)}, s32[2]{0:T(128)}, /*index=5*/bf16[1...) while((s32[]{:T(128)}, f32[2048,128]{0,1:T(8,128)}, ...), condition=%wide.region_17.17_spmd, body=%wide.region_15.16_spmd.sunk | while | flops 1023081472 | bytes 72397168 | solution.py:278
  923.4 4.6 dynamic_update_slice.64
  928.0 4.7 dynamic_update_slice.65
  984.6 61.0 %while.61 = (s32[]{:T(128)}, f32[2048,128]{0,1:T(8,128)}, f32[2048,128]{0,1:T(8,128)}, bf16[2,512,128]{1,2,0:T(8,128)(2,1)}, s32[2]{0:T(128)}, /*index=5*/bf16[1...) while((s32[]{:T(128)}, f32[2048,128]{0,1:T(8,128)}, ...), condition=%wide.region_17.17_spmd, body=%wide.region_15.16_spmd.sunk | while | flops 1023081472 | bytes 72397168 | solution.py:278
  1004.5 4.6 dynamic_update_slice.64
  1009.1 4.7 dynamic_update_slice.65
  1065.7 61.0 %while.61 = (s32[]{:T(128)}, f32[2048,128]{0,1:T(8,128)}, f32[2048,128]{0,1:T(8,128)}, bf16[2,512,128]{1,2,0:T(8,128)(2,1)}, s32[2]{0:T(128)}, /*index=5*/bf16[1...) while((s32[]{:T(128)}, f32[2048,128]{0,1:T(8,128)}, ...), condition=%wide.region_17.17_spmd, body=%wide.region_15.16_spmd.sunk | while | flops 1023081472 | bytes 72397168 | solution.py:278
  1090.3 4.7 dynamic_update_slice.65
  1146.7 61.0 %while.61 = (s32[]{:T(128)}, f32[2048,128]{0,1:T(8,128)}, f32[2048,128]{0,1:T(8,128)}, bf16[2,512,128]{1,2,0:T(8,128)(2,1)}, s32[2]{0:T(128)}, /*index=5*/bf16[1...) while((s32[]{:T(128)}, f32[2048,128]{0,1:T(8,128)}, ...), condition=%wide.region_17.17_spmd, body=%wide.region_15.16_spmd.sunk | while | flops 1023081472 | bytes 72397168 | solution.py:278
  1171.3 4.7 dynamic_update_slice.65
  1221.5 5.1 slice.143
  1232.2 10.3 collective-permute-done.3
  1243.9 17.6 collective-permute-done.2
  1267.0 14.7 convolution_bitcast_fusion.2
  1281.7 12.6 copy.162
  1296.0 11.6 convolution_bitcast_fusion
  1307.6 15.0 convolution_bitcast_fusion.1
  1322.6 18.8 pad_maximum_fusion
  1357.7 4.8 convert_reduce_fusion.1
  1362.6 11.5 add_bitcast_fusion
  1376.1 122.1 %reduce-scatter.10.cloned.1.call-done = f32[64,3072]{1,0:T(8,128)} async-done(((f32[1024,3072]{1,0:T(8,128)}), f32[64,3072]{1,0:T(8,128)}) %reduce-scatter.10.cloned.1.call-update) | async-done | bytes 786448
  1500.9 5.7 fusion.49
  1506.7 677.3 %reduce-scatter.8.cloned.1.call-done = f32[2,64,4096]{2,1,0:T(8,128)} async-done(((f32[2,1024,4096]{2,1,0:T(8,128)}), f32[2,64,4096]{2,1,0:T(8,128)}) %reduce-scatter.8.cloned.1.call-update) | async-done | bytes 2097168 | tf_op jit(solution)/shard_map/reduce_scatter | solution.py:333
  2184.0 6.5 fusion.42
  2190.6 5.4 copy.153
  2196.1 75.7 %all-reduce.4 = f32[12288]{0:T(1024)S(1)} all-reduce(f32[12288]{0:T(1024)S(1)} %constant_dynamic-update-slice_fusion.4), channel_id=5, replica_groups=mesh['grp'=2,'dp'=8,'seq'=2] {'dp','seq'}, use_global_device_ids=true, to_apply=%region_30.31.clone | all-reduce | flops 12288 | bytes 98304
  2284.9 4.6 multiply_subtract_fusion.1
  2299.7 5.0 multiply_subtract_fusion
  (1008 shorter events, 793.0 us)
Async XLA Ops:
  7.2 100.7 %all-gather.5.cloned.1.call-start = ((), (), s32[]{:S(2)}) async-start(), calls=%async_computation.3 | async-start | bytes 6684672 | tf_op jit(solution)/shard_map/all_gather | solution.py:77
  9.2 415.2 %all-gather.7.cloned.1.call-start = ((), (), s32[]{:S(2)}) async-start(), calls=%async_computation.4 | async-start | bytes 2228224 | tf_op jit(solution)/shard_map/all_gather | solution.py:78
  10.9 421.3 %all-gather.9.cloned.1.call-start = ((), (), s32[]{:S(2)}) async-start(), calls=%async_computation.5 | async-start | bytes 17825792 | tf_op jit(solution)/shard_map/all_gather | solution.py:79
  121.5 7.5 copy-start.29
  121.5 28.2 %collective-permute-start = (bf16[512,1024]{1,0:T(8,128)(2,1)}, bf16[512,1024]{1,0:T(8,128)(2,1)}, u32[]{:S(2)}, u32[]{:S(2)}) collective-permute-start(bf16[512,1024]{1,0:T(8,128)(2,1)} %get-tuple-element.661), channel_id=1, source_target_pairs={{0,1},{1,0},{2,3},{3,2},{4,5},{5,4},{6,7},{7,6},{8,9},{9,8},{10,11... | collective-permute-start | bytes 3145736 | tf_op jit(solution)/shard_map/ppermute | solution.py:27
  124.1 1250.0 %reduce-scatter.6.cloned.1.call-start = ((), (), s32[]{:S(2)}) async-start(), calls=%async_computation.6 | async-start | bytes 4456448 | tf_op jit(solution)/shard_map/reduce_scatter | solution.py:332
  125.1 7.3 copy-start.49
  131.6 45.7 %collective-permute-start.1 = (bf16[512,1024]{1,0:T(8,128)(2,1)}, bf16[512,1024]{1,0:T(8,128)(2,1)}, u32[]{:S(2)}, u32[]{:S(2)}) collective-permute-start(bf16[512,1024]{1,0:T(8,128)(2,1)} %get-tuple-element.660), channel_id=1, source_target_pairs={{0,1},{1,0},{2,3},{3,2},{4,5},{5,4},{6,7},{7,6},{8,9},{9,8},{10,11... | collective-permute-start | bytes 3145736 | tf_op jit(solution)/shard_map/ppermute | solution.py:27
  140.8 37.9 %copy-start.22 = (bf16[1024,1024]{1,0:T(8,128)(2,1)S(1)}, bf16[1024,1024]{1,0:T(8,128)(2,1)}, u32[]{:S(2)}) copy-start(bf16[1024,1024]{1,0:T(8,128)(2,1)} %get-tuple-element.657) | copy-start | bytes 6291460
  140.8 37.9 %copy-start.23 = (bf16[1024,1024]{1,0:T(8,128)(2,1)S(1)}, bf16[1024,1024]{1,0:T(8,128)(2,1)}, u32[]{:S(2)}) copy-start(bf16[1024,1024]{1,0:T(8,128)(2,1)} %get-tuple-element.658) | copy-start | bytes 6291460
  419.8 9.5 copy-start.8
  419.8 9.5 copy-start.26
  419.8 9.5 copy-start.68
  429.4 117.3 %copy-start.40 = (f32[1024]{0:T(1024)}, f32[1024]{0:T(1024)S(1)}, u32[]{:S(2)}) copy-start(f32[1024]{0:T(1024)S(1)} %broadcast_multiply_fusion.1) | copy-start | bytes 12292
  429.8 50.3 %copy-start.47 = (f32[1024]{0:T(1024)}, f32[1024]{0:T(1024)S(1)}, u32[]{:S(2)}) copy-start(f32[1024]{0:T(1024)S(1)} %multiply_reduce_fusion.4) | copy-start | bytes 12292
  429.9 116.8 %copy-start.44 = (f32[1024]{0:T(1024)}, f32[1024]{0:T(1024)S(1)}, u32[]{:S(2)}) copy-start(f32[1024]{0:T(1024)S(1)} %fusion.62) | copy-start | bytes 12292
  432.1 48.1 %copy-start.60 = (f32[1024]{0:T(1024)S(1)}, f32[1024]{0:T(1024)}, u32[]{:S(2)}) copy-start(f32[1024]{0:T(1024)} %get-tuple-element.681) | copy-start | bytes 12292
  432.2 48.0 %copy-start.6 = (f32[1024,1024]{0,1:T(8,128)S(1)}, f32[1024,1024]{0,1:T(8,128)}, u32[]{:S(2)}) copy-start(f32[1024,1024]{0,1:T(8,128)} %copy-done.5) | copy-start | bytes 12582916
  480.2 14.5 copy-start.3
  480.2 14.5 copy-start.39
  528.7 18.0 copy-start.48
  557.6 940.6 %reduce-scatter.10.cloned.1.call-start = ((), (), s32[]{:S(2)}) async-start(), calls=%async_computation.8 | async-start | bytes 13369344
  588.2 5.8 copy-start.2
  619.1 5.8 copy-start.2
  669.4 5.8 copy-start.2
  700.3 5.8 copy-start.2
  750.5 5.8 copy-start.2
  781.5 5.8 copy-start.2
  831.7 5.8 copy-start.2
  862.6 5.8 copy-start.2
  912.9 5.8 copy-start.2
  943.8 5.8 copy-start.2
  994.0 5.8 copy-start.2
  1025.0 5.8 copy-start.2
  1075.2 5.8 copy-start.2
  1106.1 5.8 copy-start.2
  1156.2 5.8 copy-start.2
  1187.2 5.8 copy-start.2
  1216.1 26.3 %collective-permute-start.3 = (bf16[512,1024]{0,1:T(8,128)(2,1)}, bf16[512,1024]{0,1:T(8,128)(2,1)}, u32[]{:S(2)}, u32[]{:S(2)}) collective-permute-start(bf16[512,1024]{0,1:T(8,128)(2,1)} %bitcast.38), channel_id=1, source_target_pairs={{0,1},{1,0},{2,3},{3,2},{4,5},{5,4},{6,7},{7,6},{8,9},{9,8},{10,11... | collective-permute-start | bytes 3145736 | tf_op jit(solution)/shard_map/ppermute | solution.py:27
  1220.8 5.8 copy-start.24
  1220.8 40.7 %collective-permute-start.2 = (bf16[512,1024]{0,1:T(8,128)(2,1)}, bf16[512,1024]{0,1:T(8,128)(2,1)S(1)}, u32[]{:S(2)}, u32[]{:S(2)}) collective-permute-start(bf16[512,1024]{0,1:T(8,128)(2,1)} %bitcast.35), channel_id=1, source_target_pairs={{0,1},{1,0},{2,3},{3,2},{4,5},{5,4},{6,7},{7,6},{8,9},{9,8},{10,11... | collective-permute-start | bytes 3145736 | tf_op jit(solution)/shard_map/ppermute | solution.py:27
  1232.1 33.0 %copy-start.17 = (bf16[1024,8,128]{0,2,1:T(8,128)(2,1)}, bf16[1024,8,128]{0,2,1:T(8,128)(2,1)S(1)}, u32[]{:S(2)}) copy-start(bf16[1024,8,128]{0,2,1:T(8,128)(2,1)S(1)} %copy.143) | copy-start | bytes 6291460
  1232.1 29.7 %copy-start.16 = (f32[1024,8,128]{0,2,1:T(8,128)S(1)}, f32[1024,8,128]{0,2,1:T(8,128)}, u32[]{:S(2)}) copy-start(f32[1024,8,128]{0,2,1:T(8,128)} %slice.143) | copy-start | bytes 12582916
  1294.4 13.2 copy-start.41
  1294.4 13.2 copy-start.43
  1294.4 13.2 copy-start.45
  1294.4 13.2 copy-start.51
  1294.4 889.5 %reduce-scatter.8.cloned.1.call-start = ((), (), s32[]{:S(2)}) async-start(), calls=%async_computation.7 | async-start | bytes 35651584 | tf_op jit(solution)/shard_map/reduce_scatter | solution.py:333
  1296.0 11.7 copy-start.7
  1341.5 943.4 %all-reduce.8.cloned.1.call-start = ((), (), s32[]{:S(2)}) async-start(), calls=%async_computation.9 | async-start | bytes 3932160 | tf_op jit(solution)/shard_map/psum | solution.py:347
  1342.6 8.9 copy-start.67
  1342.6 10.2 copy-start.65
  1342.6 10.2 copy-start.66
  1342.6 10.2 copy-start.4
  1344.3 5.6 copy-start.35
  1362.6 11.6 copy-start.28
  1362.6 11.5 copy-start.36
  1362.6 11.5 copy-start.37
  1500.9 683.0 %copy-start.11 = (f32[2,64,4096]{2,1,0:T(8,128)S(1)}, f32[2,64,4096]{2,1,0:T(8,128)}, u32[]{:S(2)}) copy-start(f32[2,64,4096]{2,1,0:T(8,128)} %param.32) | copy-start | bytes 6291460
  2190.6 5.5 copy-start.58
  2190.6 81.2 %copy-start.46 = (f32[768]{0:T(1024)S(1)}, f32[768]{0:T(1024)}, u32[]{:S(2)}) copy-start(f32[768]{0:T(1024)} %param.33) | copy-start | bytes 9220
  2190.6 85.5 %copy-start.64 = (f32[768]{0:T(1024)S(1)}, f32[768]{0:T(1024)}, u32[]{:S(2)}) copy-start(f32[768]{0:T(1024)} %param.45) | copy-start | bytes 9220
  2289.5 8.3 copy-start.38
  2289.5 10.2 copy-start.34
  (62 other events, 164.3 us)
Sparse Core Ops, SparseCore 0:
  11.5 96.3 all-gather.4
  111.1 66.5 all-gather.6
  180.6 189.8 all-gather.8
  557.7 96.3 reduce-scatter.5
  1294.5 203.6 reduce-scatter.9
  1501.0 682.9 reduce-scatter.7
  2190.6 21.1 all-reduce.7
where the time goes:
time: 2330 us; the launch traced here: 2310 us
  waiting for transfers between devices  915 us (39%)
  local copies, waits for them, and re-layouts  555 us (24%)
  matrix products  351 us (15%)
  other arithmetic  210 us (9%)
  loops' own time  138 us (6%)
  blocking collectives  121 us (5%)
    reduce_scatter x1, waiting for transfers between devices, on_device(): lax.psum_scatter(ffn_grad, ('dp', 'seq'), scatter_dimension=1, tiled=True)  677 us
    unnamed x8, waiting for transfers between devices  122 us
    unnamed x163, local copies, waits for them, and re-layouts  85.7 us
    unnamed x1, blocking collectives  75.7 us
    dynamic_update_slice x16, local copies, waits for them, and re-layouts, block_backward(): lax.dynamic_update_slice_in_dim(value_running, lax.dynamic_slice_in_dim(v...  70.7 us
    dynamic_update_slice x16, local copies, waits for them, and re-layouts, block_backward(): lax.dynamic_update_slice_in_dim(key_running, lax.dynamic_slice_in_dim(key...  70.4 us
    dot_general x32, matrix products, head_scores(): jnp.einsum('qhd,khd->hqk', query_heads, key_heads, preferred_element_type...  65.5 us
    ppermute x4, waiting for transfers between devices, partner(): lax.ppermute(x, axis, [(i, i ^ 1 << stride) for i in range(lax.axis_size(...  63 us
  transfers between devices with their start and end apart: 11, of which 7 were waited for; matrix products, arithmetic and copies ran while one was open for 41% of the time, Pallas kernels for 0%

commit v1 on v0

v1 whole, which is shorter than its diff:
```python
from functools import partial

import jax
import jax.numpy as jnp
from jax import lax
from jax.experimental import pallas as pl
from jax.experimental.pallas import tpu as pltpu
from jax.sharding import PartitionSpec as P

HD = 64
W = 512


beta_one = 0.9
beta_two = 0.95
adam_eps = 1e-08
weight_decay = 0.1
bias_one = 1.0 - 0.9**10
bias_two = 1.0 - 0.95**10
step_rates = (0.01, 0.1, 0.005, 0.2)
outer_rate = 0.7
outer_beta = 0.9
norm_eps = 1e-05
score_fill = -1e30


def partner(x, axis, stride):
    return lax.ppermute(x, axis, [(i, i ^ 1 << stride) for i in range(lax.axis_size(axis))])


def layer_norm(residue, norm_gain, norm_shift):
    average = jnp.mean(residue, axis=-1, keepdims=True)
    centred = residue - average
    variance = jnp.mean(centred * centred, axis=-1, keepdims=True)
    return centred * lax.rsqrt(variance + norm_eps) * norm_gain + norm_shift


TILE = 256
LENGTHS = (3, 4, 5, 5)


def first_tile(side, j):
    return jnp.where(side == 0, jnp.maximum(j - 2, 0), 3 - j)


def query_tile(side, j):
    return jnp.where(side == 0, j, 5 - j)


def own_tile(side, j):
    return jnp.where(side == 0, j, 3 - j)


def dot_nt(a, b):
    return lax.dot_general(a, b, (((1,), (1,)), ((), ())), preferred_element_type=jnp.float32)


def dot_tn(a, b):
    return lax.dot_general(a, b, (((0,), (0,)), ((), ())), preferred_element_type=jnp.float32)


def dot_nn(a, b):
    return lax.dot_general(a, b, (((1,), (0,)), ((), ())), preferred_element_type=jnp.float32)


def mask_bias(query_start, key_start, query_ids, key_ids):
    rows, cols = query_ids.shape[0], key_ids.shape[1]
    relative = (
        lax.broadcasted_iota(jnp.int32, (rows, cols), 1)
        - lax.broadcasted_iota(jnp.int32, (rows, cols), 0)
        + (key_start - query_start)
    )
    allowed = (relative <= W) & (relative >= -W) & (query_ids == key_ids)
    return jnp.where(allowed, 0.0, score_fill)


def pair_split(x):
    lane = lax.broadcasted_iota(jnp.int32, x.shape, 1)
    zero = jnp.zeros_like(x)
    return jnp.where(lane < HD, x, zero), jnp.where(lane < HD, zero, x)


def pick_lane(x, index):
    lane = lax.broadcasted_iota(jnp.int32, x.shape, 1)
    return jnp.sum(jnp.where(lane == index, x, 0.0), axis=1, keepdims=True)


def attend_kernel(side_ref, ids_col_ref, ids_row_ref, q_ref, k_ref, v_ref, o_ref, wide_ref, lse_ref, bias_ref):
    j, pair = pl.program_id(0), pl.program_id(1)
    side = side_ref[0]

    def run(length):
        span = length * TILE
        start = pl.multiple_of(first_tile(side, j) * TILE, TILE)

        @pl.when(pair == 0)
        def _():
            bias_ref[:, :span] = mask_bias(
                query_tile(side, j) * TILE,
                start,
                ids_col_ref[:, :1],
                ids_row_ref[:1, pl.ds(start, span)],
            )
            lse_ref[...] = jnp.zeros_like(lse_ref)

        queries = pair_split(q_ref[...] * jnp.bfloat16(HD**-0.5))
        keys = k_ref[pl.ds(start, span), :]
        values = pair_split(v_ref[pl.ds(start, span), :])
        total = None
        lane = lax.broadcasted_iota(jnp.int32, lse_ref.shape, 1)
        for h in range(2):
            scores = dot_nt(queries[h], keys) + bias_ref[:, :span]
            maximum = jnp.max(scores, axis=1, keepdims=True)
            exponent = jnp.exp(scores - maximum)
            denominator = jnp.sum(exponent, axis=1, keepdims=True)
            weights = (exponent * (1.0 / denominator)).astype(jnp.bfloat16)
            part = dot_nn(weights, values[h])
            total = part if total is None else total + part
            logsum = maximum + jnp.log(denominator)
            lse_ref[...] = jnp.where(lane == 2 * pair + h, logsum, lse_ref[...])
        o_ref[...] = total.astype(jnp.bfloat16)
        wide_ref[...] = total

    for length in sorted(set(LENGTHS)):
        hits = [i for i in range(4) if LENGTHS[i] == length]

        @pl.when((j >= hits[0]) & (j <= hits[-1]))
        def _():
            run(length)


def attend(side, ids_col, ids_row, qkv):
    rows, width = qkv.shape[0], qkv.shape[1] // 3
    pairs = width // 128
    own = rows - W
    return pl.pallas_call(
        attend_kernel,
        name="attend",
        grid_spec=pltpu.PrefetchScalarGridSpec(
            num_scalar_prefetch=1,
            grid=(own // TILE, pairs),
            in_specs=[
                pl.BlockSpec((TILE, 128), lambda j, p, s: (query_tile(s[0], j), 0)),
                pl.BlockSpec((8, rows), lambda j, p, s: (0, 0)),
                pl.BlockSpec((TILE, 128), lambda j, p, s: (query_tile(s[0], j), p)),
                pl.BlockSpec((rows, 128), lambda j, p, s: (0, pairs + p)),
                pl.BlockSpec((rows, 128), lambda j, p, s: (0, 2 * pairs + p)),
            ],
            out_specs=[
                pl.BlockSpec((TILE, 128), lambda j, p, s: (own_tile(s[0], j), p)),
                pl.BlockSpec((TILE, 128), lambda j, p, s: (own_tile(s[0], j), p)),
                pl.BlockSpec((TILE, 128), lambda j, p, s: (own_tile(s[0], j), 0)),
            ],
            scratch_shapes=[pltpu.VMEM((TILE, 5 * TILE), jnp.float32)],
        ),
        out_shape=[
            jax.ShapeDtypeStruct((own, width), jnp.bfloat16),
            jax.ShapeDtypeStruct((own, width), jnp.float32),
            jax.ShapeDtypeStruct((own, 128), jnp.float32),
        ],
        compiler_params=pltpu.CompilerParams(vmem_limit_bytes=48 << 20),
        cost_estimate=pl.CostEstimate(
            flops=4 * 17 * TILE * TILE * width * 4, bytes_accessed=30 << 20, transcendentals=0
        ),
    )(side, ids_col, ids_row, qkv, qkv, qkv)


def attend_back_kernel(
    side_ref, ids_col_ref, ids_row_ref, q_ref, k_ref, v_ref, do_ref, lse_ref, inner_ref,
    dq_ref, dk_ref, dv_ref, bias_ref, dkt_ref, dvt_ref,
):
    pair, j = pl.program_id(0), pl.program_id(1)
    side = side_ref[0]
    own = dk_ref.shape[0]

    @pl.when(j == 0)
    def _():
        dkt_ref[...] = jnp.zeros_like(dkt_ref)
        dvt_ref[...] = jnp.zeros_like(dvt_ref)

    def run(length):
        span = length * TILE
        start = pl.multiple_of(first_tile(side, j) * TILE, TILE)

        @pl.when(pair == 0)
        def _():
            bias_ref[j, :, :span] = mask_bias(
                query_tile(side, j) * TILE,
                start,
                ids_col_ref[:, :1],
                ids_row_ref[:1, pl.ds(start, span)],
            )

        scaled = q_ref[...] * jnp.bfloat16(HD**-0.5)
        outgrad = do_ref[...]
        queries = pair_split(scaled)
        outgrads = pair_split(outgrad)
        turned_q = jnp.transpose(scaled.astype(jnp.float32)).astype(jnp.bfloat16)
        turned_do = jnp.transpose(outgrad.astype(jnp.float32)).astype(jnp.bfloat16)
        keys = k_ref[pl.ds(start, span), :]
        values = v_ref[pl.ds(start, span), :]
        key_parts = pair_split(keys)
        total = None
        for h in range(2):
            logsum = pick_lane(lse_ref[...], 2 * pair + h)
            inner = pick_lane(inner_ref[...], 2 * pair + h)
            scores = dot_nt(queries[h], keys) + bias_ref[j, :, :span]
            probs = jnp.exp(scores - logsum)
            prob_grad = dot_nt(outgrads[h], values)
            score_grad = (probs * (prob_grad - inner)).astype(jnp.bfloat16)
            part = dot_nn(score_grad, key_parts[h])
            total = part if total is None else total + part
            head = slice(h * HD, (h + 1) * HD)
            dvt_ref[head, pl.ds(start, span)] += dot_nn(turned_do[head], probs.astype(jnp.bfloat16))
            dkt_ref[head, pl.ds(start, span)] += dot_nn(turned_q[head], score_grad)
        dq_ref[...] = (total * HD**-0.5).astype(jnp.bfloat16)

    for length in sorted(set(LENGTHS)):
        hits = [i for i in range(4) if LENGTHS[i] == length]

        @pl.when((j >= hits[0]) & (j <= hits[-1]))
        def _():
            run(length)

    @pl.when(j == pl.num_programs(1) - 1)
    def _():
        at = pl.multiple_of(side * W, W)
        dk_ref[...] = jnp.transpose(dkt_ref[:, pl.ds(at, own)])
        dv_ref[...] = jnp.transpose(dvt_ref[:, pl.ds(at, own)])


def attend_back(side, ids_col, ids_row, qkv, outgrad, lse, inner):
    rows, width = qkv.shape[0], qkv.shape[1] // 3
    pairs = width // 128
    own = rows - W
    return pl.pallas_call(
        attend_back_kernel,
        name="attend_back",
        grid_spec=pltpu.PrefetchScalarGridSpec(
            num_scalar_prefetch=1,
            grid=(pairs, own // TILE),
            in_specs=[
                pl.BlockSpec((TILE, 128), lambda p, j, s: (query_tile(s[0], j), 0)),
                pl.BlockSpec((8, rows), lambda p, j, s: (0, 0)),
                pl.BlockSpec((TILE, 128), lambda p, j, s: (query_tile(s[0], j), p)),
                pl.BlockSpec((rows, 128), lambda p, j, s: (0, pairs + p)),
                pl.BlockSpec((rows, 128), lambda p, j, s: (0, 2 * pairs + p)),
                pl.BlockSpec((TILE, 128), lambda p, j, s: (own_tile(s[0], j), p)),
                pl.BlockSpec((TILE, 128), lambda p, j, s: (own_tile(s[0], j), 0)),
                pl.BlockSpec((TILE, 128), lambda p, j, s: (own_tile(s[0], j), 0)),
            ],
            out_specs=[
                pl.BlockSpec((TILE, 128), lambda p, j, s: (own_tile(s[0], j), p)),
                pl.BlockSpec((own, 128), lambda p, j, s: (0, p)),
                pl.BlockSpec((own, 128), lambda p, j, s: (0, p)),
            ],
            scratch_shapes=[
                pltpu.VMEM((own // TILE, TILE, 5 * TILE), jnp.float32),
                pltpu.VMEM((128, rows), jnp.float32),
                pltpu.VMEM((128, rows), jnp.float32),
            ],
        ),
        out_shape=[
            jax.ShapeDtypeStruct((own, width), jnp.bfloat16),
            jax.ShapeDtypeStruct((own, width), jnp.float32),
            jax.ShapeDtypeStruct((own, width), jnp.float32),
        ],
        compiler_params=pltpu.CompilerParams(vmem_limit_bytes=48 << 20),
        cost_estimate=pl.CostEstimate(
            flops=10 * 17 * TILE * TILE * width * 4, bytes_accessed=40 << 20, transcendentals=0
        ),
    )(side, ids_col, ids_row, qkv, qkv, qkv, outgrad, lse, inner)


def attend_far_kernel(
    side_ref, ids_col_ref, ids_row_ref, q_ref, k_ref, v_ref, do_ref, lse_ref, inner_ref,
    dk_in_ref, dv_in_ref, dk_ref, dv_ref, bias_ref,
):
    pair = pl.program_id(0)
    side = side_ref[0]

    @pl.when(pair == 0)
    def _():
        bias_ref[...] = mask_bias(
            jnp.where(side == 0, 2 * W, 0), W, ids_col_ref[:, :1], ids_row_ref[:1, W : 2 * W]
        )

    scaled = q_ref[...] * jnp.bfloat16(HD**-0.5)
    outgrad = do_ref[...]
    queries = pair_split(scaled)
    outgrads = pair_split(outgrad)
    turned_q = jnp.transpose(scaled.astype(jnp.float32)).astype(jnp.bfloat16)
    turned_do = jnp.transpose(outgrad.astype(jnp.float32)).astype(jnp.bfloat16)
    keys, values = k_ref[...], v_ref[...]
    dk_parts, dv_parts = [], []
    for h in range(2):
        logsum = pick_lane(lse_ref[...], 2 * pair + h)
        inner = pick_lane(inner_ref[...], 2 * pair + h)
        scores = dot_nt(queries[h], keys) + bias_ref[...]
        probs = jnp.exp(scores - logsum)
        prob_grad = dot_nt(outgrads[h], values)
        score_grad = (probs * (prob_grad - inner)).astype(jnp.bfloat16)
        head = slice(h * HD, (h + 1) * HD)
        dv_parts.append(dot_nn(turned_do[head], probs.astype(jnp.bfloat16)))
        dk_parts.append(dot_nn(turned_q[head], score_grad))
    dk_far = jnp.transpose(jnp.concatenate(dk_parts, axis=0))
    dv_far = jnp.transpose(jnp.concatenate(dv_parts, axis=0))
    near = pl.multiple_of(jnp.where(side == 0, W, 0), W)
    rest = pl.multiple_of(jnp.where(side == 0, 0, W), W)
    dk_ref[pl.ds(near, W), :] = (dk_in_ref[pl.ds(near, W), :] + dk_far).astype(jnp.bfloat16)
    dv_ref[pl.ds(near, W), :] = (dv_in_ref[pl.ds(near, W), :] + dv_far).astype(jnp.bfloat16)
    dk_ref[pl.ds(rest, W), :] = dk_in_ref[pl.ds(rest, W), :].astype(jnp.bfloat16)
    dv_ref[pl.ds(rest, W), :] = dv_in_ref[pl.ds(rest, W), :].astype(jnp.bfloat16)


def attend_far(side, ids_col, ids_row, qkv, far_outgrad, far_lse, far_inner, dk, dv):
    rows, width = qkv.shape[0], qkv.shape[1] // 3
    pairs = width // 128
    own = rows - W
    far = lambda p, s: (jnp.where(s[0] == 0, 2, 0), p)
    return pl.pallas_call(
        attend_far_kernel,
        name="attend_far",
        grid_spec=pltpu.PrefetchScalarGridSpec(
            num_scalar_prefetch=1,
            grid=(pairs,),
            in_specs=[
                pl.BlockSpec((W, 128), lambda p, s: (jnp.where(s[0] == 0, 2, 0), 0)),
                pl.BlockSpec((8, rows), lambda p, s: (0, 0)),
                pl.BlockSpec((W, 128), far),
                pl.BlockSpec((W, 128), lambda p, s: (1, pairs + p)),
                pl.BlockSpec((W, 128), lambda p, s: (1, 2 * pairs + p)),
                pl.BlockSpec((W, 128), lambda p, s: (0, p)),
                pl.BlockSpec((W, 128), lambda p, s: (0, 0)),
                pl.BlockSpec((W, 128), lambda p, s: (0, 0)),
                pl.BlockSpec((own, 128), lambda p, s: (0, p)),
                pl.BlockSpec((own, 128), lambda p, s: (0, p)),
            ],
            out_specs=[
                pl.BlockSpec((own, 128), lambda p, s: (0, p)),
                pl.BlockSpec((own, 128), lambda p, s: (0, p)),
            ],
            scratch_shapes=[pltpu.VMEM((W, W), jnp.float32)],
        ),
        out_shape=[jax.ShapeDtypeStruct((own, width), jnp.bfloat16)] * 2,
        compiler_params=pltpu.CompilerParams(vmem_limit_bytes=48 << 20),
        cost_estimate=pl.CostEstimate(
            flops=8 * 4 * TILE * TILE * width * 4, bytes_accessed=20 << 20, transcendentals=0
        ),
    )(side, ids_col, ids_row, qkv, qkv, qkv, far_outgrad, far_lse, far_inner, dk, dv)


COLOURS = ((("y", "x", "z"), 3), (("x", "y", "z"), 3), (("z", "y", "x"), 2))


def axis_parts():
    total = lax.axis_size("dp")
    inner = 2 ** ((total.bit_length() - 1) // 2)
    return {"z": total // inner, "x": inner, "y": lax.axis_size("seq")}


def place(axis):
    inner = axis_parts()["x"]
    if axis == "y":
        return lax.axis_index("seq")
    return lax.axis_index("dp") // inner if axis == "z" else lax.axis_index("dp") % inner


def shift(x, axis):
    parts = axis_parts()
    size, inner = parts[axis], parts["x"]
    if axis == "y":
        return lax.ppermute(x, "seq", [(i, (i + 1) % size) for i in range(size)])
    total = parts["z"] * inner
    if axis == "z":
        return lax.ppermute(x, "dp", [(i, (i + inner) % total) for i in range(total)])
    return lax.ppermute(x, "dp", [(i, i - i % inner + (i + 1) % inner) for i in range(total)])


def add_up(terms):
    total = terms[0].astype(jnp.float32)
    for term in terms[1:]:
        total = total + term.astype(jnp.float32)
    return total


def scatter_colour(partial_rows, order):
    parts = axis_parts()
    columns = partial_rows.shape[1]
    left = ["z", "x", "y"]
    sources = [partial_rows.reshape(*[parts[a] for a in left], -1, columns)]
    for axis in order:
        size, spot = parts[axis], place(axis)
        at = left.index(axis)

        def piece(index):
            return [lax.dynamic_index_in_dim(s, index, at, keepdims=False) for s in sources]

        got = []
        for step in range(size - 1):
            chunk = (spot + 2 * size - 1 - step) % size
            got = [shift(add_up(piece(chunk) + got).astype(jnp.bfloat16), axis)]
        sources = piece(spot) + got
        left.remove(axis)
    return add_up(sources)


def scatter_rows(partial_rows):
    columns = partial_rows.shape[1] // 128
    shares = sum(share for _, share in COLOURS)
    cuts, begin, pieces = [], 0, []
    for order, share in COLOURS:
        cuts.append((begin, order))
        begin += share
    for start, share_order in enumerate(cuts):
        low = share_order[0] * columns // shares * 128
        high = cuts[start + 1][0] * columns // shares * 128 if start + 1 < len(cuts) else columns * 128
        pieces.append(scatter_colour(partial_rows[:, low:high], share_order[1]))
    return jnp.concatenate(pieces, axis=1)


def adam_step(master, gradient, first, second, step_rate):
    first_new = beta_one * first + (1.0 - beta_one) * gradient
    second_new = beta_two * second + (1.0 - beta_two) * gradient * gradient
    direction = first_new / bias_one / (jnp.sqrt(second_new / bias_two) + adam_eps)
    return (master - step_rate * (direction + weight_decay * master), first_new, second_new)


def on_device(
    tokens,
    cotangent,
    segments,
    weight_qkv,
    weight_out,
    weight_ffn,
    vectors,
    first_qkv,
    first_out,
    first_ffn,
    first_vec,
    second_qkv,
    second_out,
    second_ffn,
    second_vec,
    outer_qkv,
    outer_out,
    outer_ffn,
    outer_vec,
):
    masters = (weight_qkv, weight_out, weight_ffn, vectors)
    lowered = [master.astype(jnp.bfloat16) for master in masters]
    gathered = (
        lax.all_gather(lowered[0], ("dp", "seq"), axis=0, tiled=True),
        lax.all_gather(lowered[1], ("dp", "seq"), axis=0, tiled=True),
        lax.all_gather(lowered[2], ("dp", "seq"), axis=1, tiled=True),
        lax.all_gather(lowered[3], ("dp", "seq"), axis=0, tiled=True),
    )
    full_qkv, full_out, full_ffn, full_vec = gathered
    width = full_out.shape[0]
    vector_values = full_vec.astype(jnp.float32)
    pieces = [vector_values[position * width : (position + 1) * width] for position in range(8)]
    (
        bias_query,
        bias_value,
        bias_output,
        bias_second,
        gain_first,
        shift_first,
        gain_second,
        shift_second,
    ) = pieces
    bias_hidden = vector_values[8 * width :]
    token_rows = tokens[0]
    local_rows = token_rows.shape[0]
    side = lax.axis_index("seq")
    is_first = side == 0
    side_operand = jnp.reshape(side, (1,)).astype(jnp.int32)
    far_tokens = partner(jnp.where(is_first, token_rows[local_rows - W :], token_rows[:W]), "seq", 0)
    wide_tokens = jnp.where(
        is_first,
        jnp.concatenate([token_rows, far_tokens], axis=0),
        jnp.concatenate([far_tokens, token_rows], axis=0),
    )
    joined_bias = jnp.concatenate([bias_query, jnp.zeros_like(bias_query), bias_value])
    projected = (
        jnp.dot(wide_tokens, full_qkv, preferred_element_type=jnp.float32) + joined_bias
    ).astype(jnp.bfloat16)
    wide_ids = lax.dynamic_slice_in_dim(segments[0], side * (local_rows - W), local_rows + W, 0)
    ids_col = jnp.broadcast_to(wide_ids[:, None], (local_rows + W, 128))
    ids_row = jnp.broadcast_to(wide_ids[None, :], (8, local_rows + W))
    attended, attended_wide, logsum = attend(side_operand, ids_col, ids_row, projected)
    branch = jnp.dot(attended, full_out, preferred_element_type=jnp.float32) + bias_output
    residue_first = token_rows.astype(jnp.float32) + branch
    hidden_in, first_pullback = jax.vjp(layer_norm, residue_first, gain_first, shift_first)
    hidden_low = hidden_in.astype(jnp.bfloat16)
    inner = jnp.dot(hidden_low, full_ffn[0], preferred_element_type=jnp.float32) + bias_hidden
    activated, gelu_pullback = jax.vjp(partial(jax.nn.gelu, approximate=False), inner)
    activated_low = activated.astype(jnp.bfloat16)
    second_branch = (
        lax.dot_general(
            activated_low, full_ffn[1], (((1,), (1,)), ((), ())), preferred_element_type=jnp.float32
        )
        + bias_second
    )
    residue_second = hidden_in + second_branch
    result, second_pullback = jax.vjp(layer_norm, residue_second, gain_second, shift_second)
    upstream = cotangent[0].astype(jnp.float32)
    residue_second_grad, gain_second_grad, shift_second_grad = second_pullback(upstream)
    branch_two_low = residue_second_grad.astype(jnp.bfloat16)
    bias_second_grad = jnp.sum(branch_two_low.astype(jnp.float32), axis=0)
    down_grad = dot_tn(branch_two_low, activated_low).astype(jnp.bfloat16)
    activated_grad = jnp.dot(branch_two_low, full_ffn[1], preferred_element_type=jnp.float32)
    (inner_grad,) = gelu_pullback(activated_grad)
    inner_low = inner_grad.astype(jnp.bfloat16)
    bias_hidden_grad = jnp.sum(inner_low.astype(jnp.float32), axis=0)
    up_grad = dot_tn(hidden_low, inner_low).astype(jnp.bfloat16)
    hidden_grad = residue_second_grad + lax.dot_general(
        inner_low, full_ffn[0], (((1,), (1,)), ((), ())), preferred_element_type=jnp.float32
    )
    residue_first_grad, gain_first_grad, shift_first_grad = first_pullback(hidden_grad)
    branch_low = residue_first_grad.astype(jnp.bfloat16)
    bias_output_grad = jnp.sum(branch_low.astype(jnp.float32), axis=0)
    out_weight_grad = dot_tn(attended, branch_low).astype(jnp.bfloat16)
    mixed_grad = lax.dot_general(
        branch_low, full_out, (((1,), (1,)), ((), ())), preferred_element_type=jnp.float32
    ).astype(jnp.bfloat16)

    heads = width // HD
    head_of = jnp.arange(width, dtype=jnp.int32)[:, None] // HD
    collect = (head_of == jnp.arange(128, dtype=jnp.int32)[None, :]).astype(jnp.float32)
    inner_sums = jnp.dot(
        attended_wide * mixed_grad.astype(jnp.float32), collect, precision=lax.Precision.HIGHEST
    )

    def near_rows(x):
        return jnp.where(is_first, x[local_rows - W :], x[:W])

    far_stats = partner(
        jnp.concatenate([near_rows(logsum)[:, :heads], near_rows(inner_sums)[:, :heads]], axis=1),
        "seq",
        0,
    )
    far_outgrad = partner(near_rows(mixed_grad), "seq", 0)
    lane_pad = ((0, 0), (0, 128 - heads))
    far_logsum = jnp.pad(far_stats[:, :heads], lane_pad)
    far_inner = jnp.pad(far_stats[:, heads:], lane_pad)
    query_grad, key_near, value_near = attend_back(
        side_operand, ids_col, ids_row, projected, mixed_grad, logsum, inner_sums
    )
    key_grad, value_grad = attend_far(
        side_operand, ids_col, ids_row, projected, far_outgrad, far_logsum, far_inner, key_near, value_near
    )
    projected_grad = jnp.concatenate([query_grad, key_grad, value_grad], axis=1)
    qkv_weight_grad = dot_tn(token_rows, projected_grad).astype(jnp.bfloat16)
    projected_sums = jnp.sum(projected_grad.astype(jnp.float32), axis=0)
    input_grad = residue_first_grad + lax.dot_general(
        projected_grad, full_qkv, (((1,), (1,)), ((), ())), preferred_element_type=jnp.float32
    )
    vector_grad = jnp.concatenate(
        [
            projected_sums[:width],
            projected_sums[2 * width :],
            bias_output_grad,
            bias_second_grad,
            gain_first_grad,
            shift_first_grad,
            gain_second_grad,
            shift_second_grad,
            bias_hidden_grad,
        ]
    )
    vector_rows = vector_grad.reshape(width, -1)
    entries = vector_rows.shape[1]
    small = jnp.pad(vector_rows, ((0, 0), (0, 128 - entries))).astype(jnp.bfloat16)
    rest = scatter_rows(jnp.concatenate([qkv_weight_grad, out_weight_grad, small], axis=1))
    summed = (
        rest[:, : 3 * width],
        rest[:, 3 * width : 4 * width],
        jnp.stack([scatter_rows(up_grad), scatter_rows(down_grad)]),
        rest[:, 4 * width : 4 * width + entries].reshape(-1),
    )
    firsts = (first_qkv[0], first_out[0], first_ffn[0], first_vec[0])
    seconds = (second_qkv[0], second_out[0], second_ffn[0], second_vec[0])
    outers = (outer_qkv, outer_out, outer_ffn, outer_vec)
    stepped = [
        adam_step(
            masters[member], summed[member], firsts[member], seconds[member], step_rates[member]
        )
        for member in range(4)
    ]
    changes = [masters[member] - stepped[member][0] for member in range(4)]
    lowered_changes = [change.astype(jnp.bfloat16) for change in changes]
    other_changes = [partner(change, "grp", 0) for change in lowered_changes]
    deltas = [
        (lowered_changes[member].astype(jnp.float32) + other_changes[member].astype(jnp.float32)) / 2
        for member in range(4)
    ]
    momenta = [outer_beta * outers[member] + deltas[member] for member in range(4)]
    renewed = [
        masters[member] - outer_rate * (deltas[member] + outer_beta * momenta[member])
        for member in range(4)
    ]
    return (
        result.astype(jnp.bfloat16)[None],
        input_grad[None],
        summed[0][None],
        summed[1][None],
        summed[2][None],
        summed[3][None],
        stepped[0][1][None],
        stepped[1][1][None],
        stepped[2][1][None],
        stepped[3][1][None],
        stepped[0][2][None],
        stepped[1][2][None],
        stepped[2][2][None],
        stepped[3][2][None],
        deltas[0],
        deltas[1],
        deltas[2],
        deltas[3],
        momenta[0],
        momenta[1],
        momenta[2],
        momenta[3],
        renewed[0],
        renewed[1],
        renewed[2],
        renewed[3],
    )


def solution(mesh):
    return jax.shard_map(
        on_device,
        mesh=mesh,
        in_specs=(
            P(("grp", "dp"), "seq", None),
            P(("grp", "dp"), "seq", None),
            P(("grp", "dp"), None),
            P(("dp", "seq"), None),
            P(("dp", "seq"), None),
            P(None, ("dp", "seq"), None),
            P(("dp", "seq")),
            P("grp", ("dp", "seq"), None),
            P("grp", ("dp", "seq"), None),
            P("grp", None, ("dp", "seq"), None),
            P("grp", ("dp", "seq")),
            P("grp", ("dp", "seq"), None),
            P("grp", ("dp", "seq"), None),
            P("grp", None, ("dp", "seq"), None),
            P("grp", ("dp", "seq")),
            P(("dp", "seq"), None),
            P(("dp", "seq"), None),
            P(None, ("dp", "seq"), None),
            P(("dp", "seq")),
        ),
        out_specs=(
            P(("grp", "dp"), "seq", None),
            P(("grp", "dp"), "seq", None),
            P("grp", ("dp", "seq"), None),
            P("grp", ("dp", "seq"), None),
            P("grp", None, ("dp", "seq"), None),
            P("grp", ("dp", "seq")),
            P("grp", ("dp", "seq"), None),
            P("grp", ("dp", "seq"), None),
            P("grp", None, ("dp", "seq"), None),
            P("grp", ("dp", "seq")),
            P("grp", ("dp", "seq"), None),
            P("grp", ("dp", "seq"), None),
            P("grp", None, ("dp", "seq"), None),
            P("grp", ("dp", "seq")),
            P(("dp", "seq"), None),
            P(("dp", "seq"), None),
            P(None, ("dp", "seq"), None),
            P(("dp", "seq")),
            P(("dp", "seq"), None),
            P(("dp", "seq"), None),
            P(None, ("dp", "seq"), None),
            P(("dp", "seq")),
            P(("dp", "seq"), None),
            P(("dp", "seq"), None),
            P(None, ("dp", "seq"), None),
            P(("dp", "seq")),
        ),
        check_vma=False,
    )
```

time: 2330 us -> 916 us (0.39)
  waiting for transfers between devices: 915 us -> 312 us
  local copies, waits for them, and re-layouts: 555 us -> 56.9 us
  matrix products: 351 us -> 185 us
  loops' own time: 138 us -> 0 us
  Pallas kernels: 0 us -> 131 us
  other arithmetic: 210 us -> 101 us
  blocking collectives: 121 us -> 65.4 us
  starting transfers between devices: 4.89 us -> 38.4 us
    reduce_scatter x2 -> x0, waiting for transfers between devices: 677 us -> none  [the longest x1 677 us: on_device(): lax.psum_scatter(ffn_grad, ('dp', 'seq'), scatter_dimension=1, tiled=True)]
    dynamic_update_slice x112 -> x0, local copies, waits for them, and re-layouts: 203 us -> none  [the longest x16 70.7 us: block_backward(): lax.dynamic_update_slice_in_dim(value_running, lax.dynamic_slice_in_dim(v...]
    dynamic_slice x273 -> x3, local copies, waits for them, and re-layouts: 203 us -> 2.08 us  [the longest x2 2.06 us: piece(): lax.dynamic_index_in_dim(s, index, at, keepdims=False)]
    all_gather x1, waiting for transfers between devices: 0.02 us -> 175 us  [on_device(): lax.all_gather(lowered[2], ('dp', 'seq'), axis=1, tiled=True)]
    dot_general x117 -> x6, matrix products: 224 us -> 58.7 us  [the longest x4 39 us: dot_tn(): lax.dot_general(a, b, (((0,), (0,)), ((), ())), preferred_element_type=jn...]
    another operation x18 -> x0, loops' own time: 138 us -> none  [the longest x8 53.7 us: group_backward(): lax.scan(block_backward, start_totals, (offsets, logsum_group))]
    pallas_call x0 -> x3, Pallas kernels: none -> 131 us  [the longest x1 63.8 us: attend_back(): pl.pallas_call(attend_back_kernel, name='attend_back', grid_spec=pltpu.Pr...]
    unnamed x8 -> x3, waiting for transfers between devices: 122 us -> 0.05 us
  transfers between devices with their start and end apart: 11 -> 55, of which waited for: 7 -> 29; matrix products, arithmetic and copies ran while one was open for 41% -> 19% of each run, Pallas kernels for 0% -> 7%
where the time goes in v1:
time: 916 us; the launch traced here: 905 us
  waiting for transfers between devices  312 us (34%)
  matrix products  185 us (20%)
  Pallas kernels  131 us (14%)
  other arithmetic  101 us (11%)
  blocking collectives  65.4 us (7%)
  local copies, waits for them, and re-layouts  56.9 us (6%)
  starting transfers between devices  38.4 us (4%)
  between operations  15.6 us (2%)
    all_gather x1, waiting for transfers between devices, on_device(): lax.all_gather(lowered[2], ('dp', 'seq'), axis=1, tiled=True)  175 us
    all_gather x1, blocking collectives, on_device(): lax.all_gather(lowered[3], ('dp', 'seq'), axis=0, tiled=True)  65.4 us
    pallas_call x1, Pallas kernels, attend_back(): pl.pallas_call(attend_back_kernel, name='attend_back', grid_spec=pltpu.Pr...  63.8 us
    ppermute x27, waiting for transfers between devices, shift(): lax.ppermute(x, 'dp', [(i, (i + inner) % total) for i in range(total)])  61.4 us
    pallas_call x1, Pallas kernels, attend(): pl.pallas_call(attend_kernel, name='attend', grid_spec=pltpu.PrefetchScal...  52.6 us
    dot_general x1, matrix products, on_device(): jnp.dot(hidden_low, full_ffn[0], preferred_element_type=jnp.float32)  48 us
    convert_element_type x36, other arithmetic, scatter_colour(): got = [shift(add_up(piece(chunk) + got).astype(jnp.bfloat16), axis)]  39.1 us
    dot_general x4, matrix products, dot_tn(): lax.dot_general(a, b, (((0,), (0,)), ((), ())), preferred_element_type=jn...  39 us
  transfers between devices with their start and end apart: 55, of which 29 were waited for; matrix products, arithmetic and copies ran while one was open for 19% of the time, Pallas kernels for 7%

profile of v1, /device:TPU:0, one launch (start us, length us, event | category | flops | bytes accessed | tf_op | source)
XLA Modules:
  0.0 905.0 jit_solution(963954639069193647)
XLA Ops:
  11.0 2.7 convert_element_type.1019
  13.7 4.1 copy.123
  19.4 3.1 collective-permute-start
  22.5 65.4 %all-gather = bf16[16,1,768]{2,1,0:T(2,128)(2,1)S(1)} all-gather(bf16[1,1,768]{2,1,0:T(2,128)(2,1)S(1)} %reshape.932), channel_id=1, replica_groups=mesh['grp'=2,'dp'=8,'seq'=2] {'dp','seq'}, dimensions={0}, use_global_device_ids=true | all-gather | bytes 26112 | tf_op jit(solution)/shard_map/all_gather | solution.py:456
  87.9 2.6 copy.126
  92.7 17.6 %all-gather.5.cloned.1.call-done = bf16[1024,3072]{1,0:T(8,128)(2,1)} async-done(((bf16[64,3072]{1,0:T(8,128)(2,1)}), bf16[1024,3072]{1,0:T(8,128)(2,1)}) %all-gather.5.cloned.1.call-update) | async-done | bytes 6291472 | tf_op jit(solution)/shard_map/all_gather | solution.py:453
  110.3 17.3 %add_convert_fusion.q_ref.k_ref.v_ref = bf16[1536,3072]{1,0:T(8,128)(2,1)} fusion(bf16[1024,3072]{1,0:T(8,128)(2,1)} %all-gather.5.cloned.1.call-done, f32[3072]{0:T(1024)S(1)} %pad_maximum_fusion.7, bf16[512,1024]{0,1:T(8,128)(2,1)} %collective-permute-done, bf16[1024,1024]{0,1:T(8,128)(2,1)} %bitcast.569, pred[]{:T(512)S(6)} %eq.71), kind=kOutput, calls=%fused_computation.1 | convolution fusion | flops 9687269376 | bytes 18886656 | tf_op jit(solution)/shard_map/dot_general | solution.py:486
  127.9 52.6 %attend.1 = (bf16[1024,1024]{1,0:T(8,128)(2,1)S(1)}, f32[1024,1024]{1,0:T(8,128)}, f32[1024,128]{1,0:T(8,128)S(1)}) custom-call(s32[1]{0:T(128)} %bitcast.1.side_ref, s32[1536,128]{1,0:T(8,128)S(1)} %broadcast_in_dim.31.ids_col_ref, s32[8,1536]{1,0:T(8,128)S(1)} %broadcast_in_dim.32.ids_row_ref, bf16[1536,3072]{1,0:T(8,128)(2,1)} %add_convert_fusion.q_ref.k_ref.v_ref, ...), custom_call_target="tpu_custom_call" | custom-call | flops 18253611008 | bytes 31457280 | tf_op jit(solution)/shard_map/attend/pallas_call | solution.py:136
  182.0 6.3 fusion.145
  191.2 174.7 %all-gather.9.cloned.1.call-done = bf16[2,1024,4096]{2,1,0:T(8,128)(2,1)} async-done(((bf16[2,64,4096]{2,1,0:T(8,128)(2,1)}), bf16[2,1024,4096]{2,1,0:T(8,128)(2,1)}) %all-gather.9.cloned.1.call-update) | async-done | bytes 16777232 | tf_op jit(solution)/shard_map/all_gather | solution.py:455
  365.9 48.0 %multiply_convert_fusion = (bf16[1024,4096]{1,0:T(8,128)(2,1)}, f32[1024,4096]{1,0:T(8,128)}, f32[1024,4096]{1,0:T(8,128)}) fusion(f32[4096]{0:T(1024)S(1)} %slice.154, bf16[2,1024,4096]{2,1,0:T(8,128)(2,1)} %all-gather.9.cloned.1.call-done, bf16[1024,1024]{0,1:T(8,128)(2,1)S(1)} %fusion.132.clone.5), kind=kOutput, calls=%fused_computation.4 | convolution fusion | flops 8866758656 | bytes 52445184 | tf_op jit(solution)/shard_map/dot_general | solution.py:496
  414.0 14.8 %fusion.146 = (f32[1024]{0:T(1024)S(1)}, f32[1024,1024]{0,1:T(8,128)S(1)}) fusion(f32[1024]{0:T(1024)S(1)} %copy-done.66, bf16[1024,4096]{1,0:T(8,128)(2,1)} %get-tuple-element.171, bf16[2,1024,4096]{2,1,0:T(8,128)(2,1)} %all-gather.9.cloned.1.call-done, f32[1024]{0:T(1024)S(1)} %get-tuple-element.208, f32[1024]{0:T(1024)S(1)} %get-tuple-element.209, ...), kind=kOutput, calls=%fused_computation.339 | convolution fusion | flops 8597273600 | bytes 25190400 | tf_op jit(solution)/shard_map/dot_general | solution.py:500
  429.9 4.3 fusion.14
  434.2 3.4 fusion.134
  437.6 25.4 %fusion.147 = (bf16[4096]{0:T(1024)(128)(2,1)}, bf16[1024,4096]{1,0:T(8,128)(2,1)}) fusion(f32[1024,4096]{1,0:T(8,128)} %get-tuple-element.172, bf16[1024,1024]{0,1:T(8,128)(2,1)} %get-tuple-element.166, bf16[2,1024,4096]{2,1,0:T(8,128)(2,1)} %all-gather.9.cloned.1.call-done, f32[1024,4096]{1,0:T(8,128)} %get-tuple-element.221, f32[4096]{0:T(1024)S(1)} %slice.154), kind=kOutput, calls=%fused_computation.340 | convolution fusion | flops 8657039360 | bytes 52453376 | tf_op jit(solution)/shard_map/dot_general | solution.py:512
  463.0 17.9 %multiply_reduce_fusion = (bf16[1024]{0:T(1024)(128)(2,1)}, f32[1024]{0:T(1024)S(1)}, bf16[1024]{0:T(1024)(128)(2,1)}, f32[1024,1024]{0,1:T(8,128)}) fusion(f32[1024,1024]{0,1:T(8,128)S(1)} %copy-done.11, f32[1024]{0:T(1024)S(1)} %fusion.127, f32[1024]{0:T(1024)S(1)} %broadcast_multiply_fusion.1, f32[1024]{0:T(1024)S(1)} %get-tuple-element.209, ...), kind=kOutput, calls=%fused_computation.37 | convolution fusion | flops 8607757312 | bytes 31498240 | tf_op jit(solution)/shard_map/dot_general | solution.py:517
  480.9 3.3 fusion.136
  487.3 2.4 convolution_convert_fusion.3.do_ref
  489.8 2.4 fusion.15.inner_ref
  492.2 63.8 %attend_back.1 = (bf16[1024,1024]{1,0:T(8,128)(2,1)S(1)}, f32[1024,1024]{1,0:T(8,128)}, f32[1024,1024]{1,0:T(8,128)}) custom-call(s32[1]{0:T(128)} %bitcast.1.side_ref, s32[1536,128]{1,0:T(8,128)S(1)} %copy-done.3, s32[8,1536]{1,0:T(8,128)S(1)} %copy-done.7, bf16[1536,3072]{1,0:T(8,128)(2,1)} %add_convert_fusion.q_ref.k_ref.v_ref, ...), custom_call_target="tpu_custom_call" | custom-call | flops 45634027520 | bytes 41943040 | tf_op jit(solution)/shard_map/attend_back/pallas_call | solution.py:236
  557.2 3.7 convolution_convert_fusion.2
  560.9 11.8 %convolution_convert_fusion.1 = bf16[1024,4096]{1,0:T(8,128)(2,1)} fusion(bf16[1024,4096]{1,0:T(8,128)(2,1)S(1)} %bitcast.578, f32[1024,1024]{0,1:T(8,128)S(1)} %copy-done.11, f32[1024]{0:T(1024)S(1)} %get-tuple-element.208, f32[1024]{0:T(1024)S(1)} %get-tuple-element.209, f32[1024]{0:T(1024)S(1)} %fusion.127, f32[1024]{0:T(1024)S(1)} %broadcast_multiply_fusion.1), kind=kOutput, calls=%fused_computation.21 | convolution fusion | flops 8599371776 | bytes 20987904 | tf_op jit(solution)/shard_map/dot_general | solution.py:59
  572.7 3.3 fusion.138
  576.0 3.5 slice.176
  580.5 12.1 %convolution_convert_fusion = bf16[1024,4096]{1,0:T(8,128)(2,1)S(1)} fusion(bf16[1024,1024]{0,1:T(8,128)(2,1)S(1)} %copy-done.41, bf16[1024,4096]{1,0:T(8,128)(2,1)} %get-tuple-element.171), kind=kOutput, calls=%fused_computation.20 | convolution fusion | flops 8594128896 | bytes 18874368 | tf_op jit(solution)/shard_map/dot_general | solution.py:59
  608.3 3.9 copy.146
  613.0 3.2 collective-permute-done.28
  618.0 6.8 collective-permute-done.43
  626.6 14.9 %attend_far.1 = (bf16[1024,1024]{1,0:T(8,128)(2,1)S(1)}, bf16[1024,1024]{1,0:T(8,128)(2,1)}) custom-call(s32[1]{0:T(128)} %bitcast.1.side_ref, s32[1536,128]{1,0:T(8,128)S(1)} %copy-done.3, s32[8,1536]{1,0:T(8,128)S(1)} %copy-done.7, bf16[1536,3072]{1,0:T(8,128)(2,1)} %add_convert_fusion.q_ref.k_ref.v_ref, ...), custom_call_target="tpu_custom_call" | custom-call | flops 8589934592 | bytes 20971520 | tf_op jit(solution)/shard_map/attend_far/pallas_call | solution.py:321
  645.4 3.9 reduce.1
  649.3 11.5 %convert_bitcast_fusion = bf16[1024,3072]{1,0:T(8,128)(2,1)} fusion(bf16[1024,3072]{1,0:T(8,128)(2,1)} %constant_dynamic-update-slice_fusion, bf16[1,1024,1024]{2,1,0:T(8,128)(2,1)S(1)} %copy-done.38), kind=kOutput, calls=%fused_computation.26 | convolution fusion | flops 6445596672 | bytes 14680064 | tf_op jit(solution)/shard_map/dot_general | solution.py:59
  661.7 3.2 fusion.25
  664.9 3.0 copy.135
  670.0 2.9 fusion.50
  674.2 2.2 fusion.48
  676.4 3.5 collective-permute-start.45
  679.8 4.9 fusion.140
  684.8 11.3 %add_bitcast_fusion = f32[1,1024,1024]{1,2,0:T(8,128)} fusion(f32[1024,1024]{0,1:T(8,128)S(1)} %copy-done.15, f32[1024]{0:T(1024)S(1)} %copy-done.58, bf16[1024,3072]{1,0:T(8,128)(2,1)} %constant_dynamic-update-slice_fusion, bf16[1024,3072]{1,0:T(8,128)(2,1)S(1)} %bitcast.576), kind=kOutput, calls=%fused_computation.38 | convolution fusion | flops 6444548096 | bytes 20975616 | tf_op jit(solution)/shard_map/dot_general | solution.py:556
  696.1 5.3 copy.147
  714.8 3.9 collective-permute-done.13
  720.2 27.9 %collective-permute-done.31 = bf16[2,64,1024]{2,1,0:T(8,128)(2,1)S(1)} collective-permute-done((bf16[2,64,1024]{2,1,0:T(8,128)(2,1)S(1)}, bf16[2,64,1024]{2,1,0:T(8,128)(2,1)S(1)}, u32[]{:S(2)}, u32[]{:S(2)}) %collective-permute-start.31) | collective-permute-done | bytes 262176 | tf_op jit(solution)/shard_map/ppermute | solution.py:373
  758.6 4.8 collective-permute-done.47
  768.4 5.3 collective-permute-done.24
  774.8 9.0 collective-permute-done.34
  786.5 5.2 collective-permute-done.20
  792.7 2.9 collective-permute-done.25
  796.7 3.4 collective-permute-done.35
  801.1 4.1 collective-permute-done.40
  806.0 2.3 fusion.43
  808.2 4.4 collective-permute-done.8
  820.1 2.2 collective-permute-done.41
  822.4 2.1 collective-permute-start.37
  825.5 2.7 collective-permute-done.22
  833.7 2.3 collective-permute-done.42
  836.3 3.0 fusion.33
  841.3 2.6 fusion.26
  843.9 2.6 collective-permute-done.17
  857.9 7.8 collective-permute-done.5
  866.9 2.3 collective-permute-done.10
  870.5 4.0 collective-permute-done.6
  875.8 3.4 collective-permute-done.11
  880.3 3.2 collective-permute-done.7
  884.7 3.1 collective-permute-done.12
  890.4 4.6 multiply_subtract_fusion
  (357 shorter events, 123.7 us)
Async XLA Ops:
  7.2 84.3 %copy-start = (s32[1,2048]{1,0:T(1,128)S(1)}, s32[1,2048]{1,0:T(1,128)}, u32[]{:S(2)}) copy-start(s32[1,2048]{1,0:T(1,128)} %param.21) | copy-start | bytes 24580
  7.2 103.1 %all-gather.5.cloned.1.call-start = ((), (), s32[]{:S(2)}) async-start(), calls=%async_computation | async-start | bytes 6684672 | tf_op jit(solution)/shard_map/all_gather | solution.py:453
  9.2 172.8 %all-gather.7.cloned.1.call-start = ((), (), s32[]{:S(2)}) async-start(), calls=%async_computation.1 | async-start | bytes 2228224 | tf_op jit(solution)/shard_map/all_gather | solution.py:454
  10.9 355.0 %all-gather.9.cloned.1.call-start = ((), (), s32[]{:S(2)}) async-start(), calls=%async_computation.2 | async-start | bytes 17825792 | tf_op jit(solution)/shard_map/all_gather | solution.py:455
  13.7 74.3 %copy-start.28 = (bf16[1,1024,1024]{2,1,0:T(8,128)(2,1)S(1)}, bf16[1,1024,1024]{2,1,0:T(8,128)(2,1)}, u32[]{:S(2)}) copy-start(bf16[1,1024,1024]{2,1,0:T(8,128)(2,1)} %param.20) | copy-start | bytes 6291460
  19.4 73.3 %collective-permute-start = (bf16[512,1024]{0,1:T(8,128)(2,1)S(1)}, bf16[512,1024]{0,1:T(8,128)(2,1)}, u32[]{:S(2)}, u32[]{:S(2)}) collective-permute-start(bf16[512,1024]{0,1:T(8,128)(2,1)S(1)} %fusion.46), channel_id=1, source_target_pairs={{0,1},{1,0},{2,3},{3,2},{4,5},{5,4},{6,7},{7,6},{8,9},{9,8},{10,11... | collective-permute-start | bytes 3145736 | tf_op jit(solution)/shard_map/ppermute | solution.py:28
  188.8 225.1 %copy-start.54 = (f32[1024]{0:T(1024)}, f32[1024]{0:T(1024)S(1)}, u32[]{:S(2)}) copy-start(f32[1024]{0:T(1024)S(1)} %multiply_reduce_fusion.3) | copy-start | bytes 12292
  191.2 222.7 %copy-start.66 = (f32[1024]{0:T(1024)S(1)}, f32[1024]{0:T(1024)}, u32[]{:S(2)}) copy-start(f32[1024]{0:T(1024)} %get-tuple-element.207) | copy-start | bytes 12292
  365.9 48.0 %copy-start.11 = (f32[1024,1024]{0,1:T(8,128)S(1)}, f32[1024,1024]{0,1:T(8,128)}, u32[]{:S(2)}) copy-start(f32[1024,1024]{0,1:T(8,128)} %copy-done.10) | copy-start | bytes 12582916
  492.2 65.0 %copy-start.9 = (bf16[1024,1024]{1,0:T(8,128)(2,1)S(1)}, bf16[1024,1024]{1,0:T(8,128)(2,1)}, u32[]{:S(2)}) copy-start(bf16[1024,1024]{1,0:T(8,128)(2,1)} %copy-done.8) | copy-start | bytes 6291460
  593.4 18.8 %collective-permute-start.2 = (f32[512,32]{1,0:T(8,128)}, f32[512,32]{1,0:T(8,128)S(1)}, u32[]{:S(2)}, u32[]{:S(2)}) collective-permute-start(f32[512,32]{1,0:T(8,128)} %pad_maximum_fusion.6), channel_id=1, source_target_pairs={{0,1},{1,0},{2,3},{3,2},{4,5},{5,4},{6,7},{7,6},{8,9},{9,8},{10,11... | collective-permute-start | bytes 196616 | tf_op jit(solution)/shard_map/ppermute | solution.py:28
  594.9 31.4 %collective-permute-start.1 = (bf16[512,1024]{1,0:T(8,128)(2,1)}, bf16[512,1024]{1,0:T(8,128)(2,1)S(1)}, u32[]{:S(2)}, u32[]{:S(2)}) collective-permute-start(bf16[512,1024]{1,0:T(8,128)(2,1)} %slice_select_fusion), channel_id=1, source_target_pairs={{0,1},{1,0},{2,3},{3,2},{4,5},{5,4},{6,7},{7,6},{8,9},{9,8},{10,11... | collective-permute-start | bytes 3145736 | tf_op jit(solution)/shard_map/ppermute | solution.py:28
  596.8 108.9 %collective-permute-start.18 = (bf16[4,2,64,1536]{3,2,1,0:T(8,128)(2,1)}, bf16[4,2,64,1536]{3,2,1,0:T(8,128)(2,1)}, u32[]{:S(2)}, u32[]{:S(2)}) collective-permute-start(bf16[4,2,64,1536]{3,2,1,0:T(8,128)(2,1)} %dynamic-slice_bitcast_fusion.3), channel_id=1, source_target_pairs={{0,1},{1,0},{2,3},{3,2},{4,5},{5,4},{6,7},{7,6},{8,9},{9,8},{10,11... | collective-permute-start | bytes 4718600 | tf_op jit(solution)/shard_map/ppermute | solution.py:373
  599.5 16.6 %collective-permute-start.28 = (bf16[2,2,64,1024]{3,2,1,0:T(8,128)(2,1)S(1)}, bf16[2,2,64,1024]{3,2,1,0:T(8,128)(2,1)S(1)}, u32[]{:S(2)}, u32[]{:S(2)}) collective-permute-start(bf16[2,2,64,1024]{3,2,1,0:T(8,128)(2,1)S(1)} %dynamic-slice_bitcast_fusion.7), channel_id=1, source_target_pairs={{0,4},{2,6},{4,8},{6,10},{8,12},{10,14},{12,0},{14,2},{1,5},{3,7},... | collective-permute-start | bytes 1572872 | tf_op jit(solution)/shard_map/ppermute | solution.py:376
  604.7 20.1 %collective-permute-start.43 = (bf16[2,2,64,1024]{3,2,1,0:T(8,128)(2,1)}, bf16[2,2,64,1024]{3,2,1,0:T(8,128)(2,1)}, u32[]{:S(2)}, u32[]{:S(2)}) collective-permute-start(bf16[2,2,64,1024]{3,2,1,0:T(8,128)(2,1)} %dynamic-slice_bitcast_fusion.6), channel_id=1, source_target_pairs={{0,4},{2,6},{4,8},{6,10},{8,12},{10,14},{12,0},{14,2},{1,5},{3,7},... | collective-permute-start | bytes 1572872 | tf_op jit(solution)/shard_map/ppermute | solution.py:376
  612.2 100.0 %collective-permute-start.23 = (bf16[4,2,64,1536]{3,2,1,0:T(8,128)(2,1)}, bf16[4,2,64,1536]{3,2,1,0:T(8,128)(2,1)}, u32[]{:S(2)}, u32[]{:S(2)}) collective-permute-start(bf16[4,2,64,1536]{3,2,1,0:T(8,128)(2,1)} %dynamic-slice_bitcast_fusion.2), channel_id=1, source_target_pairs={{0,2},{2,0},{4,6},{6,4},{8,10},{10,8},{12,14},{14,12},{1,3},{3,1},... | collective-permute-start | bytes 4718600 | tf_op jit(solution)/shard_map/ppermute | solution.py:377
  616.2 93.6 %collective-permute-start.33 = (bf16[4,2,64,1536]{3,2,1,0:T(8,128)(2,1)}, bf16[4,2,64,1536]{3,2,1,0:T(8,128)(2,1)}, u32[]{:S(2)}, u32[]{:S(2)}) collective-permute-start(bf16[4,2,64,1536]{3,2,1,0:T(8,128)(2,1)} %dynamic-slice_bitcast_fusion.1), channel_id=1, source_target_pairs={{0,1},{1,0},{2,3},{3,2},{4,5},{5,4},{6,7},{7,6},{8,9},{9,8},{10,11... | collective-permute-start | bytes 4718600 | tf_op jit(solution)/shard_map/ppermute | solution.py:373
  624.8 45.2 %collective-permute-start.29 = (bf16[2,2,64,1024]{3,2,1,0:T(8,128)(2,1)S(1)}, bf16[2,2,64,1024]{3,2,1,0:T(8,128)(2,1)}, u32[]{:S(2)}, u32[]{:S(2)}) collective-permute-start(bf16[2,2,64,1024]{3,2,1,0:T(8,128)(2,1)S(1)} %fusion.49), channel_id=1, source_target_pairs={{0,4},{2,6},{4,8},{6,10},{8,12},{10,14},{12,0},{14,2},{1,5},{3,7},... | collective-permute-start | bytes 1572872 | tf_op jit(solution)/shard_map/ppermute | solution.py:376
  626.3 47.9 %collective-permute-start.44 = (bf16[2,2,64,1024]{3,2,1,0:T(8,128)(2,1)S(1)}, bf16[2,2,64,1024]{3,2,1,0:T(8,128)(2,1)}, u32[]{:S(2)}, u32[]{:S(2)}) collective-permute-start(bf16[2,2,64,1024]{3,2,1,0:T(8,128)(2,1)S(1)} %fusion.47), channel_id=1, source_target_pairs={{0,4},{2,6},{4,8},{6,10},{8,12},{10,14},{12,0},{14,2},{1,5},{3,7},... | collective-permute-start | bytes 1572872 | tf_op jit(solution)/shard_map/ppermute | solution.py:376
  672.9 30.4 %collective-permute-start.30 = (bf16[2,2,64,1024]{3,2,1,0:T(8,128)(2,1)}, bf16[2,2,64,1024]{3,2,1,0:T(8,128)(2,1)}, u32[]{:S(2)}, u32[]{:S(2)}) collective-permute-start(bf16[2,2,64,1024]{3,2,1,0:T(8,128)(2,1)} %fusion.50), channel_id=1, source_target_pairs={{0,4},{2,6},{4,8},{6,10},{8,12},{10,14},{12,0},{14,2},{1,5},{3,7},... | collective-permute-start | bytes 1572872 | tf_op jit(solution)/shard_map/ppermute | solution.py:376
  676.4 31.0 %collective-permute-start.45 = (bf16[2,2,64,1024]{3,2,1,0:T(8,128)(2,1)}, bf16[2,2,64,1024]{3,2,1,0:T(8,128)(2,1)}, u32[]{:S(2)}, u32[]{:S(2)}) collective-permute-start(bf16[2,2,64,1024]{3,2,1,0:T(8,128)(2,1)} %fusion.48), channel_id=1, source_target_pairs={{0,4},{2,6},{4,8},{6,10},{8,12},{10,14},{12,0},{14,2},{1,5},{3,7},... | collective-permute-start | bytes 1572872 | tf_op jit(solution)/shard_map/ppermute | solution.py:376
  684.7 129.1 %copy-start.16 = (bf16[1024,1536]{1,0:T(8,128)(2,1)}, bf16[1024,1536]{1,0:T(8,128)(2,1)S(1)}, u32[]{:S(2)}) copy-start(bf16[1024,1536]{1,0:T(8,128)(2,1)S(1)} %get-tuple-element.178) | copy-start | bytes 9437188
  703.3 46.3 %collective-permute-start.38 = (bf16[4,2,64,1536]{3,2,1,0:T(8,128)(2,1)S(1)}, bf16[4,2,64,1536]{3,2,1,0:T(8,128)(2,1)S(1)}, u32[]{:S(2)}, u32[]{:S(2)}) collective-permute-start(bf16[4,2,64,1536]{3,2,1,0:T(8,128)(2,1)S(1)} %copy-done.45), channel_id=1, source_target_pairs={{0,2},{2,0},{4,6},{6,4},{8,10},{10,8},{12,14},{14,12},{1,3},{3,1},... | collective-permute-start | bytes 4718600 | tf_op jit(solution)/shard_map/ppermute | solution.py:377
  705.7 13.0 %collective-permute-start.13 = (bf16[2,2,64,1152]{3,2,0,1:T(8,128)(2,1)S(1)}, bf16[2,2,64,1152]{3,2,0,1:T(8,128)(2,1)S(1)}, u32[]{:S(2)}, u32[]{:S(2)}) collective-permute-start(bf16[2,2,64,1152]{3,2,0,1:T(8,128)(2,1)S(1)} %bitcast.572), channel_id=1, source_target_pairs={{0,4},{2,6},{4,8},{6,10},{8,12},{10,14},{12,0},{14,2},{1,5},{3,7},... | collective-permute-start | bytes 1769480 | tf_op jit(solution)/shard_map/ppermute | solution.py:376
  707.4 43.9 %copy-start.22 = (bf16[1024,1536]{1,0:T(8,128)(2,1)S(1)}, bf16[1024,1536]{1,0:T(8,128)(2,1)}, u32[]{:S(2)}) copy-start(bf16[1024,1536]{1,0:T(8,128)(2,1)} %copy-done.21) | copy-start | bytes 9437188
  707.4 97.9 %collective-permute-start.3 = (bf16[4,2,64,1536]{3,2,1,0:T(8,128)(2,1)S(1)}, bf16[4,2,64,1536]{3,2,1,0:T(8,128)(2,1)S(1)}, u32[]{:S(2)}, u32[]{:S(2)}) collective-permute-start(bf16[4,2,64,1536]{3,2,1,0:T(8,128)(2,1)S(1)} %dynamic-slice_bitcast_fusion.5), channel_id=1, source_target_pairs={{0,1},{1,0},{2,3},{3,2},{4,5},{5,4},{6,7},{7,6},{8,9},{9,8},{10,11... | collective-permute-start | bytes 4718600 | tf_op jit(solution)/shard_map/ppermute | solution.py:373
  709.8 56.6 %collective-permute-start.19 = (bf16[4,64,1536]{2,1,0:T(8,128)(2,1)S(1)}, bf16[4,64,1536]{2,1,0:T(8,128)(2,1)S(1)}, u32[]{:S(2)}, u32[]{:S(2)}) collective-permute-start(bf16[4,64,1536]{2,1,0:T(8,128)(2,1)S(1)} %fusion.41), channel_id=1, source_target_pairs={{0,2},{2,0},{4,6},{6,4},{8,10},{10,8},{12,14},{14,12},{1,3},{3,1},... | collective-permute-start | bytes 2359304 | tf_op jit(solution)/shard_map/ppermute | solution.py:377
  712.2 53.9 %copy-start.35 = (bf16[1,2,2,64,1152]{4,3,2,1,0:T(8,128)(2,1)S(1)}, bf16[1,2,2,64,1152]{4,3,2,1,0:T(8,128)(2,1)}, u32[]{:S(2)}) copy-start(bf16[1,2,2,64,1152]{4,3,2,1,0:T(8,128)(2,1)} %get-tuple-element.180) | copy-start | bytes 1769476
  712.3 35.9 %collective-permute-start.31 = (bf16[2,64,1024]{2,1,0:T(8,128)(2,1)S(1)}, bf16[2,64,1024]{2,1,0:T(8,128)(2,1)S(1)}, u32[]{:S(2)}, u32[]{:S(2)}) collective-permute-start(bf16[2,64,1024]{2,1,0:T(8,128)(2,1)S(1)} %fusion.67), channel_id=1, source_target_pairs={{0,1},{1,0},{2,3},{3,2},{4,5},{5,4},{6,7},{7,6},{8,9},{9,8},{10,11... | collective-permute-start | bytes 786440 | tf_op jit(solution)/shard_map/ppermute | solution.py:373
  718.7 34.5 %collective-permute-start.46 = (bf16[2,64,1024]{2,1,0:T(8,128)(2,1)S(1)}, bf16[2,64,1024]{2,1,0:T(8,128)(2,1)S(1)}, u32[]{:S(2)}, u32[]{:S(2)}) collective-permute-start(bf16[2,64,1024]{2,1,0:T(8,128)(2,1)S(1)} %fusion.66), channel_id=1, source_target_pairs={{0,1},{1,0},{2,3},{3,2},{4,5},{5,4},{6,7},{7,6},{8,9},{9,8},{10,11... | collective-permute-start | bytes 786440 | tf_op jit(solution)/shard_map/ppermute | solution.py:373
  748.1 16.9 %collective-permute-start.14 = (bf16[2,2,64,1152]{3,2,0,1:T(8,128)(2,1)S(1)}, bf16[2,2,64,1152]{3,2,0,1:T(8,128)(2,1)S(1)}, u32[]{:S(2)}, u32[]{:S(2)}) collective-permute-start(bf16[2,2,64,1152]{3,2,0,1:T(8,128)(2,1)S(1)} %fusion.44), channel_id=1, source_target_pairs={{0,4},{2,6},{4,8},{6,10},{8,12},{10,14},{12,0},{14,2},{1,5},{3,7},... | collective-permute-start | bytes 1769480 | tf_op jit(solution)/shard_map/ppermute | solution.py:376
  749.6 7.4 collective-permute-start.32
  753.3 20.4 %collective-permute-start.24 = (bf16[4,64,1536]{2,1,0:T(8,128)(2,1)S(1)}, bf16[4,64,1536]{2,1,0:T(8,128)(2,1)S(1)}, u32[]{:S(2)}, u32[]{:S(2)}) collective-permute-start(bf16[4,64,1536]{2,1,0:T(8,128)(2,1)S(1)} %fusion.40), channel_id=1, source_target_pairs={{0,1},{1,0},{2,3},{3,2},{4,5},{5,4},{6,7},{7,6},{8,9},{9,8},{10,11... | collective-permute-start | bytes 2359304 | tf_op jit(solution)/shard_map/ppermute | solution.py:373
  757.0 6.4 collective-permute-start.47
  763.4 20.4 %collective-permute-start.34 = (bf16[4,64,1536]{2,1,0:T(8,128)(2,1)S(1)}, bf16[4,64,1536]{2,1,0:T(8,128)(2,1)S(1)}, u32[]{:S(2)}, u32[]{:S(2)}) collective-permute-start(bf16[4,64,1536]{2,1,0:T(8,128)(2,1)S(1)} %fusion.39), channel_id=1, source_target_pairs={{0,2},{2,0},{4,6},{6,4},{8,10},{10,8},{12,14},{14,12},{1,3},{3,1},... | collective-permute-start | bytes 2359304 | tf_op jit(solution)/shard_map/ppermute | solution.py:377
  765.0 20.4 %collective-permute-start.39 = (bf16[4,64,1536]{2,1,0:T(8,128)(2,1)S(1)}, bf16[4,64,1536]{2,1,0:T(8,128)(2,1)S(1)}, u32[]{:S(2)}, u32[]{:S(2)}) collective-permute-start(bf16[4,64,1536]{2,1,0:T(8,128)(2,1)S(1)} %fusion.38), channel_id=1, source_target_pairs={{0,1},{1,0},{2,3},{3,2},{4,5},{5,4},{6,7},{7,6},{8,9},{9,8},{10,11... | collective-permute-start | bytes 2359304 | tf_op jit(solution)/shard_map/ppermute | solution.py:373
  766.4 46.3 %collective-permute-start.8 = (bf16[4,2,64,1536]{3,2,1,0:T(8,128)(2,1)S(1)}, bf16[4,2,64,1536]{3,2,1,0:T(8,128)(2,1)S(1)}, u32[]{:S(2)}, u32[]{:S(2)}) collective-permute-start(bf16[4,2,64,1536]{3,2,1,0:T(8,128)(2,1)S(1)} %dynamic-slice_bitcast_fusion.4), channel_id=1, source_target_pairs={{0,2},{2,0},{4,6},{6,4},{8,10},{10,8},{12,14},{14,12},{1,3},{3,1},... | collective-permute-start | bytes 4718600 | tf_op jit(solution)/shard_map/ppermute | solution.py:377
  773.7 48.7 %collective-permute-start.15 = (bf16[2,2,64,1152]{3,2,0,1:T(8,128)(2,1)S(1)}, bf16[2,2,64,1152]{3,2,0,1:T(8,128)(2,1)S(1)}, u32[]{:S(2)}, u32[]{:S(2)}) collective-permute-start(bf16[2,2,64,1152]{3,2,0,1:T(8,128)(2,1)S(1)} %fusion.45), channel_id=1, source_target_pairs={{0,4},{2,6},{4,8},{6,10},{8,12},{10,14},{12,0},{14,2},{1,5},{3,7},... | collective-permute-start | bytes 1769480 | tf_op jit(solution)/shard_map/ppermute | solution.py:376
  783.8 7.9 collective-permute-start.20
  785.4 10.3 %collective-permute-start.25 = (bf16[64,1536]{1,0:T(8,128)(2,1)S(1)}, bf16[64,1536]{1,0:T(8,128)(2,1)S(1)}, u32[]{:S(2)}, u32[]{:S(2)}) collective-permute-start(bf16[64,1536]{1,0:T(8,128)(2,1)S(1)} %fusion.80), channel_id=1, source_target_pairs={{0,4},{2,6},{4,8},{6,10},{8,12},{10,14},{12,0},{14,2},{1,5},{3,7},... | collective-permute-start | bytes 589832 | tf_op jit(solution)/shard_map/ppermute | solution.py:376
  791.7 8.4 collective-permute-start.35
  795.6 9.6 %collective-permute-start.40 = (bf16[64,1536]{1,0:T(8,128)(2,1)S(1)}, bf16[64,1536]{1,0:T(8,128)(2,1)S(1)}, u32[]{:S(2)}, u32[]{:S(2)}) collective-permute-start(bf16[64,1536]{1,0:T(8,128)(2,1)S(1)} %fusion.68), channel_id=1, source_target_pairs={{0,4},{2,6},{4,8},{6,10},{8,12},{10,14},{12,0},{14,2},{1,5},{3,7},... | collective-permute-start | bytes 589832 | tf_op jit(solution)/shard_map/ppermute | solution.py:376
  800.1 14.8 %collective-permute-start.21 = (bf16[64,1536]{1,0:T(8,128)(2,1)S(1)}, bf16[64,1536]{1,0:T(8,128)(2,1)S(1)}, u32[]{:S(2)}, u32[]{:S(2)}) collective-permute-start(bf16[64,1536]{1,0:T(8,128)(2,1)S(1)} %fusion.88), channel_id=1, source_target_pairs={{0,4},{2,6},{4,8},{6,10},{8,12},{10,14},{12,0},{14,2},{1,5},{3,7},... | collective-permute-start | bytes 589832 | tf_op jit(solution)/shard_map/ppermute | solution.py:376
  805.2 11.0 %collective-permute-start.26 = (bf16[64,1536]{1,0:T(8,128)(2,1)S(1)}, bf16[64,1536]{1,0:T(8,128)(2,1)S(1)}, u32[]{:S(2)}, u32[]{:S(2)}) collective-permute-start(bf16[64,1536]{1,0:T(8,128)(2,1)S(1)} %fusion.82), channel_id=1, source_target_pairs={{0,4},{2,6},{4,8},{6,10},{8,12},{10,14},{12,0},{14,2},{1,5},{3,7},... | collective-permute-start | bytes 589832 | tf_op jit(solution)/shard_map/ppermute | solution.py:376
  805.3 13.4 %collective-permute-start.36 = (bf16[64,1536]{1,0:T(8,128)(2,1)S(1)}, bf16[64,1536]{1,0:T(8,128)(2,1)S(1)}, u32[]{:S(2)}, u32[]{:S(2)}) collective-permute-start(bf16[64,1536]{1,0:T(8,128)(2,1)S(1)} %fusion.76), channel_id=1, source_target_pairs={{0,4},{2,6},{4,8},{6,10},{8,12},{10,14},{12,0},{14,2},{1,5},{3,7},... | collective-permute-start | bytes 589832 | tf_op jit(solution)/shard_map/ppermute | solution.py:376
  812.7 9.6 %collective-permute-start.41 = (bf16[64,1536]{1,0:T(8,128)(2,1)S(1)}, bf16[64,1536]{1,0:T(8,128)(2,1)S(1)}, u32[]{:S(2)}, u32[]{:S(2)}) collective-permute-start(bf16[64,1536]{1,0:T(8,128)(2,1)S(1)} %fusion.70), channel_id=1, source_target_pairs={{0,4},{2,6},{4,8},{6,10},{8,12},{10,14},{12,0},{14,2},{1,5},{3,7},... | collective-permute-start | bytes 589832 | tf_op jit(solution)/shard_map/ppermute | solution.py:376
  814.9 39.7 %collective-permute-start.4 = (bf16[4,64,1536]{2,1,0:T(8,128)(2,1)}, bf16[4,64,1536]{2,1,0:T(8,128)(2,1)}, u32[]{:S(2)}, u32[]{:S(2)}) collective-permute-start(bf16[4,64,1536]{2,1,0:T(8,128)(2,1)} %fusion.43), channel_id=1, source_target_pairs={{0,2},{2,0},{4,6},{6,4},{8,10},{10,8},{12,14},{14,12},{1,3},{3,1},... | collective-permute-start | bytes 2359304 | tf_op jit(solution)/shard_map/ppermute | solution.py:377
  816.3 39.8 %collective-permute-start.9 = (bf16[4,64,1536]{2,1,0:T(8,128)(2,1)}, bf16[4,64,1536]{2,1,0:T(8,128)(2,1)}, u32[]{:S(2)}, u32[]{:S(2)}) collective-permute-start(bf16[4,64,1536]{2,1,0:T(8,128)(2,1)} %fusion.42), channel_id=1, source_target_pairs={{0,1},{1,0},{2,3},{3,2},{4,5},{5,4},{6,7},{7,6},{8,9},{9,8},{10,11... | collective-permute-start | bytes 2359304 | tf_op jit(solution)/shard_map/ppermute | solution.py:373
  818.8 9.4 %collective-permute-start.22 = (bf16[64,1536]{1,0:T(8,128)(2,1)S(1)}, bf16[64,1536]{1,0:T(8,128)(2,1)S(1)}, u32[]{:S(2)}, u32[]{:S(2)}) collective-permute-start(bf16[64,1536]{1,0:T(8,128)(2,1)S(1)} %fusion.90), channel_id=1, source_target_pairs={{0,4},{2,6},{4,8},{6,10},{8,12},{10,14},{12,0},{14,2},{1,5},{3,7},... | collective-permute-start | bytes 589832 | tf_op jit(solution)/shard_map/ppermute | solution.py:376
  822.2 8.1 collective-permute-start.27
  822.4 10.1 %collective-permute-start.37 = (bf16[64,1536]{1,0:T(8,128)(2,1)S(1)}, bf16[64,1536]{1,0:T(8,128)(2,1)S(1)}, u32[]{:S(2)}, u32[]{:S(2)}) collective-permute-start(bf16[64,1536]{1,0:T(8,128)(2,1)S(1)} %fusion.78), channel_id=1, source_target_pairs={{0,4},{2,6},{4,8},{6,10},{8,12},{10,14},{12,0},{14,2},{1,5},{3,7},... | collective-permute-start | bytes 589832 | tf_op jit(solution)/shard_map/ppermute | solution.py:376
  828.2 7.7 collective-permute-start.42
  830.3 8.9 collective-permute-start.16
  839.2 51.1 %collective-permute-start.50 = (bf16[2,64,4096]{2,1,0:T(8,128)(2,1)S(1)}, bf16[2,64,4096]{2,1,0:T(8,128)(2,1)}, u32[]{:S(2)}, u32[]{:S(2)}) collective-permute-start(bf16[2,64,4096]{2,1,0:T(8,128)(2,1)S(1)} %get-tuple-element.183), channel_id=1, source_target_pairs={{0,16},{16,0},{1,17},{17,1},{2,18},{18,2},{3,19},{19,3},{4,20},{20... | collective-permute-start | bytes 3145736 | tf_op jit(solution)/shard_map/ppermute | solution.py:28
  840.2 6.3 collective-permute-start.17
  849.1 2.6 collective-permute-start.51
  851.3 1.5 collective-permute-start.49
  856.0 9.6 %collective-permute-start.5 = (bf16[64,1536]{1,0:T(8,128)(2,1)S(1)}, bf16[64,1536]{1,0:T(8,128)(2,1)S(1)}, u32[]{:S(2)}, u32[]{:S(2)}) collective-permute-start(bf16[64,1536]{1,0:T(8,128)(2,1)S(1)} %fusion.98), channel_id=1, source_target_pairs={{0,4},{2,6},{4,8},{6,10},{8,12},{10,14},{12,0},{14,2},{1,5},{3,7},... | collective-permute-start | bytes 589832 | tf_op jit(solution)/shard_map/ppermute | solution.py:376
  857.2 12.0 %collective-permute-start.10 = (bf16[64,1536]{1,0:T(8,128)(2,1)S(1)}, bf16[64,1536]{1,0:T(8,128)(2,1)S(1)}, u32[]{:S(2)}, u32[]{:S(2)}) collective-permute-start(bf16[64,1536]{1,0:T(8,128)(2,1)S(1)} %fusion.92), channel_id=1, source_target_pairs={{0,4},{2,6},{4,8},{6,10},{8,12},{10,14},{12,0},{14,2},{1,5},{3,7},... | collective-permute-start | bytes 589832 | tf_op jit(solution)/shard_map/ppermute | solution.py:376
  866.8 7.6 collective-permute-start.6
  870.4 8.7 collective-permute-start.11
  875.7 7.8 collective-permute-start.7
  880.3 7.5 collective-permute-start.12
  890.4 6.0 collective-permute-start.48
  (68 other events, 651.5 us)
Sparse Core Ops, SparseCore 0:
  11.5 98.7 all-gather.4
  113.6 59.0 all-gather.6
  176.0 189.8 all-gather.8

commit v2 on v1

--- a/solution.py
+++ b/solution.py
@@ -350,7 +350,10 @@
     )(side, ids_col, ids_row, qkv, qkv, qkv, far_outgrad, far_lse, far_inner, dk, dv)
 
 
-COLOURS = ((("y", "x", "z"), 3), (("x", "y", "z"), 3), (("z", "y", "x"), 2))
+AXES = ("z", "x", "y")
+GATHER_ORDERS = ((("z", "x", "y"), 3), (("z", "y", "x"), 3), (("x", "y", "z"), 2))
+SCATTER_ORDERS = ((("y", "x", "z"), 3), (("x", "y", "z"), 3), (("z", "y", "x"), 2))
+PIECE = 2048
 
 
 def axis_parts():
@@ -359,64 +362,306 @@
     return {"z": total // inner, "x": inner, "y": lax.axis_size("seq")}
 
 
-def place(axis):
+def places():
     inner = axis_parts()["x"]
-    if axis == "y":
-        return lax.axis_index("seq")
-    return lax.axis_index("dp") // inner if axis == "z" else lax.axis_index("dp") % inner
-
-
-def shift(x, axis):
+    row = lax.axis_index("dp")
+    return {"z": lax.div(row, inner), "x": lax.rem(row, inner), "y": lax.axis_index("seq")}
+
+
+def neighbour(axis, step):
+    parts, spots = axis_parts(), places()
+    size = parts[axis]
+    spots[axis] = lax.rem(spots[axis] + step + size, size)
+    return (lax.axis_index("grp"), spots["z"] * parts["x"] + spots["x"], spots["y"])
+
+
+def twin():
+    return (1 - lax.axis_index("grp"), lax.axis_index("dp"), lax.axis_index("seq"))
+
+
+def greet(peers):
+    barrier = pltpu.get_barrier_semaphore()
+    for peer in peers:
+        pl.semaphore_signal(barrier, inc=1, device_id=peer, device_id_type=pl.DeviceIdType.MESH)
+    pl.semaphore_wait(barrier, len(peers))
+
+
+def ring_peers():
+    return [neighbour(axis, step) for axis in AXES for step in (1, -1)]
+
+
+def flows_of(widths, orders):
+    flows = []
+    for member, width in enumerate(widths):
+        pieces = max(1, width // PIECE)
+        for piece in range(pieces):
+            tiles, begin = width // pieces // 128, piece * (width // pieces)
+            if tiles < len(orders):
+                flows.append((member, orders[0][0], begin, tiles * 128, piece))
+                continue
+            total = sum(share for _, share in orders)
+            low, used = 0, 0
+            for order, share in orders:
+                used += share
+                high = -(-used * tiles // total)
+                flows.append((member, order, begin + low * 128, (high - low) * 128, piece))
+                low = high
+    return flows
+
+
+def delays(flows, gap):
+    seen, found = [], []
+    for member, _, _, _, piece in flows:
+        if (member, piece) not in seen:
+            seen.append((member, piece))
+        found.append((len(seen) - 1) * gap)
+    return found
+
+
+def gather_kernel(shared, *refs):
+    count = len(shared)
+    shards, wholes = refs[:count], refs[count : 2 * count]
+    send_sems, recv_sems, own_sems = refs[2 * count :]
+    parts, spots = axis_parts(), places()
+    core = lax.axis_index("grp")
+    greet(ring_peers() + [twin()])
+    spans = [s.shape[1] if shared[m] else s.shape[1] // 2 for m, s in enumerate(shards)]
+
+    def columns(member, begin, width):
+        if shared[member]:
+            return pl.ds(begin, width)
+        return pl.ds(pl.multiple_of(core * spans[member] + begin, 128), width)
+
+    own = []
+    for member in range(count):
+        cut = columns(member, 0, spans[member])
+        own.append(
+            pltpu.make_async_copy(
+                shards[member].at[:, cut],
+                wholes[member].at[spots["z"], spots["x"], spots["y"], :, cut],
+                own_sems.at[member],
+            )
+        )
+        own[-1].start()
+
+    flows = flows_of(spans, GATHER_ORDERS)
+    chains = []
+    for member, order, begin, width, _ in flows:
+        cut = columns(member, begin, width)
+        steps, done = [], []
+        for axis in order:
+            for turn in range(parts[axis] - 1):
+                select = []
+                for a in AXES:
+                    if a == axis:
+                        select.append(pl.ds(lax.rem(spots[a] + parts[a] - turn, parts[a]), 1))
+                    elif a in done:
+                        select.append(pl.ds(0, parts[a]))
+                    else:
+                        select.append(pl.ds(spots[a], 1))
+                steps.append((wholes[member].at[(*select, slice(None), cut)], neighbour(axis, 1)))
+            done.append(axis)
+        if not shared[member]:
+            steps.append((wholes[member].at[:, :, :, :, cut], twin()))
+        chains.append(steps)
+    number, started = 0, []
+    late = delays(flows, 2)
+    length = max(late[i] + len(chains[i]) for i in range(len(flows)))
+    last = [None] * len(flows)
+    for copy in own:
+        copy.wait()
+    for tick in range(length + 1):
+        for i, steps in enumerate(chains):
+            at = tick - late[i]
+            if at < 0 or at > len(steps):
+                continue
+            if last[i] is not None:
+                last[i].wait_recv()
+            if at < len(steps):
+                block, peer = steps[at]
+                last[i] = pltpu.make_async_remote_copy(
+                    src_ref=block,
+                    dst_ref=block,
+                    send_sem=send_sems.at[number],
+                    recv_sem=recv_sems.at[number],
+                    device_id=peer,
+                    device_id_type=pl.DeviceIdType.MESH,
+                )
+                last[i].start()
+                started.append(last[i])
+                number += 1
+    for copy in started:
+        copy.wait_send()
+
+
+def gather_all(shards, shared):
     parts = axis_parts()
-    size, inner = parts[axis], parts["x"]
-    if axis == "y":
-        return lax.ppermute(x, "seq", [(i, (i + 1) % size) for i in range(size)])
-    total = parts["z"] * inner
-    if axis == "z":
-        return lax.ppermute(x, "dp", [(i, (i + inner) % total) for i in range(total)])
-    return lax.ppermute(x, "dp", [(i, i - i % inner + (i + 1) % inner) for i in range(total)])
-
-
-def add_up(terms):
-    total = terms[0].astype(jnp.float32)
-    for term in terms[1:]:
-        total = total + term.astype(jnp.float32)
-    return total
-
-
-def scatter_colour(partial_rows, order):
+    hops = sum(size - 1 for size in parts.values()) + 1
+    spans = [s.shape[1] if shared[m] else s.shape[1] // 2 for m, s in enumerate(shards)]
+    copies = hops * len(flows_of(spans, GATHER_ORDERS))
+    wholes = pl.pallas_call(
+        partial(gather_kernel, shared),
+        name="gather_all",
+        in_specs=[pl.BlockSpec(memory_space=pltpu.VMEM)] * len(shards),
+        out_specs=[pl.BlockSpec(memory_space=pl.ANY)] * len(shards),
+        out_shape=[
+            jax.ShapeDtypeStruct((parts["z"], parts["x"], parts["y"], *s.shape), s.dtype) for s in shards
+        ],
+        scratch_shapes=[
+            pltpu.SemaphoreType.DMA((copies,)),
+            pltpu.SemaphoreType.DMA((copies,)),
+            pltpu.SemaphoreType.DMA((len(shards),)),
+        ],
+        compiler_params=pltpu.CompilerParams(collective_id=0, has_side_effects=True),
+    )(*shards)
+    return [w.reshape(-1, w.shape[-1]) for w in wholes]
+
+
+def scatter_plan(widths):
     parts = axis_parts()
-    columns = partial_rows.shape[1]
-    left = ["z", "x", "y"]
-    sources = [partial_rows.reshape(*[parts[a] for a in left], -1, columns)]
-    for axis in order:
-        size, spot = parts[axis], place(axis)
-        at = left.index(axis)
-
-        def piece(index):
-            return [lax.dynamic_index_in_dim(s, index, at, keepdims=False) for s in sources]
-
-        got = []
-        for step in range(size - 1):
-            chunk = (spot + 2 * size - 1 - step) % size
-            got = [shift(add_up(piece(chunk) + got).astype(jnp.bfloat16), axis)]
-        sources = piece(spot) + got
-        left.remove(axis)
-    return add_up(sources)
-
-
-def scatter_rows(partial_rows):
-    columns = partial_rows.shape[1] // 128
-    shares = sum(share for _, share in COLOURS)
-    cuts, begin, pieces = [], 0, []
-    for order, share in COLOURS:
-        cuts.append((begin, order))
-        begin += share
-    for start, share_order in enumerate(cuts):
-        low = share_order[0] * columns // shares * 128
-        high = cuts[start + 1][0] * columns // shares * 128 if start + 1 < len(cuts) else columns * 128
-        pieces.append(scatter_colour(partial_rows[:, low:high], share_order[1]))
-    return jnp.concatenate(pieces, axis=1)
+    plan = []
+    for member, order, begin, width, piece in flows_of(widths, SCATTER_ORDERS):
+        left, levels = list(AXES), []
+        for axis in order:
+            left.remove(axis)
+            levels.append((axis, tuple(parts[a] for a in left), [a for a in left]))
+        plan.append((member, order, begin, width, piece, levels))
+    return plan
+
+
+def scatter_kernel(widths, *refs):
+    count = len(widths)
+    partials, sums = refs[:count], refs[count : 2 * count]
+    plan = scatter_plan(widths)
+    rest = refs[2 * count :]
+    send_sems, recv_sems, load_sems = rest[:3]
+    buffers = list(rest[3:])
+    parts, spots = axis_parts(), places()
+    rows = sums[0].shape[0]
+    greet(ring_peers())
+    chains, loads = [], 0
+    for member, order, begin, width, _, levels in plan:
+        cut = pl.ds(begin, width)
+        chain = []
+        source, before = partials[member], list(AXES)
+        for depth, (axis, extent, left) in enumerate(levels):
+            size = parts[axis]
+            inbox = [buffers.pop(0) for _ in range(size - 1)]
+            terms = []
+            for turn in range(size):
+                index = lax.rem(spots[axis] + 2 * size - 1 - turn, size)
+                select = tuple(index if a == axis else slice(None) for a in before)
+                if depth:
+                    terms.append(source.at[select])
+                else:
+                    terms.append(source.at[(*select, slice(None), cut)])
+            ready = []
+            if depth == 0:
+                for turn in range(1, size):
+                    local = buffers.pop(0)
+                    copy = pltpu.make_async_copy(terms[turn], local, load_sems.at[loads])
+                    copy.start()
+                    loads += 1
+                    ready.append(copy)
+                    terms[turn] = local
+            chain.append((axis, extent, inbox, terms, ready))
+            source, before = inbox[-1], left
+        chains.append(chain)
+
+    def accumulate(target, term, extent):
+        total = 1
+        for size in extent:
+            total *= size
+
+        def body(index, carry):
+            where, left = [], index
+            for size in reversed(extent):
+                where.insert(0, lax.rem(left, size))
+                left = lax.div(left, size)
+            where = tuple(where)
+            target[where] = (
+                target[where].astype(jnp.float32) + term[where].astype(jnp.float32)
+            ).astype(jnp.bfloat16)
+            return carry
+
+        lax.fori_loop(0, total, body, 0)
+
+    flat = []
+    for chain in chains:
+        steps = []
+        for depth, (axis, extent, inbox, terms, ready) in enumerate(chain):
+            size = parts[axis]
+            for turn in range(size - 1):
+                steps.append((depth, axis, turn))
+        flat.append(steps)
+    late = delays([p[:5] for p in plan], 2)
+    length = max(late[i] + len(flat[i]) for i in range(len(plan)))
+    last, started, number = [None] * len(plan), [], 0
+    for tick in range(length + 1):
+        for i, steps in enumerate(flat):
+            at = tick - late[i]
+            if at < 0 or at > len(steps):
+                continue
+            if last[i] is not None:
+                last[i].wait_recv()
+                depth, axis, turn = steps[at - 1]
+                _, extent, inbox, terms, ready = chains[i][depth]
+                if ready:
+                    ready[turn].wait()
+                if at < len(steps):
+                    accumulate(inbox[turn], terms[turn + 1], extent)
+                else:
+                    member, _, begin, width = plan[i][:4]
+                    sums[member][:, begin : begin + width] = inbox[turn][...].astype(
+                        jnp.float32
+                    ) + terms[turn + 1][...].astype(jnp.float32)
+            if at < len(steps):
+                depth, axis, turn = steps[at]
+                _, extent, inbox, terms, ready = chains[i][depth]
+                last[i] = pltpu.make_async_remote_copy(
+                    src_ref=inbox[turn - 1] if turn else terms[0],
+                    dst_ref=inbox[turn],
+                    send_sem=send_sems.at[number],
+                    recv_sem=recv_sems.at[number],
+                    device_id=neighbour(axis, 1),
+                    device_id_type=pl.DeviceIdType.MESH,
+                )
+                last[i].start()
+                started.append(last[i])
+                number += 1
+    for copy in started:
+        copy.wait_send()
+
+
+def scatter_all(partials):
+    parts = axis_parts()
+    widths = [p.shape[1] for p in partials]
+    rows = partials[0].shape[0] // (parts["z"] * parts["x"] * parts["y"])
+    buffers, copies, loads = [], 0, 0
+    for _, order, _, width, _, levels in scatter_plan(widths):
+        for depth, (axis, extent, _) in enumerate(levels):
+            slots = parts[axis] - 1
+            copies += slots
+            if depth == 0:
+                loads += slots
+                slots *= 2
+            buffers += [pltpu.VMEM((*extent, rows, width), jnp.bfloat16)] * slots
+    return pl.pallas_call(
+        partial(scatter_kernel, widths),
+        name="scatter_all",
+        in_specs=[pl.BlockSpec(memory_space=pl.ANY)] * len(partials),
+        out_specs=[pl.BlockSpec(memory_space=pltpu.VMEM)] * len(partials),
+        out_shape=[jax.ShapeDtypeStruct((rows, width), jnp.float32) for width in widths],
+        scratch_shapes=[
+            pltpu.SemaphoreType.DMA((copies,)),
+            pltpu.SemaphoreType.DMA((copies,)),
+            pltpu.SemaphoreType.DMA((loads,)),
+            *buffers,
+        ],
+        compiler_params=pltpu.CompilerParams(
+            collective_id=1, has_side_effects=True, vmem_limit_bytes=67043328
+        ),
+    )(*[p.reshape(parts["z"], parts["x"], parts["y"], rows, p.shape[1]) for p in partials])
 
 
 def adam_step(master, gradient, first, second, step_rate):
@@ -449,14 +694,15 @@
 ):
     masters = (weight_qkv, weight_out, weight_ffn, vectors)
     lowered = [master.astype(jnp.bfloat16) for master in masters]
-    gathered = (
-        lax.all_gather(lowered[0], ("dp", "seq"), axis=0, tiled=True),
-        lax.all_gather(lowered[1], ("dp", "seq"), axis=0, tiled=True),
-        lax.all_gather(lowered[2], ("dp", "seq"), axis=1, tiled=True),
-        lax.all_gather(lowered[3], ("dp", "seq"), axis=0, tiled=True),
-    )
-    full_qkv, full_out, full_ffn, full_vec = gathered
-    width = full_out.shape[0]
+    width = weight_out.shape[1]
+    entries = vectors.shape[0] // weight_out.shape[0]
+    vector_block = jnp.pad(lowered[3].reshape(-1, entries), ((0, 0), (0, 128 - entries)))
+    full_qkv, vector_rows, full_out, full_up, full_down = gather_all(
+        [lowered[0], vector_block, lowered[1], lowered[2][0], lowered[2][1]],
+        (False, True, False, False, False),
+    )
+    full_ffn = (full_up, full_down)
+    full_vec = vector_rows[:, :entries].reshape(-1)
     vector_values = full_vec.astype(jnp.float32)
     pieces = [vector_values[position * width : (position + 1) * width] for position in range(8)]
     (
@@ -569,16 +815,11 @@
             bias_hidden_grad,
         ]
     )
-    vector_rows = vector_grad.reshape(width, -1)
-    entries = vector_rows.shape[1]
-    small = jnp.pad(vector_rows, ((0, 0), (0, 128 - entries))).astype(jnp.bfloat16)
-    rest = scatter_rows(jnp.concatenate([qkv_weight_grad, out_weight_grad, small], axis=1))
-    summed = (
-        rest[:, : 3 * width],
-        rest[:, 3 * width : 4 * width],
-        jnp.stack([scatter_rows(up_grad), scatter_rows(down_grad)]),
-        rest[:, 4 * width : 4 * width + entries].reshape(-1),
-    )
+    small = jnp.pad(vector_grad.reshape(width, -1), ((0, 0), (0, 128 - entries))).astype(jnp.bfloat16)
+    down_sum, up_sum, qkv_sum, small_sum, out_sum = scatter_all(
+        [down_grad, up_grad, qkv_weight_grad, small, out_weight_grad]
+    )
+    summed = (qkv_sum, out_sum, jnp.stack([up_sum, down_sum]), small_sum[:, :entries].reshape(-1))
     firsts = (first_qkv[0], first_out[0], first_ffn[0], first_vec[0])
     seconds = (second_qkv[0], second_out[0], second_ffn[0], second_vec[0])
     outers = (outer_qkv, outer_out, outer_ffn, outer_vec)

time: 916 us -> 774 us (0.84)
  Pallas kernels: 131 us -> 474 us
  waiting for transfers between devices: 312 us -> 19.2 us
  blocking collectives: 65.4 us -> 0 us
  other arithmetic: 101 us -> 41.2 us
  starting transfers between devices: 38.4 us -> 6.2 us
  local copies, waits for them, and re-layouts: 56.9 us -> 38.3 us
  between operations: 15.6 us -> 1.83 us
    pallas_call x0 -> x2, Pallas kernels: none -> 346 us  [the longest x1 211 us: scatter_all(): pl.pallas_call(partial(scatter_kernel, widths), name='scatter_all', in_sp...]
    all_gather x3 -> x0, waiting for transfers between devices: 192 us -> none  [the longest x1 175 us: on_device(): lax.all_gather(lowered[2], ('dp', 'seq'), axis=1, tiled=True)]
    ppermute x45 -> x0, waiting for transfers between devices: 119 us -> none  [the longest x27 61.4 us: shift(): lax.ppermute(x, 'dp', [(i, (i + inner) % total) for i in range(total)])]
    all_gather x1 -> x0, blocking collectives: 65.4 us -> none  [on_device(): lax.all_gather(lowered[3], ('dp', 'seq'), axis=0, tiled=True)]
    convert_element_type x36 -> x0, other arithmetic: 39.1 us -> none  [scatter_colour(): got = [shift(add_up(piece(chunk) + got).astype(jnp.bfloat16), axis)]]
    ppermute x45 -> x0, starting transfers between devices: 32.7 us -> none  [the longest x27 15.1 us: shift(): lax.ppermute(x, 'dp', [(i, (i + inner) % total) for i in range(total)])]
    ppermute x7, waiting for transfers between devices: 0.39 us -> 19.2 us  [partner(): lax.ppermute(x, axis, [(i, i ^ 1 << stride) for i in range(lax.axis_size(...]
    slice x6 -> x0, local copies, waits for them, and re-layouts: 12.5 us -> none  [the longest x5 12.5 us: scatter_rows(): pieces.append(scatter_colour(partial_rows[:, low:high], share_order[1]))]
  transfers between devices with their start and end apart: 55 -> 7, of which waited for: 29 -> 1; matrix products, arithmetic and copies ran while one was open for 19% -> 5% of each run, Pallas kernels for 7% -> 18%
where the time goes in v2:
time: 774 us; the launch traced here: 766 us
  Pallas kernels  474 us (61%)
  matrix products  186 us (24%)
  other arithmetic  41.2 us (5%)
  local copies, waits for them, and re-layouts  38.3 us (5%)
  waiting for transfers between devices  19.2 us (2%)
    pallas_call x1, Pallas kernels, scatter_all(): pl.pallas_call(partial(scatter_kernel, widths), name='scatter_all', in_sp...  211 us
    pallas_call x1, Pallas kernels, gather_all(): pl.pallas_call(partial(gather_kernel, shared), name='gather_all', in_spec...  136 us
    pallas_call x1, Pallas kernels, attend_back(): pl.pallas_call(attend_back_kernel, name='attend_back', grid_spec=pltpu.Pr...  61.2 us
    pallas_call x1, Pallas kernels, attend(): pl.pallas_call(attend_kernel, name='attend', grid_spec=pltpu.PrefetchScal...  52.1 us
    dot_general x1, matrix products, on_device(): jnp.dot(hidden_low, full_ffn[0], preferred_element_type=jnp.float32)  46.4 us
    dot_general x4, matrix products, dot_tn(): lax.dot_general(a, b, (((0,), (0,)), ((), ())), preferred_element_type=jn...  45.2 us
    unnamed x146, local copies, waits for them, and re-layouts  29.6 us
    dot_general x1, matrix products, on_device(): jnp.dot(branch_two_low, full_ffn[1], preferred_element_type=jnp.float32)  25.5 us
  transfers between devices with their start and end apart: 7, of which 1 were waited for; matrix products, arithmetic and copies ran while one was open for 5% of the time, Pallas kernels for 18%

profile of v2, /device:TPU:0, one launch (start us, length us, event | category | flops | bytes accessed | tf_op | source)
XLA Modules:
  0.0 766.5 jit_solution(3146211795553792488)
XLA Ops:
  0.7 4.1 copy.81
  4.8 1.7 fusion.32
  6.5 3.1 collective-permute-start
  9.7 1.0 slice_bitcast_fusion
  10.8 0.8 convert_element_type.127.refs_0_
  11.6 0.7 convert_element_type.129.refs_2_
  12.4 3.9 copy.84
  16.3 0.9 reduce.4
  17.3 0.6 pad.16.refs_1_
  17.9 135.5 %gather_all.1 = (bf16[4,2,2,64,3072]{4,3,2,1,0:T(8,128)(2,1)}, bf16[4,2,2,64,128]{4,3,2,1,0:T(8,128)(2,1)}, bf16[4,2,2,64,1024]{4,3,2,1,0:T(8,128)(2,1)}, bf16[4...) custom-call(bf16[64,3072]{1,0:T(8,128)(2,1)} %convert_element_type.127.refs_0_, bf16[64,128]{1,0:T(8,128)(2,1)} %pad.16.refs_1_, ...), custom_call_target="tpu_custom_call" | custom-call | tf_op jit(solution)/shard_map/gather_all/pallas_call | solution.py:502
  153.4 1.0 slice_convert_fusion
  154.8 0.6 add_select_fusion
  155.4 0.6 fusion.69
  156.1 17.4 %add_convert_fusion.q_ref.k_ref.v_ref = bf16[1536,3072]{1,0:T(8,128)(2,1)} fusion(bf16[1024,3072]{1,0:T(8,128)(2,1)} %bitcast.136, f32[3072]{0:T(1024)S(1)} %pad_maximum_fusion.3, bf16[512,1024]{0,1:T(8,128)(2,1)} %collective-permute-done, bf16[1024,1024]{0,1:T(8,128)(2,1)} %bitcast.117, pred[]{:T(512)S(6)} %eq.16), kind=kOutput, calls=%fused_computation.1 | convolution fusion | flops 9687269376 | bytes 18886656 | tf_op jit(solution)/shard_map/dot_general | solution.py:732
  173.8 52.1 %attend.1 = (bf16[1024,1024]{1,0:T(8,128)(2,1)S(1)}, f32[1024,1024]{1,0:T(8,128)}, f32[1024,128]{1,0:T(8,128)S(1)}) custom-call(s32[1]{0:T(128)} %bitcast.1.side_ref, s32[1536,128]{1,0:T(8,128)S(1)} %broadcast_in_dim.35.ids_col_ref, s32[8,1536]{1,0:T(8,128)S(1)} %broadcast_in_dim.36.ids_row_ref, bf16[1536,3072]{1,0:T(8,128)(2,1)} %add_convert_fusion.q_ref.k_ref.v_ref, ...), custom_call_target="tpu_custom_call" | custom-call | flops 18253611008 | bytes 31457280 | tf_op jit(solution)/shard_map/attend/pallas_call | solution.py:136
  226.0 2.7 fusion.70
  228.7 0.5 multiply_reduce_fusion.3
  229.2 0.7 fusion.59.clone.4
  229.9 3.7 copy-done.60
  233.6 46.4 %multiply_convert_fusion = (bf16[1024,4096]{1,0:T(8,128)(2,1)}, f32[1024,4096]{1,0:T(8,128)}, f32[1024,4096]{1,0:T(8,128)}) fusion(f32[4096]{0:T(1024)S(1)} %slice.122, bf16[1024,4096]{1,0:T(8,128)(2,1)S(1)} %bitcast.131, bf16[1024,1024]{0,1:T(8,128)(2,1)S(1)} %fusion.59.clone.4), kind=kOutput, calls=%fused_computation.4 | convolution fusion | flops 8866758656 | bytes 52445184 | tf_op jit(solution)/shard_map/dot_general | solution.py:742
  280.1 12.2 %fusion.71 = (f32[1024]{0:T(1024)S(1)}, f32[1024,1024]{0,1:T(8,128)S(1)}) fusion(f32[1024]{0:T(1024)S(1)} %copy-done.54, bf16[1024,4096]{1,0:T(8,128)(2,1)} %get-tuple-element.193, bf16[1024,4096]{1,0:T(8,128)(2,1)S(1)} %bitcast.135, f32[1024]{0:T(1024)S(1)} %get-tuple-element.217, f32[1024]{0:T(1024)S(1)} %get-tuple-element.218, f32[1024]{0:T(1024)S(1)} %fusion.53, ...), kind=kOutput, calls=%fused_computation.168 | convolution fusion | flops 8597273600 | bytes 25190400 | tf_op jit(solution)/shard_map/dot_general | solution.py:746
  292.3 1.0 fusion.8
  293.4 4.2 fusion.9
  297.6 3.4 fusion.62
  301.0 25.5 %fusion.61 = (bf16[4096]{0:T(1024)(128)(2,1)}, bf16[1024,4096]{1,0:T(8,128)(2,1)}) fusion(f32[1024,4096]{1,0:T(8,128)} %get-tuple-element.194, f32[1024,4096]{1,0:T(8,128)} %get-tuple-element.230, f32[4096]{0:T(1024)S(1)} %slice.122, bf16[1024,1024]{0,1:T(8,128)(2,1)} %get-tuple-element.188, bf16[1024,4096]{1,0:T(8,128)(2,1)} %bitcast.132), kind=kOutput, calls=%fused_computation.159 | convolution fusion | flops 8657039360 | bytes 52453376 | tf_op jit(solution)/shard_map/dot_general | solution.py:758
  326.5 18.5 %multiply_reduce_fusion = (bf16[1024]{0:T(1024)(128)(2,1)}, f32[1024]{0:T(1024)S(1)}, bf16[1024]{0:T(1024)(128)(2,1)}, f32[1024,1024]{0,1:T(8,128)S(1)}) fusion(f32[1024,1024]{0,1:T(8,128)} %copy-done.6, f32[1024]{0:T(1024)S(1)} %fusion.53, f32[1024]{0:T(1024)S(1)} %broadcast_multiply_fusion.1, f32[1024]{0:T(1024)S(1)} %get-tuple-element.218, ...), kind=kOutput, calls=%fused_computation.29 | convolution fusion | flops 8607757312 | bytes 31498240 | tf_op jit(solution)/shard_map/dot_general | solution.py:763
  345.0 1.1 fusion.64
  346.6 1.7 copy-done.12
  348.2 1.0 copy-done.62
  349.2 2.4 convolution_convert_fusion.4.do_ref
  351.7 2.3 fusion.10.inner_ref
  354.0 0.8 fusion.66
  354.9 61.2 %attend_back.1 = (bf16[1024,1024]{1,0:T(8,128)(2,1)S(1)}, f32[1024,1024]{1,0:T(8,128)}, f32[1024,1024]{1,0:T(8,128)}) custom-call(s32[1]{0:T(128)} %bitcast.1.side_ref, s32[1536,128]{1,0:T(8,128)S(1)} %copy-done.1, s32[8,1536]{1,0:T(8,128)S(1)} %copy-done.3, bf16[1536,3072]{1,0:T(8,128)(2,1)} %add_convert_fusion.q_ref.k_ref.v_ref, ...), custom_call_target="tpu_custom_call" | custom-call | flops 45634027520 | bytes 41943040 | tf_op jit(solution)/shard_map/attend_back/pallas_call | solution.py:236
  416.2 15.5 %convolution_convert_fusion = bf16[1024,4096]{1,0:T(8,128)(2,1)} fusion(bf16[1024,4096]{1,0:T(8,128)(2,1)} %get-tuple-element.186, f32[1024,1024]{0,1:T(8,128)S(1)} %copy-done.7, f32[1024]{0:T(1024)S(1)} %get-tuple-element.217, f32[1024]{0:T(1024)S(1)} %get-tuple-element.218, f32[1024]{0:T(1024)S(1)} %fusion.53, f32[1024]{0:T(1024)S(1)} %broadcast_multiply_fusion.1), kind=kOutput, calls=%fused_computation.18 | convolution fusion | flops 8599371776 | bytes 20987904 | tf_op jit(solution)/shard_map/dot_general | solution.py:59
  431.7 14.3 %convolution_convert_fusion.1 = bf16[1024,4096]{1,0:T(8,128)(2,1)} fusion(bf16[1024,1024]{0,1:T(8,128)(2,1)S(1)} %copy-done.31, bf16[1024,4096]{1,0:T(8,128)(2,1)} %get-tuple-element.193), kind=kOutput, calls=%fused_computation.19 | convolution fusion | flops 8594128896 | bytes 18874368 | tf_op jit(solution)/shard_map/dot_general | solution.py:59
  446.5 1.9 collective-permute-start.2
  448.4 3.7 convolution_convert_fusion.3
  452.1 1.6 constant_dynamic-update-slice_fusion.2
  453.7 3.9 copy.90
  457.6 19.2 %collective-permute-done.2 = f32[512,32]{1,0:T(8,128)S(1)} collective-permute-done((f32[512,32]{1,0:T(8,128)S(1)}, f32[512,32]{1,0:T(8,128)S(1)}, u32[]{:S(2)}, u32[]{:S(2)}) %collective-permute-start.2) | collective-permute-done | bytes 65568 | tf_op jit(solution)/shard_map/ppermute | solution.py:28
  477.0 14.5 %attend_far.1 = (bf16[1024,1024]{1,0:T(8,128)(2,1)S(1)}, bf16[1024,1024]{1,0:T(8,128)(2,1)}) custom-call(s32[1]{0:T(128)} %bitcast.1.side_ref, s32[1536,128]{1,0:T(8,128)S(1)} %copy-done.1, s32[8,1536]{1,0:T(8,128)S(1)} %copy-done.3, bf16[1536,3072]{1,0:T(8,128)(2,1)} %add_convert_fusion.q_ref.k_ref.v_ref, ...), custom_call_target="tpu_custom_call" | custom-call | flops 8589934592 | bytes 20971520 | tf_op jit(solution)/shard_map/attend_far/pallas_call | solution.py:321
  491.5 1.5 constant_dynamic-update-slice_fusion.1
  493.0 0.8 copy-done.29
  493.8 1.6 constant_dynamic-update-slice_fusion
  495.4 3.9 reduce.1
  499.3 11.6 %convolution_convert_fusion.2 = bf16[3072,1024]{0,1:T(8,128)(2,1)} fusion(bf16[1024,3072]{1,0:T(8,128)(2,1)} %constant_dynamic-update-slice_fusion, bf16[1,1024,1024]{2,1,0:T(8,128)(2,1)S(1)} %copy-done.28), kind=kOutput, calls=%fused_computation.22 | convolution fusion | flops 6445596672 | bytes 14680064 | tf_op jit(solution)/shard_map/dot_general | solution.py:59
  511.1 0.6 reshape.356
  511.7 0.8 pad.19
  512.4 210.9 %scatter_all.1 = (f32[64,4096]{1,0:T(8,128)}, f32[64,4096]{1,0:T(8,128)}, f32[64,3072]{1,0:T(8,128)}, f32[64,128]{1,0:T(8,128)}, f32[64,1024]{1,0:T(8,128)}) custom-call(bf16[4,2,2,64,4096]{4,3,2,1,0:T(8,128)(2,1)} %bitcast.116, bf16[4,2,2,64,4096]{4,3,2,1,0:T(8,128)(2,1)} %bitcast.115, bf16[4,2,2,64,3072]{4,3,2,1,0:T(8,128)(2,1)} %bitcast.118, ...), custom_call_target="tpu_custom_call" | custom-call | tf_op jit(solution)/shard_map/scatter_all/pallas_call | solution.py:649
  723.3 0.9 broadcast_in_dim_reshape.3
  724.2 0.9 reshape.359
  725.2 13.0 %add_bitcast_fusion = f32[1,1024,1024]{1,2,0:T(8,128)} fusion(f32[1024,1024]{0,1:T(8,128)} %copy-done.12, f32[1024]{0:T(1024)} %copy-done.46, bf16[1024,3072]{1,0:T(8,128)(2,1)} %constant_dynamic-update-slice_fusion, bf16[1024,3072]{1,0:T(8,128)(2,1)} %bitcast.137), kind=kOutput, calls=%fused_computation.30 | convolution fusion | flops 6444548096 | bytes 20975616 | tf_op jit(solution)/shard_map/dot_general | solution.py:802
  738.2 0.6 multiply_reduce_fusion.5
  739.0 3.3 fusion.27
  742.8 1.0 fusion.36
  743.8 1.8 fusion.34
  746.0 2.6 fusion.20
  748.7 5.3 copy.91
  754.0 0.6 multiply_subtract_fusion.3
  754.7 2.0 multiply_subtract_fusion.2
  756.7 2.9 multiply_subtract_fusion.1
  759.6 5.0 multiply_subtract_fusion
  764.6 0.9 copy.107
  765.5 0.7 copy.108
  (173 shorter events, 3.6 us)
Async XLA Ops:
  0.7 8.9 %copy-start.10 = (f32[2,64,4096]{2,1,0:T(8,128)S(1)}, f32[2,64,4096]{2,1,0:T(8,128)}, u32[]{:S(2)}) copy-start(f32[2,64,4096]{2,1,0:T(8,128)} %param.24) | copy-start | bytes 6291460
  4.8 6.0 copy-start.17
  4.8 6.8 copy-start.24
  6.5 5.7 copy-start.41
  6.5 149.5 %collective-permute-start = (bf16[512,1024]{0,1:T(8,128)(2,1)S(1)}, bf16[512,1024]{0,1:T(8,128)(2,1)}, u32[]{:S(2)}, u32[]{:S(2)}) collective-permute-start(bf16[512,1024]{0,1:T(8,128)(2,1)S(1)} %fusion.32), channel_id=1, source_target_pairs={{0,1},{1,0},{2,3},{3,2},{4,5},{5,4},{6,7},{7,6},{8,9},{9,8},{10,11... | collective-permute-start | bytes 3145736 | tf_op jit(solution)/shard_map/ppermute | solution.py:28
  9.7 6.6 copy-start.13
  12.4 142.4 %copy-start.53 = (s32[1,2048]{1,0:T(1,128)S(1)}, s32[1,2048]{1,0:T(1,128)}, u32[]{:S(2)}) copy-start(s32[1,2048]{1,0:T(1,128)} %param.21) | copy-start | bytes 24580
  173.7 52.2 %copy-start = (s32[1536,128]{1,0:T(8,128)}, s32[1536,128]{1,0:T(8,128)S(1)}, u32[]{:S(2)}) copy-start(s32[1536,128]{1,0:T(8,128)S(1)} %broadcast_in_dim.35.ids_col_ref) | copy-start | bytes 2359300
  173.8 52.2 %copy-start.2 = (s32[8,1536]{1,0:T(8,128)}, s32[8,1536]{1,0:T(8,128)S(1)}, u32[]{:S(2)}) copy-start(s32[8,1536]{1,0:T(8,128)S(1)} %broadcast_in_dim.36.ids_row_ref) | copy-start | bytes 147460
  173.8 52.2 %copy-start.16 = (bf16[1,1024,1024]{1,2,0:T(8,128)(2,1)S(1)}, bf16[1,1024,1024]{1,2,0:T(8,128)(2,1)}, u32[]{:S(2)}) copy-start(bf16[1,1024,1024]{1,2,0:T(8,128)(2,1)} %copy.81) | copy-start | bytes 6291460
  173.8 52.2 %copy-start.61 = (bf16[4,2,2,64,1024]{4,3,2,1,0:T(8,128)(2,1)S(1)}, bf16[4,2,2,64,1024]{4,3,2,1,0:T(8,128)(2,1)}, u32[]{:S(2)}) copy-start(bf16[4,2,2,64,1024]{4,3,2,1,0:T(8,128)(2,1)} %get-tuple-element.47) | copy-start | bytes 6291460
  228.7 51.3 %copy-start.6 = (f32[1024,1024]{0,1:T(8,128)}, f32[1024,1024]{0,1:T(8,128)S(1)}, u32[]{:S(2)}) copy-start(f32[1024,1024]{0,1:T(8,128)S(1)} %get-tuple-element.229) | copy-start | bytes 12582916
  228.7 4.9 copy-start.60
  229.2 50.8 %copy-start.43 = (f32[1024]{0:T(1024)}, f32[1024]{0:T(1024)S(1)}, u32[]{:S(2)}) copy-start(f32[1024]{0:T(1024)S(1)} %multiply_reduce_fusion.3) | copy-start | bytes 12292
  229.2 50.8 %slice-start = ((s8[8388608]{0:T(1024)(128)(4,1)}), s8[4194304]{0:T(1024)(128)(4,1)S(1)}, s32[]{:S(2)}) async-start(s8[8388608]{0:T(1024)(128)(4,1)} %bitcast.133), calls=%async_computation | async-start | bytes 8388608
  233.6 46.4 %copy-start.54 = (f32[1024]{0:T(1024)S(1)}, f32[1024]{0:T(1024)}, u32[]{:S(2)}) copy-start(f32[1024]{0:T(1024)} %get-tuple-element.216) | copy-start | bytes 12292
  233.6 46.4 %slice-start.1 = ((s8[8388608]{0:T(1024)(128)(4,1)}), s8[4194304]{0:T(1024)(128)(4,1)S(1)}, s32[]{:S(2)}) async-start(s8[8388608]{0:T(1024)(128)(4,1)} %bitcast.133), calls=%async_computation.1 | async-start | bytes 8388608
  280.1 12.3 %copy-start.9 = (bf16[1,1024,1024]{1,2,0:T(8,128)(2,1)S(1)}, bf16[1,1024,1024]{1,2,0:T(8,128)(2,1)}, u32[]{:S(2)}) copy-start(bf16[1,1024,1024]{1,2,0:T(8,128)(2,1)} %copy.84) | copy-start | bytes 6291460
  280.1 12.2 %copy-start.40 = (f32[1024]{0:T(1024)S(1)}, f32[1024]{0:T(1024)}, u32[]{:S(2)}) copy-start(f32[1024]{0:T(1024)} %get-tuple-element.214) | copy-start | bytes 12292
  292.3 5.3 copy-start.8
  326.5 18.5 %copy-start.44 = (f32[1024]{0:T(1024)S(1)}, f32[1024]{0:T(1024)}, u32[]{:S(2)}) copy-start(f32[1024]{0:T(1024)} %copy-done.43) | copy-start | bytes 12292
  326.5 18.5 %copy-start.7 = (f32[1024,1024]{0,1:T(8,128)S(1)}, f32[1024,1024]{0,1:T(8,128)}, u32[]{:S(2)}) copy-start(f32[1024,1024]{0,1:T(8,128)} %copy-done.6) | copy-start | bytes 12582916
  346.1 5.5 copy-start.46
  348.2 3.4 copy-start.26
  351.7 3.2 copy-start.1
  416.2 15.6 %copy-start.31 = (bf16[1024,1024]{0,1:T(8,128)(2,1)S(1)}, bf16[1024,1024]{0,1:T(8,128)(2,1)}, u32[]{:S(2)}) copy-start(bf16[1024,1024]{0,1:T(8,128)(2,1)} %get-tuple-element.188) | copy-start | bytes 6291460
  431.7 14.6 %copy-start.34 = (f32[512,128]{1,0:T(8,128)S(1)}, f32[512,128]{1,0:T(8,128)}, u32[]{:S(2)}) copy-start(f32[512,128]{1,0:T(8,128)} %get-tuple-element.208) | copy-start | bytes 786436
  431.7 14.6 %copy-start.35 = (f32[512,128]{1,0:T(8,128)S(1)}, f32[512,128]{1,0:T(8,128)}, u32[]{:S(2)}) copy-start(f32[512,128]{1,0:T(8,128)} %get-tuple-element.209) | copy-start | bytes 786436
  431.7 16.6 %copy-start.5 = (bf16[1024,1024]{1,0:T(8,128)(2,1)S(1)}, bf16[1024,1024]{1,0:T(8,128)(2,1)}, u32[]{:S(2)}) copy-start(bf16[1024,1024]{1,0:T(8,128)(2,1)} %copy-done.4) | copy-start | bytes 6291460
  431.7 16.6 %copy-start.27 = (bf16[1024,1024]{0,1:T(8,128)(2,1)S(1)}, bf16[1024,1024]{0,1:T(8,128)(2,1)}, u32[]{:S(2)}) copy-start(bf16[1024,1024]{0,1:T(8,128)(2,1)} %copy-done.26) | copy-start | bytes 6291460
  446.1 30.9 %collective-permute-start.1 = (bf16[512,1024]{1,0:T(8,128)(2,1)S(1)}, bf16[512,1024]{1,0:T(8,128)(2,1)S(1)}, u32[]{:S(2)}, u32[]{:S(2)}) collective-permute-start(bf16[512,1024]{1,0:T(8,128)(2,1)S(1)} %slice_select_fusion), channel_id=1, source_target_pairs={{0,1},{1,0},{2,3},{3,2},{4,5},{5,4},{6,7},{7,6},{8,9},{9,8},{10,11... | collective-permute-start | bytes 3145736 | tf_op jit(solution)/shard_map/ppermute | solution.py:28
  446.5 30.3 %collective-permute-start.2 = (f32[512,32]{1,0:T(8,128)S(1)}, f32[512,32]{1,0:T(8,128)S(1)}, u32[]{:S(2)}, u32[]{:S(2)}) collective-permute-start(f32[512,32]{1,0:T(8,128)S(1)} %pad_maximum_fusion.2), channel_id=1, source_target_pairs={{0,1},{1,0},{2,3},{3,2},{4,5},{5,4},{6,7},{7,6},{8,9},{9,8},{10,11... | collective-permute-start | bytes 196616 | tf_op jit(solution)/shard_map/ppermute | solution.py:28
  495.4 3.9 copy-start.28
  499.2 11.7 %copy-start.49 = (bf16[1024]{0:T(1024)(128)(2,1)S(1)}, bf16[1024]{0:T(1024)(128)(2,1)}, u32[]{:S(2)}) copy-start(bf16[1024]{0:T(1024)(128)(2,1)} %get-tuple-element.187) | copy-start | bytes 6148
  499.2 11.7 %copy-start.59 = (bf16[1024]{0:T(1024)(128)(2,1)S(1)}, bf16[1024]{0:T(1024)(128)(2,1)}, u32[]{:S(2)}) copy-start(bf16[1024]{0:T(1024)(128)(2,1)} %get-tuple-element.166) | copy-start | bytes 6148
  499.2 11.7 %copy-start.58 = (bf16[1024]{0:T(1024)(128)(2,1)S(1)}, bf16[1024]{0:T(1024)(128)(2,1)}, u32[]{:S(2)}) copy-start(bf16[1024]{0:T(1024)(128)(2,1)} %get-tuple-element.172) | copy-start | bytes 6148
  499.3 11.8 %copy-start.52 = (bf16[1024]{0:T(1024)(128)(2,1)S(1)}, bf16[1024]{0:T(1024)(128)(2,1)}, u32[]{:S(2)}) copy-start(bf16[1024]{0:T(1024)(128)(2,1)} %get-tuple-element.168) | copy-start | bytes 6148
  499.3 11.8 %copy-start.51 = (bf16[1024]{0:T(1024)(128)(2,1)S(1)}, bf16[1024]{0:T(1024)(128)(2,1)}, u32[]{:S(2)}) copy-start(bf16[1024]{0:T(1024)(128)(2,1)} %reduce.4) | copy-start | bytes 6148
  499.3 11.8 %copy-start.50 = (bf16[4096]{0:T(1024)(128)(2,1)S(1)}, bf16[4096]{0:T(1024)(128)(2,1)}, u32[]{:S(2)}) copy-start(bf16[4096]{0:T(1024)(128)(2,1)} %get-tuple-element.185) | copy-start | bytes 24580
  724.2 13.9 %copy-start.48 = (f32[1,768]{1,0:T(1,128)}, f32[1,768]{1,0:T(1,128)S(1)}, u32[]{:S(2)}) copy-start(f32[1,768]{1,0:T(1,128)S(1)} %broadcast_in_dim_reshape.3) | copy-start | bytes 9220
  725.1 13.1 %copy-start.56 = (f32[1,768]{1,0:T(1,128)S(1)}, f32[1,768]{1,0:T(1,128)}, u32[]{:S(2)}) copy-start(f32[1,768]{1,0:T(1,128)} %param.29) | copy-start | bytes 9220
  725.1 13.1 %copy-start.57 = (f32[1,768]{1,0:T(1,128)S(1)}, f32[1,768]{1,0:T(1,128)}, u32[]{:S(2)}) copy-start(f32[1,768]{1,0:T(1,128)} %param.33) | copy-start | bytes 9220
  725.1 13.7 %copy-start.42 = (f32[768]{0:T(1024)S(1)}, f32[768]{0:T(1024)}, u32[]{:S(2)}) copy-start(f32[768]{0:T(1024)} %param.25) | copy-start | bytes 9220
  725.1 13.8 %copy-start.11 = (f32[2,64,4096]{2,1,0:T(8,128)S(1)}, f32[2,64,4096]{2,1,0:T(8,128)}, u32[]{:S(2)}) copy-start(f32[2,64,4096]{2,1,0:T(8,128)} %param.24) | copy-start | bytes 6291460
  725.1 13.8 %copy-start.14 = (f32[1,2,64,4096]{3,2,1,0:T(8,128)S(1)}, f32[1,2,64,4096]{3,2,1,0:T(8,128)}, u32[]{:S(2)}) copy-start(f32[1,2,64,4096]{3,2,1,0:T(8,128)} %param.32) | copy-start | bytes 6291460
  725.1 13.8 %copy-start.15 = (f32[1,2,64,4096]{3,2,1,0:T(8,128)S(1)}, f32[1,2,64,4096]{3,2,1,0:T(8,128)}, u32[]{:S(2)}) copy-start(f32[1,2,64,4096]{3,2,1,0:T(8,128)} %param.28) | copy-start | bytes 6291460
  725.1 13.8 %copy-start.20 = (f32[64,4096]{1,0:T(8,128)S(1)}, f32[64,4096]{1,0:T(8,128)}, u32[]{:S(2)}) copy-start(f32[64,4096]{1,0:T(8,128)} %get-tuple-element.60) | copy-start | bytes 3145732
  725.2 13.8 %copy-start.21 = (f32[64,4096]{1,0:T(8,128)S(1)}, f32[64,4096]{1,0:T(8,128)}, u32[]{:S(2)}) copy-start(f32[64,4096]{1,0:T(8,128)} %get-tuple-element.59) | copy-start | bytes 3145732
  738.8 15.3 %collective-permute-start.6 = (bf16[768]{0:T(1024)(128)(2,1)S(1)}, bf16[768]{0:T(1024)(128)(2,1)S(1)}, u32[]{:S(2)}, u32[]{:S(2)}) collective-permute-start(bf16[768]{0:T(1024)(128)(2,1)S(1)} %fusion.51), channel_id=1, source_target_pairs={{0,16},{16,0},{1,17},{17,1},{2,18},{18,2},{3,19},{19,3},{4,20},{20... | collective-permute-start | bytes 4616 | tf_op jit(solution)/shard_map/ppermute | solution.py:28
  738.9 3.9 copy-start.25
  738.9 3.9 copy-start.32
  738.9 3.9 copy-start.38
  739.0 3.8 copy-start.39
  739.0 4.8 copy-start.18
  739.0 4.8 copy-start.22
  739.0 4.8 copy-start.36
  739.0 4.8 copy-start.37
  742.3 17.3 %collective-permute-start.5 = (bf16[2,64,4096]{2,1,0:T(8,128)(2,1)}, bf16[2,64,4096]{2,1,0:T(8,128)(2,1)}, u32[]{:S(2)}, u32[]{:S(2)}) collective-permute-start(bf16[2,64,4096]{2,1,0:T(8,128)(2,1)} %get-tuple-element.196), channel_id=1, source_target_pairs={{0,16},{16,0},{1,17},{17,1},{2,18},{18,2},{3,19},{19,3},{4,20},{20... | collective-permute-start | bytes 3145736 | tf_op jit(solution)/shard_map/ppermute | solution.py:28
  743.8 10.9 %collective-permute-start.4 = (bf16[64,1024]{1,0:T(8,128)(2,1)}, bf16[64,1024]{1,0:T(8,128)(2,1)}, u32[]{:S(2)}, u32[]{:S(2)}) collective-permute-start(bf16[64,1024]{1,0:T(8,128)(2,1)} %get-tuple-element.205), channel_id=1, source_target_pairs={{0,16},{16,0},{1,17},{17,1},{2,18},{18,2},{3,19},{19,3},{4,20},{20... | collective-permute-start | bytes 393224 | tf_op jit(solution)/shard_map/ppermute | solution.py:28
  745.6 11.1 %collective-permute-start.3 = (bf16[64,3072]{1,0:T(8,128)(2,1)S(1)}, bf16[64,3072]{1,0:T(8,128)(2,1)}, u32[]{:S(2)}, u32[]{:S(2)}) collective-permute-start(bf16[64,3072]{1,0:T(8,128)(2,1)S(1)} %get-tuple-element.200), channel_id=1, source_target_pairs={{0,16},{16,0},{1,17},{17,1},{2,18},{18,2},{3,19},{19,3},{4,20},{20... | collective-permute-start | bytes 1179656 | tf_op jit(solution)/shard_map/ppermute | solution.py:28
  748.7 5.4 copy-start.55
  754.0 5.6 copy-start.30
  759.6 5.0 copy-start.23
  759.6 5.9 copy-start.33
  (8 other events, 19.5 us)

commit v3 on v2

--- a/solution.py
+++ b/solution.py
@@ -85,9 +85,19 @@
     return jnp.sum(jnp.where(lane == index, x, 0.0), axis=1, keepdims=True)
 
 
-def attend_kernel(side_ref, ids_col_ref, ids_row_ref, q_ref, k_ref, v_ref, o_ref, wide_ref, lse_ref, bias_ref):
+def attend_kernel(
+    shared, ids_col_ref, ids_row_ref, q_ref, k_ref, v_ref, *refs
+):
+    count = len(shared)
+    o_ref, wide_ref, lse_ref = refs[count : count + 3]
+    wholes = refs[count + 3 : 2 * count + 3]
+    bias_ref = refs[2 * count + 3]
     j, pair = pl.program_id(0), pl.program_id(1)
-    side = side_ref[0]
+    side = lax.axis_index("seq")
+    now = j * pl.num_programs(1) + pair
+    slots = 32
+    work = gather_steps(shared, refs[:count], wholes, *refs[2 * count + 4 :])
+    spread(work, now, slots)
 
     def run(length):
         span = length * TILE
@@ -128,50 +138,71 @@
         def _():
             run(length)
 
-
-def attend(side, ids_col, ids_row, qkv):
+    @pl.when(now == slots - 1)
+    def _():
+        for step in work[-2:]:
+            step()
+
+
+def attend(ids_col, ids_row, qkv, shards):
     rows, width = qkv.shape[0], qkv.shape[1] // 3
     pairs = width // 128
     own = rows - W
-    return pl.pallas_call(
-        attend_kernel,
+    shared = (False,) * len(shards)
+    got = pl.pallas_call(
+        partial(attend_kernel, shared),
         name="attend",
         grid_spec=pltpu.PrefetchScalarGridSpec(
-            num_scalar_prefetch=1,
+            num_scalar_prefetch=0,
             grid=(own // TILE, pairs),
             in_specs=[
-                pl.BlockSpec((TILE, 128), lambda j, p, s: (query_tile(s[0], j), 0)),
-                pl.BlockSpec((8, rows), lambda j, p, s: (0, 0)),
-                pl.BlockSpec((TILE, 128), lambda j, p, s: (query_tile(s[0], j), p)),
-                pl.BlockSpec((rows, 128), lambda j, p, s: (0, pairs + p)),
-                pl.BlockSpec((rows, 128), lambda j, p, s: (0, 2 * pairs + p)),
+                pl.BlockSpec((TILE, 128), lambda j, p: (query_tile(lax.axis_index("seq"), j), 0)),
+                pl.BlockSpec((8, rows), lambda j, p: (0, 0)),
+                pl.BlockSpec((TILE, 128), lambda j, p: (query_tile(lax.axis_index("seq"), j), p)),
+                pl.BlockSpec((rows, 128), lambda j, p: (0, pairs + p)),
+                pl.BlockSpec((rows, 128), lambda j, p: (0, 2 * pairs + p)),
+                *[pl.BlockSpec(s.shape, lambda j, p: (0, 0)) for s in shards],
             ],
             out_specs=[
-                pl.BlockSpec((TILE, 128), lambda j, p, s: (own_tile(s[0], j), p)),
-                pl.BlockSpec((TILE, 128), lambda j, p, s: (own_tile(s[0], j), p)),
-                pl.BlockSpec((TILE, 128), lambda j, p, s: (own_tile(s[0], j), 0)),
+                pl.BlockSpec((TILE, 128), lambda j, p: (own_tile(lax.axis_index("seq"), j), p)),
+                pl.BlockSpec((TILE, 128), lambda j, p: (own_tile(lax.axis_index("seq"), j), p)),
+                pl.BlockSpec((TILE, 128), lambda j, p: (own_tile(lax.axis_index("seq"), j), 0)),
+                *[pl.BlockSpec(memory_space=pl.ANY) for s in shards],
             ],
-            scratch_shapes=[pltpu.VMEM((TILE, 5 * TILE), jnp.float32)],
+            scratch_shapes=[
+                pltpu.VMEM((TILE, 5 * TILE), jnp.float32),
+                *gather_scratch(shards, shared),
+            ],
         ),
         out_shape=[
             jax.ShapeDtypeStruct((own, width), jnp.bfloat16),
             jax.ShapeDtypeStruct((own, width), jnp.float32),
             jax.ShapeDtypeStruct((own, 128), jnp.float32),
+            *gather_shapes(shards),
         ],
-        compiler_params=pltpu.CompilerParams(vmem_limit_bytes=48 << 20),
+        compiler_params=pltpu.CompilerParams(
+            vmem_limit_bytes=48 << 20, collective_id=2, has_side_effects=True
+        ),
         cost_estimate=pl.CostEstimate(
             flops=4 * 17 * TILE * TILE * width * 4, bytes_accessed=30 << 20, transcendentals=0
         ),
-    )(side, ids_col, ids_row, qkv, qkv, qkv)
+    )(ids_col, ids_row, qkv, qkv, qkv, *shards)
+    return [*got[:3], *[w.reshape(-1, w.shape[-1]) for w in got[3:]]]
 
 
 def attend_back_kernel(
-    side_ref, ids_col_ref, ids_row_ref, q_ref, k_ref, v_ref, do_ref, lse_ref, inner_ref,
-    dq_ref, dk_ref, dv_ref, bias_ref, dkt_ref, dvt_ref,
+    widths, ids_col_ref, ids_row_ref, q_ref, k_ref, v_ref, do_ref, lse_ref, inner_ref, *refs
 ):
+    count = len(widths)
+    dq_ref, dk_ref, dv_ref = refs[count : count + 3]
+    sums = refs[count + 3 : 2 * count + 3]
+    bias_ref, dkt_ref, dvt_ref = refs[2 * count + 3 : 2 * count + 6]
     pair, j = pl.program_id(0), pl.program_id(1)
-    side = side_ref[0]
+    side = lax.axis_index("seq")
     own = dk_ref.shape[0]
+    now, slots = pair * pl.num_programs(1) + j, 32
+    work = scatter_steps(widths, refs[:count], sums, *refs[2 * count + 6 :])
+    spread(work, now, slots)
 
     @pl.when(j == 0)
     def _():
@@ -228,48 +259,62 @@
         dk_ref[...] = jnp.transpose(dkt_ref[:, pl.ds(at, own)])
         dv_ref[...] = jnp.transpose(dvt_ref[:, pl.ds(at, own)])
 
-
-def attend_back(side, ids_col, ids_row, qkv, outgrad, lse, inner):
+    @pl.when(now == slots - 1)
+    def _():
+        for step in work[-2:]:
+            step()
+
+
+def attend_back(ids_col, ids_row, qkv, outgrad, lse, inner, partials):
     rows, width = qkv.shape[0], qkv.shape[1] // 3
     pairs = width // 128
     own = rows - W
+    operands = scatter_operands(partials)
+    widths = [p.shape[1] for p in partials]
+    shard_rows = operands[0].shape[3]
     return pl.pallas_call(
-        attend_back_kernel,
+        partial(attend_back_kernel, widths),
         name="attend_back",
         grid_spec=pltpu.PrefetchScalarGridSpec(
-            num_scalar_prefetch=1,
+            num_scalar_prefetch=0,
             grid=(pairs, own // TILE),
             in_specs=[
-                pl.BlockSpec((TILE, 128), lambda p, j, s: (query_tile(s[0], j), 0)),
-                pl.BlockSpec((8, rows), lambda p, j, s: (0, 0)),
-                pl.BlockSpec((TILE, 128), lambda p, j, s: (query_tile(s[0], j), p)),
-                pl.BlockSpec((rows, 128), lambda p, j, s: (0, pairs + p)),
-                pl.BlockSpec((rows, 128), lambda p, j, s: (0, 2 * pairs + p)),
-                pl.BlockSpec((TILE, 128), lambda p, j, s: (own_tile(s[0], j), p)),
-                pl.BlockSpec((TILE, 128), lambda p, j, s: (own_tile(s[0], j), 0)),
-                pl.BlockSpec((TILE, 128), lambda p, j, s: (own_tile(s[0], j), 0)),
+                pl.BlockSpec((TILE, 128), lambda p, j: (query_tile(lax.axis_index("seq"), j), 0)),
+                pl.BlockSpec((8, rows), lambda p, j: (0, 0)),
+                pl.BlockSpec((TILE, 128), lambda p, j: (query_tile(lax.axis_index("seq"), j), p)),
+                pl.BlockSpec((rows, 128), lambda p, j: (0, pairs + p)),
+                pl.BlockSpec((rows, 128), lambda p, j: (0, 2 * pairs + p)),
+                pl.BlockSpec((TILE, 128), lambda p, j: (own_tile(lax.axis_index("seq"), j), p)),
+                pl.BlockSpec((TILE, 128), lambda p, j: (own_tile(lax.axis_index("seq"), j), 0)),
+                pl.BlockSpec((TILE, 128), lambda p, j: (own_tile(lax.axis_index("seq"), j), 0)),
+                *[pl.BlockSpec(memory_space=pl.ANY) for _ in widths],
             ],
             out_specs=[
-                pl.BlockSpec((TILE, 128), lambda p, j, s: (own_tile(s[0], j), p)),
-                pl.BlockSpec((own, 128), lambda p, j, s: (0, p)),
-                pl.BlockSpec((own, 128), lambda p, j, s: (0, p)),
+                pl.BlockSpec((TILE, 128), lambda p, j: (own_tile(lax.axis_index("seq"), j), p)),
+                pl.BlockSpec((own, 128), lambda p, j: (0, p)),
+                pl.BlockSpec((own, 128), lambda p, j: (0, p)),
+                *[pl.BlockSpec((shard_rows, w), lambda p, j: (0, 0)) for w in widths],
             ],
             scratch_shapes=[
                 pltpu.VMEM((own // TILE, TILE, 5 * TILE), jnp.float32),
                 pltpu.VMEM((128, rows), jnp.float32),
                 pltpu.VMEM((128, rows), jnp.float32),
+                *scatter_scratch(widths, shard_rows),
             ],
         ),
         out_shape=[
             jax.ShapeDtypeStruct((own, width), jnp.bfloat16),
             jax.ShapeDtypeStruct((own, width), jnp.float32),
             jax.ShapeDtypeStruct((own, width), jnp.float32),
+            *[jax.ShapeDtypeStruct((shard_rows, w), jnp.float32) for w in widths],
         ],
-        compiler_params=pltpu.CompilerParams(vmem_limit_bytes=48 << 20),
+        compiler_params=pltpu.CompilerParams(
+            vmem_limit_bytes=67043328, collective_id=3, has_side_effects=True
+        ),
         cost_estimate=pl.CostEstimate(
             flops=10 * 17 * TILE * TILE * width * 4, bytes_accessed=40 << 20, transcendentals=0
         ),
-    )(side, ids_col, ids_row, qkv, qkv, qkv, outgrad, lse, inner)
+    )(ids_col, ids_row, qkv, qkv, qkv, outgrad, lse, inner, *operands)
 
 
 def attend_far_kernel(
@@ -353,7 +398,7 @@
 AXES = ("z", "x", "y")
 GATHER_ORDERS = ((("z", "x", "y"), 3), (("z", "y", "x"), 3), (("x", "y", "z"), 2))
 SCATTER_ORDERS = ((("y", "x", "z"), 3), (("x", "y", "z"), 3), (("z", "y", "x"), 2))
-PIECE = 2048
+PIECE = 512
 
 
 def axis_parts():
@@ -393,7 +438,7 @@
 def flows_of(widths, orders):
     flows = []
     for member, width in enumerate(widths):
-        pieces = max(1, width // PIECE)
+        pieces = max(1, min(4, width // PIECE))
         for piece in range(pieces):
             tiles, begin = width // pieces // 128, piece * (width // pieces)
             if tiles < len(orders):
@@ -418,13 +463,10 @@
     return found
 
 
-def gather_kernel(shared, *refs):
+def gather_steps(shared, shards, wholes, send_sems, recv_sems, own_sems):
     count = len(shared)
-    shards, wholes = refs[:count], refs[count : 2 * count]
-    send_sems, recv_sems, own_sems = refs[2 * count :]
     parts, spots = axis_parts(), places()
     core = lax.axis_index("grp")
-    greet(ring_peers() + [twin()])
     spans = [s.shape[1] if shared[m] else s.shape[1] // 2 for m, s in enumerate(shards)]
 
     def columns(member, begin, width):
@@ -432,20 +474,16 @@
             return pl.ds(begin, width)
         return pl.ds(pl.multiple_of(core * spans[member] + begin, 128), width)
 
-    own = []
-    for member in range(count):
+    def own(member):
         cut = columns(member, 0, spans[member])
-        own.append(
-            pltpu.make_async_copy(
-                shards[member].at[:, cut],
-                wholes[member].at[spots["z"], spots["x"], spots["y"], :, cut],
-                own_sems.at[member],
-            )
+        return pltpu.make_async_copy(
+            shards[member].at[:, cut],
+            wholes[member].at[spots["z"], spots["x"], spots["y"], :, cut],
+            own_sems.at[member],
         )
-        own[-1].start()
 
     flows = flows_of(spans, GATHER_ORDERS)
-    chains = []
+    chains, first = [], []
     for member, order, begin, width, _ in flows:
         cut = columns(member, begin, width)
         steps, done = [], []
@@ -463,55 +501,77 @@
             done.append(axis)
         if not shared[member]:
             steps.append((wholes[member].at[:, :, :, :, cut], twin()))
+        first.append(sum(len(c) for c in chains))
         chains.append(steps)
-    number, started = 0, []
-    late = delays(flows, 2)
+
+    def remote(i, at):
+        block, peer = chains[i][at]
+        return pltpu.make_async_remote_copy(
+            src_ref=block,
+            dst_ref=block,
+            send_sem=send_sems.at[first[i] + at],
+            recv_sem=recv_sems.at[first[i] + at],
+            device_id=peer,
+            device_id_type=pl.DeviceIdType.MESH,
+        )
+
+    late = delays(flows, 1)
     length = max(late[i] + len(chains[i]) for i in range(len(flows)))
-    last = [None] * len(flows)
-    for copy in own:
-        copy.wait()
-    for tick in range(length + 1):
+
+    def begin():
+        greet(ring_peers() + [twin()])
+        for member in range(count):
+            own(member).start()
+        for member in range(count):
+            own(member).wait()
+
+    def tick(time):
         for i, steps in enumerate(chains):
-            at = tick - late[i]
-            if at < 0 or at > len(steps):
-                continue
-            if last[i] is not None:
-                last[i].wait_recv()
-            if at < len(steps):
-                block, peer = steps[at]
-                last[i] = pltpu.make_async_remote_copy(
-                    src_ref=block,
-                    dst_ref=block,
-                    send_sem=send_sems.at[number],
-                    recv_sem=recv_sems.at[number],
-                    device_id=peer,
-                    device_id_type=pl.DeviceIdType.MESH,
-                )
-                last[i].start()
-                started.append(last[i])
-                number += 1
-    for copy in started:
-        copy.wait_send()
-
-
-def gather_all(shards, shared):
+            at = time - late[i]
+            if 1 <= at <= len(steps):
+                remote(i, at - 1).wait_recv()
+            if 0 <= at < len(steps):
+                remote(i, at).start()
+
+    def finish():
+        for i, steps in enumerate(chains):
+            for at in range(len(steps)):
+                remote(i, at).wait_send()
+
+    return [begin] + [partial(tick, time) for time in range(length + 1)] + [finish]
+
+
+def gather_kernel(shared, *refs):
+    count = len(shared)
+    for step in gather_steps(shared, refs[:count], refs[count : 2 * count], *refs[2 * count :]):
+        step()
+
+
+def gather_scratch(shards, shared):
     parts = axis_parts()
     hops = sum(size - 1 for size in parts.values()) + 1
     spans = [s.shape[1] if shared[m] else s.shape[1] // 2 for m, s in enumerate(shards)]
     copies = hops * len(flows_of(spans, GATHER_ORDERS))
+    return [
+        pltpu.SemaphoreType.DMA((copies,)),
+        pltpu.SemaphoreType.DMA((copies,)),
+        pltpu.SemaphoreType.DMA((len(shards),)),
+    ]
+
+
+def gather_shapes(shards):
+    parts = axis_parts()
+    return [jax.ShapeDtypeStruct((parts["z"], parts["x"], parts["y"], *s.shape), s.dtype) for s in shards]
+
+
+def gather_all(shards, shared):
     wholes = pl.pallas_call(
         partial(gather_kernel, shared),
         name="gather_all",
         in_specs=[pl.BlockSpec(memory_space=pltpu.VMEM)] * len(shards),
         out_specs=[pl.BlockSpec(memory_space=pl.ANY)] * len(shards),
-        out_shape=[
-            jax.ShapeDtypeStruct((parts["z"], parts["x"], parts["y"], *s.shape), s.dtype) for s in shards
-        ],
-        scratch_shapes=[
-            pltpu.SemaphoreType.DMA((copies,)),
-            pltpu.SemaphoreType.DMA((copies,)),
-            pltpu.SemaphoreType.DMA((len(shards),)),
-        ],
+        out_shape=gather_shapes(shards),
+        scratch_shapes=gather_scratch(shards, shared),
         compiler_params=pltpu.CompilerParams(collective_id=0, has_side_effects=True),
     )(*shards)
     return [w.reshape(-1, w.shape[-1]) for w in wholes]
@@ -529,17 +589,11 @@
     return plan
 
 
-def scatter_kernel(widths, *refs):
-    count = len(widths)
-    partials, sums = refs[:count], refs[count : 2 * count]
+def scatter_steps(widths, partials, sums, send_sems, recv_sems, load_sems, *buffers):
     plan = scatter_plan(widths)
-    rest = refs[2 * count :]
-    send_sems, recv_sems, load_sems = rest[:3]
-    buffers = list(rest[3:])
+    buffers = list(buffers)
     parts, spots = axis_parts(), places()
-    rows = sums[0].shape[0]
-    greet(ring_peers())
-    chains, loads = [], 0
+    chains, copies = [], []
     for member, order, begin, width, _, levels in plan:
         cut = pl.ds(begin, width)
         chain = []
@@ -559,10 +613,8 @@
             if depth == 0:
                 for turn in range(1, size):
                     local = buffers.pop(0)
-                    copy = pltpu.make_async_copy(terms[turn], local, load_sems.at[loads])
-                    copy.start()
-                    loads += 1
-                    ready.append(copy)
+                    copies.append((terms[turn], local))
+                    ready.append(len(copies) - 1)
                     terms[turn] = local
             chain.append((axis, extent, inbox, terms, ready))
             source, before = inbox[-1], left
@@ -586,28 +638,46 @@
 
         lax.fori_loop(0, total, body, 0)
 
-    flat = []
+    flat, first = [], []
     for chain in chains:
         steps = []
         for depth, (axis, extent, inbox, terms, ready) in enumerate(chain):
-            size = parts[axis]
-            for turn in range(size - 1):
+            for turn in range(parts[axis] - 1):
                 steps.append((depth, axis, turn))
+        first.append(sum(len(f) for f in flat))
         flat.append(steps)
-    late = delays([p[:5] for p in plan], 2)
+    late = delays([p[:5] for p in plan], 1)
     length = max(late[i] + len(flat[i]) for i in range(len(plan)))
-    last, started, number = [None] * len(plan), [], 0
-    for tick in range(length + 1):
+
+    def load(index):
+        return pltpu.make_async_copy(*copies[index], load_sems.at[index])
+
+    def remote(i, at):
+        depth, axis, turn = flat[i][at]
+        _, extent, inbox, terms, ready = chains[i][depth]
+        return pltpu.make_async_remote_copy(
+            src_ref=inbox[turn - 1] if turn else terms[0],
+            dst_ref=inbox[turn],
+            send_sem=send_sems.at[first[i] + at],
+            recv_sem=recv_sems.at[first[i] + at],
+            device_id=neighbour(axis, 1),
+            device_id_type=pl.DeviceIdType.MESH,
+        )
+
+    def begin():
+        greet(ring_peers())
+        for index in range(len(copies)):
+            load(index).start()
+
+    def tick(time):
         for i, steps in enumerate(flat):
-            at = tick - late[i]
-            if at < 0 or at > len(steps):
-                continue
-            if last[i] is not None:
-                last[i].wait_recv()
+            at = time - late[i]
+            if 1 <= at <= len(steps):
+                remote(i, at - 1).wait_recv()
                 depth, axis, turn = steps[at - 1]
                 _, extent, inbox, terms, ready = chains[i][depth]
                 if ready:
-                    ready[turn].wait()
+                    load(ready[turn]).wait()
                 if at < len(steps):
                     accumulate(inbox[turn], terms[turn + 1], extent)
                 else:
@@ -615,28 +685,25 @@
                     sums[member][:, begin : begin + width] = inbox[turn][...].astype(
                         jnp.float32
                     ) + terms[turn + 1][...].astype(jnp.float32)
-            if at < len(steps):
-                depth, axis, turn = steps[at]
-                _, extent, inbox, terms, ready = chains[i][depth]
-                last[i] = pltpu.make_async_remote_copy(
-                    src_ref=inbox[turn - 1] if turn else terms[0],
-                    dst_ref=inbox[turn],
-                    send_sem=send_sems.at[number],
-                    recv_sem=recv_sems.at[number],
-                    device_id=neighbour(axis, 1),
-                    device_id_type=pl.DeviceIdType.MESH,
-                )
-                last[i].start()
-                started.append(last[i])
-                number += 1
-    for copy in started:
-        copy.wait_send()
-
-
-def scatter_all(partials):
+            if 0 <= at < len(steps):
+                remote(i, at).start()
+
+    def finish():
+        for i, steps in enumerate(flat):
+            for at in range(len(steps)):
+                remote(i, at).wait_send()
+
+    return [begin] + [partial(tick, time) for time in range(length + 1)] + [finish]
+
+
+def scatter_kernel(widths, *refs):
+    count = len(widths)
+    for step in scatter_steps(widths, refs[:count], refs[count : 2 * count], *refs[2 * count :]):
+        step()
+
+
+def scatter_scratch(widths, rows):
     parts = axis_parts()
-    widths = [p.shape[1] for p in partials]
-    rows = partials[0].shape[0] // (parts["z"] * parts["x"] * parts["y"])
     buffers, copies, loads = [], 0, 0
     for _, order, _, width, _, levels in scatter_plan(widths):
         for depth, (axis, extent, _) in enumerate(levels):
@@ -646,22 +713,98 @@
                 loads += slots
                 slots *= 2
             buffers += [pltpu.VMEM((*extent, rows, width), jnp.bfloat16)] * slots
+    return [
+        pltpu.SemaphoreType.DMA((copies,)),
+        pltpu.SemaphoreType.DMA((copies,)),
+        pltpu.SemaphoreType.DMA((loads,)),
+        *buffers,
+    ]
+
+
+def scatter_operands(partials):
+    parts = axis_parts()
+    return [p.reshape(parts["z"], parts["x"], parts["y"], -1, p.shape[1]) for p in partials]
+
+
+def spread(work, now, slots):
+    for order, step in enumerate(work[:-2]):
+        slot = 0 if order < 2 else min(slots - 1, (order - 1) * (slots - 1) // (len(work) - 2))
+        pl.when(now == slot)(step)
+
+
+def scatter_all(partials):
+    operands = scatter_operands(partials)
+    widths = [p.shape[1] for p in partials]
+    rows = operands[0].shape[3]
     return pl.pallas_call(
         partial(scatter_kernel, widths),
         name="scatter_all",
         in_specs=[pl.BlockSpec(memory_space=pl.ANY)] * len(partials),
         out_specs=[pl.BlockSpec(memory_space=pltpu.VMEM)] * len(partials),
         out_shape=[jax.ShapeDtypeStruct((rows, width), jnp.float32) for width in widths],
-        scratch_shapes=[
-            pltpu.SemaphoreType.DMA((copies,)),
-            pltpu.SemaphoreType.DMA((copies,)),
-            pltpu.SemaphoreType.DMA((loads,)),
-            *buffers,
-        ],
+        scratch_shapes=scatter_scratch(widths, rows),
         compiler_params=pltpu.CompilerParams(
             collective_id=1, has_side_effects=True, vmem_limit_bytes=67043328
         ),
-    )(*[p.reshape(parts["z"], parts["x"], parts["y"], rows, p.shape[1]) for p in partials])
+    )(*operands)
+
+
+def ffn_up_kernel(shared, x_ref, w_ref, bias_ref, *refs):
+    count = len(shared)
+    active_ref, slope_ref = refs[count : count + 2]
+    wholes = refs[count + 2 : 2 * count + 2]
+    work = gather_steps(shared, refs[:count], wholes, *refs[2 * count + 2 :])
+    now, slots = pl.program_id(0), 16
+    spread(work, now, slots)
+    rows = 256
+    for begin in range(0, x_ref.shape[0], rows):
+        block = slice(begin, begin + rows)
+        u = dot_nn(x_ref[block, :], w_ref[...]) + bias_ref[:1, :]
+        share = 0.5 + 0.5 * lax.erf(u * 0.5**0.5)
+        density = (0.5 / jnp.pi) ** 0.5 * jnp.exp(-0.5 * u * u)
+        active_ref[block, :] = (u * share).astype(jnp.bfloat16)
+        slope_ref[block, :] = (share + u * density).astype(jnp.bfloat16)
+
+    @pl.when(now == slots - 1)
+    def _():
+        for step in work[-2:]:
+            step()
+
+
+def ffn_up(x, weight, bias, shards):
+    rows, depth = x.shape
+    width = weight.shape[1]
+    tile = width // 16
+    shared = (False,) * len(shards)
+    got = pl.pallas_call(
+        partial(ffn_up_kernel, shared),
+        name="ffn_up",
+        grid=(16,),
+        in_specs=[
+            pl.BlockSpec((rows, depth), lambda i: (0, 0)),
+            pl.BlockSpec((depth, tile), lambda i: (0, i)),
+            pl.BlockSpec((8, tile), lambda i: (0, i)),
+            *[pl.BlockSpec(s.shape, lambda i: (0, 0)) for s in shards],
+        ],
+        out_specs=[
+            pl.BlockSpec((rows, tile), lambda i: (0, i)),
+            pl.BlockSpec((rows, tile), lambda i: (0, i)),
+            *[pl.BlockSpec(memory_space=pl.ANY) for s in shards],
+        ],
+        out_shape=[
+            jax.ShapeDtypeStruct((rows, width), jnp.bfloat16),
+            jax.ShapeDtypeStruct((rows, width), jnp.bfloat16),
+            *gather_shapes(shards),
+        ],
+        scratch_shapes=gather_scratch(shards, shared),
+        compiler_params=pltpu.CompilerParams(
+            vmem_limit_bytes=48 << 20, collective_id=4, has_side_effects=True
+        ),
+        cost_estimate=pl.CostEstimate(
+            flops=2 * rows * depth * width, bytes_accessed=40 << 20, transcendentals=0
+        ),
+    )(x, weight, jnp.broadcast_to(bias[None, :], (8, width)), *shards)
+    return [*got[:2], *[w.reshape(-1, w.shape[-1]) for w in got[2:]]]
 
 
 def adam_step(master, gradient, first, second, step_rate):
@@ -697,11 +840,7 @@
     width = weight_out.shape[1]
     entries = vectors.shape[0] // weight_out.shape[0]
     vector_block = jnp.pad(lowered[3].reshape(-1, entries), ((0, 0), (0, 128 - entries)))
-    full_qkv, vector_rows, full_out, full_up, full_down = gather_all(
-        [lowered[0], vector_block, lowered[1], lowered[2][0], lowered[2][1]],
-        (False, True, False, False, False),
-    )
-    full_ffn = (full_up, full_down)
+    full_qkv, vector_rows = gather_all([lowered[0], vector_block], (False, True))
     full_vec = vector_rows[:, :entries].reshape(-1)
     vector_values = full_vec.astype(jnp.float32)
     pieces = [vector_values[position * width : (position + 1) * width] for position in range(8)]
@@ -734,14 +873,15 @@
     wide_ids = lax.dynamic_slice_in_dim(segments[0], side * (local_rows - W), local_rows + W, 0)
     ids_col = jnp.broadcast_to(wide_ids[:, None], (local_rows + W, 128))
     ids_row = jnp.broadcast_to(wide_ids[None, :], (8, local_rows + W))
-    attended, attended_wide, logsum = attend(side_operand, ids_col, ids_row, projected)
+    attended, attended_wide, logsum, full_out, full_up = attend(
+        ids_col, ids_row, projected, [lowered[1], lowered[2][0]]
+    )
     branch = jnp.dot(attended, full_out, preferred_element_type=jnp.float32) + bias_output
     residue_first = token_rows.astype(jnp.float32) + branch
     hidden_in, first_pullback = jax.vjp(layer_norm, residue_first, gain_first, shift_first)
     hidden_low = hidden_in.astype(jnp.bfloat16)
-    inner = jnp.dot(hidden_low, full_ffn[0], preferred_element_type=jnp.float32) + bias_hidden
-    activated, gelu_pullback = jax.vjp(partial(jax.nn.gelu, approximate=False), inner)
-    activated_low = activated.astype(jnp.bfloat16)
+    activated_low, slope, full_down = ffn_up(hidden_low, full_up, bias_hidden, [lowered[2][1]])
+    full_ffn = (full_up, full_down)
     second_branch = (
         lax.dot_general(
             activated_low, full_ffn[1], (((1,), (1,)), ((), ())), preferred_element_type=jnp.float32
@@ -756,8 +896,7 @@
     bias_second_grad = jnp.sum(branch_two_low.astype(jnp.float32), axis=0)
     down_grad = dot_tn(branch_two_low, activated_low).astype(jnp.bfloat16)
     activated_grad = jnp.dot(branch_two_low, full_ffn[1], preferred_element_type=jnp.float32)
-    (inner_grad,) = gelu_pullback(activated_grad)
-    inner_low = inner_grad.astype(jnp.bfloat16)
+    inner_low = (activated_grad * slope.astype(jnp.float32)).astype(jnp.bfloat16)
     bias_hidden_grad = jnp.sum(inner_low.astype(jnp.float32), axis=0)
     up_grad = dot_tn(hidden_low, inner_low).astype(jnp.bfloat16)
     hidden_grad = residue_second_grad + lax.dot_general(
@@ -790,8 +929,8 @@
     lane_pad = ((0, 0), (0, 128 - heads))
     far_logsum = jnp.pad(far_stats[:, :heads], lane_pad)
     far_inner = jnp.pad(far_stats[:, heads:], lane_pad)
-    query_grad, key_near, value_near = attend_back(
-        side_operand, ids_col, ids_row, projected, mixed_grad, logsum, inner_sums
+    query_grad, key_near, value_near, down_sum, up_sum = attend_back(
+        ids_col, ids_row, projected, mixed_grad, logsum, inner_sums, [down_grad, up_grad]
     )
     key_grad, value_grad = attend_far(
         side_operand, ids_col, ids_row, projected, far_outgrad, far_logsum, far_inner, key_near, value_near
@@ -816,9 +955,7 @@
         ]
     )
     small = jnp.pad(vector_grad.reshape(width, -1), ((0, 0), (0, 128 - entries))).astype(jnp.bfloat16)
-    down_sum, up_sum, qkv_sum, small_sum, out_sum = scatter_all(
-        [down_grad, up_grad, qkv_weight_grad, small, out_weight_grad]
-    )
+    qkv_sum, small_sum, out_sum = scatter_all([qkv_weight_grad, small, out_weight_grad])
     summed = (qkv_sum, out_sum, jnp.stack([up_sum, down_sum]), small_sum[:, :entries].reshape(-1))
     firsts = (first_qkv[0], first_out[0], first_ffn[0], first_vec[0])
     seconds = (second_qkv[0], second_out[0], second_ffn[0], second_vec[0])

time: 774 us -> 672 us (0.87)
  matrix products: 186 us -> 126 us
  local copies, waits for them, and re-layouts: 38.3 us -> 15 us
  waiting for transfers between devices: 19.2 us -> 0.02 us
  other arithmetic: 41.2 us -> 50.4 us
    pallas_call x2 -> x3, Pallas kernels: 113 us -> 306 us  [the longest x1 167 us: attend_back(): pl.pallas_call(partial(attend_back_kernel, widths), name='attend_back', g...]
    pallas_call x1, Pallas kernels: 211 us -> 92.8 us  [scatter_all(): pl.pallas_call(partial(scatter_kernel, widths), name='scatter_all', in_sp...]
    pallas_call x1, Pallas kernels: 136 us -> 56.7 us  [gather_all(): pl.pallas_call(partial(gather_kernel, shared), name='gather_all', in_spec...]
    dot_general x1 -> x0, matrix products: 46.4 us -> none  [on_device(): jnp.dot(hidden_low, full_ffn[0], preferred_element_type=jnp.float32)]
    unnamed x146 -> x122, local copies, waits for them, and re-layouts: 29.6 us -> 8.9 us
    ppermute x7, waiting for transfers between devices: 19.2 us -> 0.02 us  [partner(): lax.ppermute(x, axis, [(i, i ^ 1 << stride) for i in range(lax.axis_size(...]
    dot_general x1, matrix products: 25.5 us -> 15.7 us  [on_device(): jnp.dot(branch_two_low, full_ffn[1], preferred_element_type=jnp.float32)]
  transfers between devices with their start and end apart: 7 -> 7, of which waited for: 1 -> 0; matrix products, arithmetic and copies ran while one was open for 5% -> 10% of each run, Pallas kernels for 18% -> 50%
where the time goes in v3:
time: 672 us; the launch traced here: 669 us
  Pallas kernels  470 us (70%)
  matrix products  126 us (19%)
  other arithmetic  50.4 us (8%)
  local copies, waits for them, and re-layouts  15 us (2%)
    pallas_call x1, Pallas kernels, attend_back(): pl.pallas_call(partial(attend_back_kernel, widths), name='attend_back', g...  167 us
    pallas_call x1, Pallas kernels, scatter_all(): pl.pallas_call(partial(scatter_kernel, widths), name='scatter_all', in_sp...  92.8 us
    pallas_call x1, Pallas kernels, attend(): pl.pallas_call(partial(attend_kernel, shared), name='attend', grid_spec=p...  79.5 us
    pallas_call x1, Pallas kernels, ffn_up(): pl.pallas_call(partial(ffn_up_kernel, shared), name='ffn_up', grid=(16,),...  58.7 us
    pallas_call x1, Pallas kernels, gather_all(): pl.pallas_call(partial(gather_kernel, shared), name='gather_all', in_spec...  56.7 us
    dot_general x4, matrix products, dot_tn(): lax.dot_general(a, b, (((0,), (0,)), ((), ())), preferred_element_type=jn...  42 us
    dot_general x1, matrix products, on_device(): jnp.dot(wide_tokens, full_qkv, preferred_element_type=jnp.float32)  17.9 us
    dot_general x1, matrix products, on_device(): lax.dot_general(inner_low, full_ffn[0], (((1,), (1,)), ((), ())), preferr...  17 us
  transfers between devices with their start and end apart: 7, of which 0 were waited for; matrix products, arithmetic and copies ran while one was open for 10% of the time, Pallas kernels for 50%

profile of v3, /device:TPU:0, one launch (start us, length us, event | category | flops | bytes accessed | tf_op | source)
XLA Modules:
  0.0 668.8 jit_solution(687314504199025869)
XLA Ops:
  0.7 2.8 select_bitcast_fusion
  3.5 3.0 collective-permute-start
  6.5 1.9 convert_element_type.127.refs_0_
  8.5 0.6 pad.16.refs_1_
  9.2 56.7 %gather_all.1 = (bf16[4,2,2,64,3072]{4,3,2,1,0:T(8,128)(2,1)}, bf16[4,2,2,64,128]{4,3,2,1,0:T(8,128)(2,1)}) custom-call(bf16[64,3072]{1,0:T(8,128)(2,1)} %convert_element_type.127.refs_0_, bf16[64,128]{1,0:T(8,128)(2,1)} %pad.16.refs_1_), custom_call_target="tpu_custom_call" | custom-call | tf_op jit(solution)/shard_map/gather_all/pallas_call | solution.py:568
  65.9 1.0 slice_convert_fusion
  66.9 0.4 reshape.360
  67.3 0.6 add_select_fusion
  67.9 1.7 convert_element_type.133
  69.7 1.0 reduce.4
  70.7 17.9 %add_convert_fusion.q_ref.k_ref.v_ref = bf16[1536,3072]{1,0:T(8,128)(2,1)} fusion(bf16[1024,3072]{1,0:T(8,128)(2,1)} %bitcast.121, f32[3072]{0:T(1024)S(1)} %pad_maximum_fusion.3, bf16[512,1024]{1,0:T(8,128)(2,1)} %collective-permute-done, bf16[1024,1024]{1,0:T(8,128)(2,1)} %bitcast.114, pred[]{:T(512)S(6)} %eq.16), kind=kOutput, calls=%fused_computation | convolution fusion | flops 9687269376 | bytes 18886656 | tf_op jit(solution)/shard_map/dot_general | solution.py:871
  88.6 0.3 broadcast_in_dim.37.ids_col_ref
  88.9 79.5 %attend.1 = (bf16[1024,1024]{1,0:T(8,128)(2,1)S(1)}, f32[1024,1024]{1,0:T(8,128)}, f32[1024,128]{1,0:T(8,128)S(1)}, bf16[4,2,2,64,1024]{4,3,2,1,0:T(8,128)(2,1)S(1)}, bf16[4,2,2,64,4096]{4,3,2,1,0:T(8,128)(2,1)}) custom-call(s32[1536,128]{1,0:T(8,128)S(1)} %broadcast_in_dim.37.ids_col_ref, s32[8,1536]{1,0:T(8,128)S(1)} %broadcast_in_dim.38.ids_row_ref, ...), custom_call_target="tpu_custom_call" | custom-call | flops 18253611008 | bytes 31457280 | tf_op jit(solution)/shard_map/attend/pallas_call | solution.py:152
  168.4 2.5 fusion.58
  170.9 0.5 multiply_reduce_fusion.3
  171.5 0.7 fusion.7.x_ref
  172.3 58.7 %ffn_up.1 = (bf16[1024,4096]{1,0:T(8,128)(2,1)}, bf16[1024,4096]{1,0:T(8,128)(2,1)}, bf16[4,2,2,64,4096]{4,3,2,1,0:T(8,128)(2,1)}) custom-call(bf16[1024,1024]{1,0:T(8,128)(2,1)S(1)} %fusion.7.x_ref, bf16[1024,4096]{1,0:T(8,128)(2,1)} %bitcast.124, f32[8,4096]{1,0:T(8,128)S(1)} %broadcast_in_dim.40.bias_ref, bf16[64,4096]{1,0:T(8,128)(2,1)S(1)} %get-tuple-element.99.refs_0_), custom_call_target="tpu_custom_call" | custom-call | flops 8589934592 | bytes 41943040 | tf_op jit(solution)/shard_map/ffn_up/pallas_call | solution.py:779
  231.0 14.5 %fusion.59 = (f32[1024]{0:T(1024)S(1)}, f32[1024,1024]{1,0:T(8,128)S(1)}) fusion(f32[1024]{0:T(1024)S(1)} %get-tuple-element.112, bf16[1024,4096]{1,0:T(8,128)(2,1)} %get-tuple-element.51, bf16[1024,4096]{1,0:T(8,128)(2,1)} %bitcast.127, f32[1024]{0:T(1024)S(1)} %get-tuple-element.113, f32[1024]{0:T(1024)S(1)} %get-tuple-element.114, ...), kind=kOutput, calls=%fused_computation.149 | convolution fusion | flops 8597273600 | bytes 25190400 | tf_op jit(solution)/shard_map/dot_general | solution.py:886
  245.5 0.6 multiply_reduce_fusion.2
  246.1 1.0 copy-done.8
  247.1 2.6 fusion.3
  249.7 3.4 fusion.53
  253.1 1.0 fusion.50
  254.1 14.6 %convolution_convert_fusion.1 = bf16[1024,4096]{1,0:T(8,128)(2,1)} fusion(bf16[1024,1024]{1,0:T(8,128)(2,1)S(1)} %get-tuple-element.84, bf16[1024,4096]{1,0:T(8,128)(2,1)} %get-tuple-element.51), kind=kOutput, calls=%fused_computation.3 | convolution fusion | flops 8594128896 | bytes 18874368 | tf_op jit(solution)/shard_map/dot_general | solution.py:59
  268.7 15.7 %fusion.60 = (bf16[4096]{0:T(1024)(128)(2,1)}, bf16[1024,4096]{1,0:T(8,128)(2,1)}) fusion(bf16[1024,4096]{1,0:T(8,128)(2,1)} %get-tuple-element.53, bf16[1024,1024]{1,0:T(8,128)(2,1)S(1)} %get-tuple-element.84, bf16[1024,4096]{1,0:T(8,128)(2,1)} %bitcast.128), kind=kOutput, calls=%fused_computation.150 | convolution fusion | flops 8606707712 | bytes 27271168 | tf_op jit(solution)/shard_map/dot_general | solution.py:898
  284.4 17.0 %multiply_reduce_fusion = (bf16[1024]{0:T(1024)(128)(2,1)}, f32[1024]{0:T(1024)S(1)}, bf16[1024]{0:T(1024)(128)(2,1)}, f32[1024,1024]{1,0:T(8,128)}) fusion(f32[1024,1024]{1,0:T(8,128)S(1)} %get-tuple-element.123, f32[1024]{0:T(1024)S(1)} %fusion.45, f32[1024]{0:T(1024)S(1)} %broadcast_multiply_fusion.1, f32[1024]{0:T(1024)S(1)} %get-tuple-element.114, ...), kind=kOutput, calls=%fused_computation.13 | convolution fusion | flops 8600417280 | bytes 29384704 | tf_op jit(solution)/shard_map/dot_general | solution.py:902
  301.4 14.7 %convolution_convert_fusion = bf16[1024,4096]{1,0:T(8,128)(2,1)} fusion(bf16[1024,1024]{1,0:T(8,128)(2,1)S(1)} %fusion.7.x_ref, bf16[1024,4096]{1,0:T(8,128)(2,1)} %get-tuple-element.128), kind=kOutput, calls=%fused_computation.2 | convolution fusion | flops 8594128896 | bytes 18874368 | tf_op jit(solution)/shard_map/dot_general | solution.py:59
  316.2 2.2 fusion.52
  318.4 1.3 fusion.51
  319.7 2.4 convolution_convert_fusion.4.do_ref
  322.1 1.2 slice_select_fusion
  323.3 2.3 fusion.4.inner_ref
  325.8 0.7 copy-done.26
  326.5 0.8 pad_maximum_fusion.2
  327.3 2.0 collective-permute-start.2
  329.4 167.4 %attend_back.1 = (bf16[1024,1024]{1,0:T(8,128)(2,1)}, f32[1024,1024]{1,0:T(8,128)}, f32[1024,1024]{1,0:T(8,128)}, f32[64,4096]{1,0:T(8,128)}, f32[64,4096]{1,0:T(8,128)}) custom-call(s32[1536,128]{1,0:T(8,128)} %copy-done, s32[8,1536]{1,0:T(8,128)} %copy-done.3, bf16[1536,3072]{1,0:T(8,128)(2,1)} %add_convert_fusion.q_ref.k_ref.v_ref, ...), custom_call_target="tpu_custom_call" | custom-call | flops 45634027520 | bytes 41943040 | tf_op jit(solution)/shard_map/attend_back/pallas_call | solution.py:275
  496.8 6.8 %fusion.21 = (bf16[2,64,4096]{2,1,0:T(8,128)(2,1)}, f32[1,2,64,4096]{3,2,1,0:T(8,128)}) fusion(f32[2,64,4096]{2,1,0:T(8,128)} %param.24, f32[1,2,64,4096]{3,2,1,0:T(8,128)} %param.32, f32[1,2,64,4096]{3,2,1,0:T(8,128)} %param.28, f32[1,64,4096]{2,1,0:T(8,128)} %bitcast.109, f32[1,64,4096]{2,1,0:T(8,128)} %bitcast.111), kind=kLoop, calls=%fused_computation.46 | loop fusion | flops 9437184 | bytes 11534336 | tf_op jit(solution)/shard_map/convert_element_type | solution.py:970
  503.6 2.8 fusion.14
  506.4 0.9 copy-done.25
  507.3 3.8 convolution_convert_fusion.3
  511.1 0.2 constant_dynamic-update-slice_fusion.2
  511.3 1.2 fusion.56
  512.6 14.4 %attend_far.1 = (bf16[1024,1024]{1,0:T(8,128)(2,1)S(1)}, bf16[1024,1024]{1,0:T(8,128)(2,1)}) custom-call(s32[1]{0:T(128)} %bitcast.13.side_ref, s32[1536,128]{1,0:T(8,128)S(1)} %copy-done.1, s32[8,1536]{1,0:T(8,128)S(1)} %copy-done.4, bf16[1536,3072]{1,0:T(8,128)(2,1)} %add_convert_fusion.q_ref.k_ref.v_ref, ...), custom_call_target="tpu_custom_call" | custom-call | flops 8589934592 | bytes 20971520 | tf_op jit(solution)/shard_map/attend_far/pallas_call | solution.py:366
  527.0 0.2 constant_dynamic-update-slice_fusion.1
  527.1 1.4 copy-done.30
  528.7 2.6 copy-done.12
  531.4 9.0 %convolution_convert_fusion.2 = bf16[3072,1024]{0,1:T(8,128)(2,1)} fusion(bf16[1024,3072]{1,0:T(8,128)(2,1)S(1)} %constant_dynamic-update-slice_fusion, bf16[1,1024,1024]{2,1,0:T(8,128)(2,1)S(1)} %copy-done.28), kind=kOutput, calls=%fused_computation.6 | convolution fusion | flops 6445596672 | bytes 14680064 | tf_op jit(solution)/shard_map/dot_general | solution.py:59
  540.4 3.7 reduce.1
  544.3 0.6 reshape.356
  544.9 0.8 pad.19
  545.7 92.8 %scatter_all.1 = (f32[64,3072]{1,0:T(8,128)}, f32[64,128]{1,0:T(8,128)}, f32[64,1024]{1,0:T(8,128)}) custom-call(bf16[4,2,2,64,3072]{4,3,2,1,0:T(8,128)(2,1)} %bitcast.108, bf16[4,2,2,64,128]{4,3,2,1,0:T(8,128)(2,1)} %bitcast.116, bf16[4,2,2,64,1024]{4,3,2,1,0:T(8,128)(2,1)} %bitcast.115), custom_call_target="tpu_custom_call" | custom-call | tf_op jit(solution)/shard_map/scatter_all/pallas_call | solution.py:739
  638.6 0.9 broadcast_in_dim_reshape.3
  639.5 0.9 reshape.359
  640.4 3.7 fusion.26
  644.2 1.0 fusion.28
  645.2 0.5 collective-permute-start.4
  645.7 0.6 multiply_reduce_fusion.5
  646.4 12.1 %add_bitcast_fusion = f32[1,1024,1024]{2,1,0:T(8,128)} fusion(f32[1024,1024]{1,0:T(8,128)S(1)} %copy-done.11, f32[1024]{0:T(1024)S(1)} %copy-done.41, bf16[1024,3072]{1,0:T(8,128)(2,1)} %copy-done.12, bf16[1024,3072]{1,0:T(8,128)(2,1)} %bitcast.122), kind=kOutput, calls=%fused_computation.14 | convolution fusion | flops 6444548096 | bytes 20975616 | tf_op jit(solution)/shard_map/dot_general | solution.py:941
  658.6 5.1 multiply_subtract_fusion
  663.7 0.6 multiply_subtract_fusion.3
  664.3 1.0 multiply_subtract_fusion.2
  665.3 1.7 multiply_subtract_fusion.1
  666.9 0.9 copy.83
  667.8 0.7 copy.84
  (152 shorter events, 1.1 us)
Async XLA Ops:
  0.7 7.7 %copy-start.38 = (f32[768]{0:T(1024)S(1)}, f32[768]{0:T(1024)}, u32[]{:S(2)}) copy-start(f32[768]{0:T(1024)} %param.25) | copy-start | bytes 9220
  0.7 67.2 %copy-start.22 = (f32[64,1024]{1,0:T(8,128)S(1)}, f32[64,1024]{1,0:T(8,128)}, u32[]{:S(2)}) copy-start(f32[64,1024]{1,0:T(8,128)} %param.23) | copy-start | bytes 786436
  0.7 68.9 %copy-start.49 = (s32[1,2048]{1,0:T(1,128)S(1)}, s32[1,2048]{1,0:T(1,128)}, u32[]{:S(2)}) copy-start(s32[1,2048]{1,0:T(1,128)} %param.21) | copy-start | bytes 24580
  0.7 69.0 %copy-start.7 = (bf16[1,1024,1024]{2,1,0:T(8,128)(2,1)S(1)}, bf16[1,1024,1024]{2,1,0:T(8,128)(2,1)}, u32[]{:S(2)}) copy-start(bf16[1,1024,1024]{2,1,0:T(8,128)(2,1)} %param.20) | copy-start | bytes 6291460
  3.5 67.2 %collective-permute-start = (bf16[512,1024]{1,0:T(8,128)(2,1)}, bf16[512,1024]{1,0:T(8,128)(2,1)}, u32[]{:S(2)}, u32[]{:S(2)}) collective-permute-start(bf16[512,1024]{1,0:T(8,128)(2,1)} %select_bitcast_fusion), channel_id=1, source_target_pairs={{0,1},{1,0},{2,3},{3,2},{4,5},{5,4},{6,7},{7,6},{8,9},{9,8},{10,11... | collective-permute-start | bytes 3145736 | tf_op jit(solution)/shard_map/ppermute | solution.py:28
  67.2 21.3 %copy-start.37 = (f32[12288]{0:T(1024)}, f32[12288]{0:T(1024)S(1)}, u32[]{:S(2)}) copy-start(f32[12288]{0:T(1024)S(1)} %reshape.360) | copy-start | bytes 147460
  88.8 79.5 %copy-start = (s32[1536,128]{1,0:T(8,128)}, s32[1536,128]{1,0:T(8,128)S(1)}, u32[]{:S(2)}) copy-start(s32[1536,128]{1,0:T(8,128)S(1)} %broadcast_in_dim.37.ids_col_ref) | copy-start | bytes 2359300
  88.9 79.5 %copy-start.3 = (s32[8,1536]{1,0:T(8,128)}, s32[8,1536]{1,0:T(8,128)S(1)}, u32[]{:S(2)}) copy-start(s32[8,1536]{1,0:T(8,128)S(1)} %broadcast_in_dim.38.ids_row_ref) | copy-start | bytes 147460
  88.9 79.5 %copy-start.27 = (bf16[1,1024,1024]{2,1,0:T(8,128)(2,1)S(1)}, bf16[1,1024,1024]{2,1,0:T(8,128)(2,1)}, u32[]{:S(2)}) copy-start(bf16[1,1024,1024]{2,1,0:T(8,128)(2,1)} %param.19) | copy-start | bytes 6291460
  168.4 2.5 copy-start.5
  168.4 157.3 %copy-start.2 = (f32[1024,128]{1,0:T(8,128)}, f32[1024,128]{1,0:T(8,128)S(1)}, u32[]{:S(2)}) copy-start(f32[1024,128]{1,0:T(8,128)S(1)} %get-tuple-element.54.lse_ref) | copy-start | bytes 1572868
  171.5 0.8 slice-start
  245.5 1.6 copy-start.8
  301.4 14.8 %copy-start.17 = (f32[1024,1024]{1,0:T(8,128)S(1)}, f32[1024,1024]{1,0:T(8,128)}, u32[]{:S(2)}) copy-start(f32[1024,1024]{1,0:T(8,128)} %get-tuple-element.126) | copy-start | bytes 12582916
  318.3 3.8 copy-start.10
  318.4 1.3 copy-start.40
  319.7 2.4 copy-start.24
  319.7 3.6 copy-start.18
  319.7 3.6 copy-start.42
  322.1 3.5 copy-start.13
  323.3 189.2 %collective-permute-start.1 = (bf16[512,1024]{1,0:T(8,128)(2,1)}, bf16[512,1024]{1,0:T(8,128)(2,1)}, u32[]{:S(2)}, u32[]{:S(2)}) collective-permute-start(bf16[512,1024]{1,0:T(8,128)(2,1)} %slice_select_fusion), channel_id=1, source_target_pairs={{0,1},{1,0},{2,3},{3,2},{4,5},{5,4},{6,7},{7,6},{8,9},{9,8},{10,11... | collective-permute-start | bytes 3145736 | tf_op jit(solution)/shard_map/ppermute | solution.py:28
  325.7 0.8 copy-start.26
  327.3 183.9 %collective-permute-start.2 = (f32[512,32]{1,0:T(8,128)}, f32[512,32]{1,0:T(8,128)}, u32[]{:S(2)}, u32[]{:S(2)}) collective-permute-start(f32[512,32]{1,0:T(8,128)} %pad_maximum_fusion.2), channel_id=1, source_target_pairs={{0,1},{1,0},{2,3},{3,2},{4,5},{5,4},{6,7},{7,6},{8,9},{9,8},{10,11... | collective-permute-start | bytes 196616 | tf_op jit(solution)/shard_map/ppermute | solution.py:28
  496.8 6.8 %copy-start.14 = (f32[1,2,64,4096]{3,2,1,0:T(8,128)S(1)}, f32[1,2,64,4096]{3,2,1,0:T(8,128)}, u32[]{:S(2)}) copy-start(f32[1,2,64,4096]{3,2,1,0:T(8,128)} %param.32) | copy-start | bytes 6291460
  496.8 6.8 %copy-start.15 = (f32[1,2,64,4096]{3,2,1,0:T(8,128)S(1)}, f32[1,2,64,4096]{3,2,1,0:T(8,128)}, u32[]{:S(2)}) copy-start(f32[1,2,64,4096]{3,2,1,0:T(8,128)} %param.28) | copy-start | bytes 6291460
  496.8 6.8 %copy-start.19 = (f32[64,4096]{1,0:T(8,128)S(1)}, f32[64,4096]{1,0:T(8,128)}, u32[]{:S(2)}) copy-start(f32[64,4096]{1,0:T(8,128)} %get-tuple-element.64) | copy-start | bytes 3145732
  496.8 6.8 %copy-start.20 = (f32[64,4096]{1,0:T(8,128)S(1)}, f32[64,4096]{1,0:T(8,128)}, u32[]{:S(2)}) copy-start(f32[64,4096]{1,0:T(8,128)} %get-tuple-element.63) | copy-start | bytes 3145732
  503.6 155.0 %collective-permute-start.5 = (bf16[2,64,4096]{2,1,0:T(8,128)(2,1)}, bf16[2,64,4096]{2,1,0:T(8,128)(2,1)}, u32[]{:S(2)}, u32[]{:S(2)}) collective-permute-start(bf16[2,64,4096]{2,1,0:T(8,128)(2,1)} %get-tuple-element.92), channel_id=1, source_target_pairs={{0,16},{16,0},{1,17},{17,1},{2,18},{18,2},{3,19},{19,3},{4,20},{20... | collective-permute-start | bytes 3145736 | tf_op jit(solution)/shard_map/ppermute | solution.py:28
  503.6 2.8 copy-start.6
  503.6 3.7 copy-start.25
  507.3 3.8 copy-start.29
  511.1 1.5 copy-start.1
  511.1 1.5 copy-start.4
  527.0 1.6 copy-start.30
  527.0 4.4 copy-start.28
  528.7 2.6 copy-start.12
  540.3 3.8 copy-start.45
  540.3 3.8 copy-start.44
  540.4 3.9 copy-start.54
  540.4 3.9 copy-start.53
  540.4 3.9 copy-start.46
  540.4 3.9 copy-start.48
  540.4 3.9 copy-start.47
  638.5 5.7 copy-start.23
  638.5 5.7 copy-start.32
  638.5 5.7 copy-start.34
  638.5 5.7 copy-start.35
  638.5 7.1 %copy-start.51 = (f32[1,768]{1,0:T(1,128)S(1)}, f32[1,768]{1,0:T(1,128)}, u32[]{:S(2)}) copy-start(f32[1,768]{1,0:T(1,128)} %param.29) | copy-start | bytes 9220
  638.5 7.1 %copy-start.52 = (f32[1,768]{1,0:T(1,128)S(1)}, f32[1,768]{1,0:T(1,128)}, u32[]{:S(2)}) copy-start(f32[1,768]{1,0:T(1,128)} %param.33) | copy-start | bytes 9220
  638.6 7.7 %copy-start.39 = (f32[768]{0:T(1024)S(1)}, f32[768]{0:T(1024)}, u32[]{:S(2)}) copy-start(f32[768]{0:T(1024)} %param.25) | copy-start | bytes 9220
  638.6 7.8 %copy-start.41 = (f32[1024]{0:T(1024)S(1)}, f32[1024]{0:T(1024)}, u32[]{:S(2)}) copy-start(f32[1024]{0:T(1024)} %copy-done.40) | copy-start | bytes 12292
  639.5 19.0 %copy-start.43 = (f32[1,768]{1,0:T(1,128)}, f32[1,768]{1,0:T(1,128)S(1)}, u32[]{:S(2)}) copy-start(f32[1,768]{1,0:T(1,128)S(1)} %broadcast_in_dim_reshape.3) | copy-start | bytes 9220
  640.4 6.0 copy-start.11
  644.2 21.1 %collective-permute-start.3 = (bf16[64,3072]{1,0:T(8,128)(2,1)S(1)}, bf16[64,3072]{1,0:T(8,128)(2,1)S(1)}, u32[]{:S(2)}, u32[]{:S(2)}) collective-permute-start(bf16[64,3072]{1,0:T(8,128)(2,1)S(1)} %get-tuple-element.96), channel_id=1, source_target_pairs={{0,16},{16,0},{1,17},{17,1},{2,18},{18,2},{3,19},{19,3},{4,20},{20... | collective-permute-start | bytes 1179656 | tf_op jit(solution)/shard_map/ppermute | solution.py:28
  645.2 19.1 %collective-permute-start.4 = (bf16[64,1024]{1,0:T(8,128)(2,1)S(1)}, bf16[64,1024]{1,0:T(8,128)(2,1)S(1)}, u32[]{:S(2)}, u32[]{:S(2)}) collective-permute-start(bf16[64,1024]{1,0:T(8,128)(2,1)S(1)} %get-tuple-element.101), channel_id=1, source_target_pairs={{0,16},{16,0},{1,17},{17,1},{2,18},{18,2},{3,19},{19,3},{4,20},{20... | collective-permute-start | bytes 393224 | tf_op jit(solution)/shard_map/ppermute | solution.py:28
  646.3 12.3 %copy-start.9 = (f32[2,64,4096]{2,1,0:T(8,128)S(1)}, f32[2,64,4096]{2,1,0:T(8,128)}, u32[]{:S(2)}) copy-start(f32[2,64,4096]{2,1,0:T(8,128)} %param.24) | copy-start | bytes 6291460
  646.3 12.3 %copy-start.31 = (f32[2,64,4096]{2,1,0:T(8,128)S(1)}, f32[2,64,4096]{2,1,0:T(8,128)}, u32[]{:S(2)}) copy-start(f32[2,64,4096]{2,1,0:T(8,128)} %param.36) | copy-start | bytes 6291460
  646.3 17.4 %collective-permute-start.6 = (bf16[768]{0:T(1024)(128)(2,1)S(1)}, bf16[768]{0:T(1024)(128)(2,1)S(1)}, u32[]{:S(2)}, u32[]{:S(2)}) collective-permute-start(bf16[768]{0:T(1024)(128)(2,1)S(1)} %fusion.43), channel_id=1, source_target_pairs={{0,16},{16,0},{1,17},{17,1},{2,18},{18,2},{3,19},{19,3},{4,20},{20... | collective-permute-start | bytes 4616 | tf_op jit(solution)/shard_map/ppermute | solution.py:28
  658.5 5.2 copy-start.50
  658.5 5.8 copy-start.36
  658.5 6.7 %copy-start.16 = (f32[64,3072]{1,0:T(8,128)S(1)}, f32[64,3072]{1,0:T(8,128)}, u32[]{:S(2)}) copy-start(f32[64,3072]{1,0:T(8,128)} %param.22) | copy-start | bytes 2359300
  658.5 6.7 %copy-start.33 = (f32[64,3072]{1,0:T(8,128)S(1)}, f32[64,3072]{1,0:T(8,128)}, u32[]{:S(2)}) copy-start(f32[64,3072]{1,0:T(8,128)} %param.34) | copy-start | bytes 2359300
  663.7 3.3 copy-start.21

commit v4 on v3

--- a/solution.py
+++ b/solution.py
@@ -97,7 +97,7 @@
     now = j * pl.num_programs(1) + pair
     slots = 32
     work = gather_steps(shared, refs[:count], wholes, *refs[2 * count + 4 :])
-    spread(work, now, slots)
+    spread(work, now, slots, 0)
 
     def run(length):
         span = length * TILE
@@ -202,7 +202,7 @@
     own = dk_ref.shape[0]
     now, slots = pair * pl.num_programs(1) + j, 32
     work = scatter_steps(widths, refs[:count], sums, *refs[2 * count + 6 :])
-    spread(work, now, slots)
+    spread(work, now, slots, chunks(widths))
 
     @pl.when(j == 0)
     def _():
@@ -438,7 +438,7 @@
 def flows_of(widths, orders):
     flows = []
     for member, width in enumerate(widths):
-        pieces = max(1, min(4, width // PIECE))
+        pieces = chunks([width])
         for piece in range(pieces):
             tiles, begin = width // pieces // 128, piece * (width // pieces)
             if tiles < len(orders):
@@ -696,12 +696,6 @@
     return [begin] + [partial(tick, time) for time in range(length + 1)] + [finish]
 
 
-def scatter_kernel(widths, *refs):
-    count = len(widths)
-    for step in scatter_steps(widths, refs[:count], refs[count : 2 * count], *refs[2 * count :]):
-        step()
-
-
 def scatter_scratch(widths, rows):
     parts = axis_parts()
     buffers, copies, loads = [], 0, 0
@@ -726,27 +720,21 @@
     return [p.reshape(parts["z"], parts["x"], parts["y"], -1, p.shape[1]) for p in partials]
 
 
-def spread(work, now, slots):
+def spread(work, now, slots, busy):
+    ticks = len(work) - 3
     for order, step in enumerate(work[:-2]):
-        slot = 0 if order < 2 else min(slots - 1, (order - 1) * (slots - 1) // (len(work) - 2))
+        time = max(0, order - 1)
+        if busy:
+            slot = min(slots - 1, time * slots // busy)
+        elif time < 4:
+            slot = time
+        else:
+            slot = 3 + (time - 3) * (slots - 4) // (ticks - 3)
         pl.when(now == slot)(step)
 
 
-def scatter_all(partials):
-    operands = scatter_operands(partials)
-    widths = [p.shape[1] for p in partials]
-    rows = operands[0].shape[3]
-    return pl.pallas_call(
-        partial(scatter_kernel, widths),
-        name="scatter_all",
-        in_specs=[pl.BlockSpec(memory_space=pl.ANY)] * len(partials),
-        out_specs=[pl.BlockSpec(memory_space=pltpu.VMEM)] * len(partials),
-        out_shape=[jax.ShapeDtypeStruct((rows, width), jnp.float32) for width in widths],
-        scratch_shapes=scatter_scratch(widths, rows),
-        compiler_params=pltpu.CompilerParams(
-            collective_id=1, has_side_effects=True, vmem_limit_bytes=67043328
-        ),
-    )(*operands)
+def chunks(widths):
+    return sum(max(1, min(4, width // PIECE)) for width in widths)
 
 
 def ffn_up_kernel(shared, x_ref, w_ref, bias_ref, *refs):
@@ -755,7 +743,7 @@
     wholes = refs[count + 2 : 2 * count + 2]
     work = gather_steps(shared, refs[:count], wholes, *refs[2 * count + 2 :])
     now, slots = pl.program_id(0), 16
-    spread(work, now, slots)
+    spread(work, now, slots, 0)
     rows = 256
     for begin in range(0, x_ref.shape[0], rows):
         block = slice(begin, begin + rows)
@@ -805,6 +793,122 @@
         ),
     )(x, weight, jnp.broadcast_to(bias[None, :], (8, width)), *shards)
     return [*got[:2], *[w.reshape(-1, w.shape[-1]) for w in got[2:]]]
+
+
+def ffn_back_kernel(widths, dz_ref, down_ref, slope_ref, turned_ref, up_ref, *refs):
+    count = len(widths)
+    up_grad_ref, bias_ref, total_ref = refs[count : count + 3]
+    sums = refs[count + 3 : 2 * count + 3]
+    work = scatter_steps(widths, refs[:count], sums, *refs[2 * count + 3 :])
+    now, slots = pl.program_id(0), 16
+    spread(work, now, slots, chunks(widths))
+
+    @pl.when(now == 0)
+    def _():
+        total_ref[...] = jnp.zeros_like(total_ref)
+
+    inner = (dot_nn(dz_ref[...], down_ref[...]) * slope_ref[...].astype(jnp.float32)).astype(jnp.bfloat16)
+    column = jnp.sum(inner.astype(jnp.float32), axis=0, keepdims=True)
+    bias_ref[...] = jnp.broadcast_to(column, bias_ref.shape)
+    up_grad_ref[...] = dot_nn(turned_ref[...], inner).astype(jnp.bfloat16)
+    total_ref[...] += dot_nt(inner, up_ref[...])
+
+    @pl.when(now == slots - 1)
+    def _():
+        for step in work[-2:]:
+            step()
+
+
+def ffn_back(dz, weight_down, slope, turned, weight_up, partials):
+    rows, depth = dz.shape
+    width = weight_up.shape[1]
+    tile = width // 16
+    operands = scatter_operands(partials)
+    widths = [p.shape[1] for p in partials]
+    shard_rows = operands[0].shape[3]
+    whole = pl.BlockSpec((rows, depth), lambda i: (0, 0))
+    return pl.pallas_call(
+        partial(ffn_back_kernel, widths),
+        name="ffn_back",
+        grid=(16,),
+        in_specs=[
+            whole,
+            pl.BlockSpec((depth, tile), lambda i: (0, i)),
+            pl.BlockSpec((rows, tile), lambda i: (0, i)),
+            pl.BlockSpec((depth, rows), lambda i: (0, 0)),
+            pl.BlockSpec((depth, tile), lambda i: (0, i)),
+            *[pl.BlockSpec(memory_space=pl.ANY) for _ in widths],
+        ],
+        out_specs=[
+            pl.BlockSpec((depth, tile), lambda i: (0, i)),
+            pl.BlockSpec((8, tile), lambda i: (0, i)),
+            whole,
+            *[pl.BlockSpec((shard_rows, w), lambda i: (0, 0)) for w in widths],
+        ],
+        out_shape=[
+            jax.ShapeDtypeStruct((depth, width), jnp.bfloat16),
+            jax.ShapeDtypeStruct((8, width), jnp.float32),
+            jax.ShapeDtypeStruct((rows, depth), jnp.float32),
+            *[jax.ShapeDtypeStruct((shard_rows, w), jnp.float32) for w in widths],
+        ],
+        scratch_shapes=scatter_scratch(widths, shard_rows),
+        compiler_params=pltpu.CompilerParams(
+            vmem_limit_bytes=67043328, collective_id=5, has_side_effects=True
+        ),
+        cost_estimate=pl.CostEstimate(
+            flops=6 * rows * depth * width, bytes_accessed=60 << 20, transcendentals=0
+        ),
+    )(dz, weight_down, slope, turned, weight_up, *operands)
+
+
+def finish_kernel(widths, base_ref, grad_ref, weight_ref, *refs):
+    count = len(widths)
+    out_ref = refs[count]
+    sums = refs[count + 1 : 2 * count + 1]
+    work = scatter_steps(widths, refs[:count], sums, *refs[2 * count + 1 :])
+    now, slots = pl.program_id(0), 16
+    spread(work, now, slots, chunks(widths))
+    out_ref[...] = base_ref[...] + dot_nt(grad_ref[...], weight_ref[...])
+
+    @pl.when(now == slots - 1)
+    def _():
+        for step in work[-2:]:
+            step()
+
+
+def finish(base, grad, weight, partials):
+    rows, depth = base.shape
+    width = grad.shape[1]
+    tile = rows // 16
+    operands = scatter_operands(partials)
+    widths = [p.shape[1] for p in partials]
+    shard_rows = operands[0].shape[3]
+    return pl.pallas_call(
+        partial(finish_kernel, widths),
+        name="finish",
+        grid=(16,),
+        in_specs=[
+            pl.BlockSpec((tile, depth), lambda i: (i, 0)),
+            pl.BlockSpec((tile, width), lambda i: (i, 0)),
+            pl.BlockSpec((depth, width), lambda i: (0, 0)),
+            *[pl.BlockSpec(memory_space=pl.ANY) for _ in widths],
+        ],
+        out_specs=[
+            pl.BlockSpec((tile, depth), lambda i: (i, 0)),
+            *[pl.BlockSpec((shard_rows, w), lambda i: (0, 0)) for w in widths],
+        ],
+        out_shape=[
+            jax.ShapeDtypeStruct((rows, depth), jnp.float32),
+            *[jax.ShapeDtypeStruct((shard_rows, w), jnp.float32) for w in widths],
+        ],
+        scratch_shapes=scatter_scratch(widths, shard_rows),
+        compiler_params=pltpu.CompilerParams(
+            vmem_limit_bytes=67043328, collective_id=1, has_side_effects=True
+        ),
+        cost_estimate=pl.CostEstimate(
+            flops=2 * rows * depth * width, bytes_accessed=30 << 20, transcendentals=0
+        ),
+    )(base, grad, weight, *operands)
 
 
 def adam_step(master, gradient, first, second, step_rate):
@@ -881,10 +985,9 @@
     hidden_in, first_pullback = jax.vjp(layer_norm, residue_first, gain_first, shift_first)
     hidden_low = hidden_in.astype(jnp.bfloat16)
     activated_low, slope, full_down = ffn_up(hidden_low, full_up, bias_hidden, [lowered[2][1]])
-    full_ffn = (full_up, full_down)
     second_branch = (
         lax.dot_general(
-            activated_low, full_ffn[1], (((1,), (1,)), ((), ())), preferred_element_type=jnp.float32
+            activated_low, full_down, (((1,), (1,)), ((), ())), preferred_element_type=jnp.float32
         )
         + bias_second
     )
@@ -895,13 +998,11 @@
     branch_two_low = residue_second_grad.astype(jnp.bfloat16)
     bias_second_grad = jnp.sum(branch_two_low.astype(jnp.float32), axis=0)
     down_grad = dot_tn(branch_two_low, activated_low).astype(jnp.bfloat16)
-    activated_grad = jnp.dot(branch_two_low, full_ffn[1], preferred_element_type=jnp.float32)
-    inner_low = (activated_grad * slope.astype(jnp.float32)).astype(jnp.bfloat16)
-    bias_hidden_grad = jnp.sum(inner_low.astype(jnp.float32), axis=0)
-    up_grad = dot_tn(hidden_low, inner_low).astype(jnp.bfloat16)
-    hidden_grad = residue_second_grad + lax.dot_general(
-        inner_low, full_ffn[0], (((1,), (1,)), ((), ())), preferred_element_type=jnp.float32
-    )
+    up_grad, bias_rows, hidden_total, down_sum = ffn_back(
+        branch_two_low, full_down, slope, jnp.transpose(hidden_low), full_up, [down_grad]
+    )
+    bias_hidden_grad = bias_rows[0]
+    hidden_grad = residue_second_grad + hidden_total
     residue_first_grad, gain_first_grad, shift_first_grad = first_pullback(hidden_grad)
     branch_low = residue_first_grad.astype(jnp.bfloat16)
     bias_output_grad = jnp.sum(branch_low.astype(jnp.float32), axis=0)
@@ -929,8 +1030,8 @@
     lane_pad = ((0, 0), (0, 128 - heads))
     far_logsum = jnp.pad(far_stats[:, :heads], lane_pad)
     far_inner = jnp.pad(far_stats[:, heads:], lane_pad)
-    query_grad, key_near, value_near, down_sum, up_sum = attend_back(
-        ids_col, ids_row, projected, mixed_grad, logsum, inner_sums, [down_grad, up_grad]
+    query_grad, key_near, value_near, up_sum = attend_back(
+        ids_col, ids_row, projected, mixed_grad, logsum, inner_sums, [up_grad]
     )
     key_grad, value_grad = attend_far(
         side_operand, ids_col, ids_row, projected, far_outgrad, far_logsum, far_inner, key_near, value_near
@@ -938,9 +1039,6 @@
     projected_grad = jnp.concatenate([query_grad, key_grad, value_grad], axis=1)
     qkv_weight_grad = dot_tn(token_rows, projected_grad).astype(jnp.bfloat16)
     projected_sums = jnp.sum(projected_grad.astype(jnp.float32), axis=0)
-    input_grad = residue_first_grad + lax.dot_general(
-        projected_grad, full_qkv, (((1,), (1,)), ((), ())), preferred_element_type=jnp.float32
-    )
     vector_grad = jnp.concatenate(
         [
             projected_sums[:width],
@@ -955,7 +1053,9 @@
         ]
     )
     small = jnp.pad(vector_grad.reshape(width, -1), ((0, 0), (0, 128 - entries))).astype(jnp.bfloat16)
-    qkv_sum, small_sum, out_sum = scatter_all([qkv_weight_grad, small, out_weight_grad])
+    input_grad, qkv_sum, small_sum, out_sum = finish(
+        residue_first_grad, projected_grad, full_qkv, [qkv_weight_grad, small, out_weight_grad]
+    )
     summed = (qkv_sum, out_sum, jnp.stack([up_sum, down_sum]), small_sum[:, :entries].reshape(-1))
     firsts = (first_qkv[0], first_out[0], first_ffn[0], first_vec[0])
     seconds = (second_qkv[0], second_out[0], second_ffn[0], second_vec[0])

time: 672 us -> 656 us (0.976)
  matrix products: 126 us -> 66.9 us
  Pallas kernels: 470 us -> 488 us
  other arithmetic: 50.4 us -> 63.2 us
  local copies, waits for them, and re-layouts: 15 us -> 22.6 us
    pallas_call x1 -> x2, Pallas kernels: 92.8 us -> 181 us  [the longest x1 90.8 us: finish(): pl.pallas_call(partial(finish_kernel, widths), name='finish', grid=(16,),...]
    pallas_call x1, Pallas kernels: 167 us -> 98.2 us  [attend_back(): pl.pallas_call(partial(attend_back_kernel, widths), name='attend_back', g...]
    dot_general x4 -> x1, matrix products: 59.3 us -> 14.4 us  [on_device(): lax.dot_general(activated_low, full_down, (((1,), (1,)), ((), ())), prefe...]
    dot_general x4 -> x3, matrix products: 42 us -> 28 us  [dot_tn(): lax.dot_general(a, b, (((0,), (0,)), ((), ())), preferred_element_type=jn...]
    reduce_sum x2 -> x3, other arithmetic: 3.56 us -> 10.6 us  [layer_norm(): return centred * lax.rsqrt(variance + norm_eps) * norm_gain + norm_shift]
  transfers between devices with their start and end apart: 7 -> 7, of which waited for: 0 -> 1; matrix products, arithmetic and copies ran while one was open for 10% -> 8% of each run, Pallas kernels for 50% -> 25%
where the time goes in v4:
time: 656 us; the launch traced here: 652 us
  Pallas kernels  488 us (74%)
  matrix products  66.9 us (10%)
  other arithmetic  63.2 us (10%)
  local copies, waits for them, and re-layouts  22.6 us (3%)
    pallas_call x1, Pallas kernels, attend_back(): pl.pallas_call(partial(attend_back_kernel, widths), name='attend_back', g...  98.2 us
    pallas_call x1, Pallas kernels, finish(): pl.pallas_call(partial(finish_kernel, widths), name='finish', grid=(16,),...  90.8 us
    pallas_call x1, Pallas kernels, ffn_back(): pl.pallas_call(partial(ffn_back_kernel, widths), name='ffn_back', grid=(1...  90.1 us
    pallas_call x1, Pallas kernels, attend(): pl.pallas_call(partial(attend_kernel, shared), name='attend', grid_spec=p...  78.4 us
    pallas_call x1, Pallas kernels, ffn_up(): pl.pallas_call(partial(ffn_up_kernel, shared), name='ffn_up', grid=(16,),...  59.4 us
    pallas_call x1, Pallas kernels, gather_all(): pl.pallas_call(partial(gather_kernel, shared), name='gather_all', in_spec...  56.7 us
    dot_general x3, matrix products, dot_tn(): lax.dot_general(a, b, (((0,), (0,)), ((), ())), preferred_element_type=jn...  28 us
    dot_general x1, matrix products, on_device(): jnp.dot(wide_tokens, full_qkv, preferred_element_type=jnp.float32)  17.2 us
  transfers between devices with their start and end apart: 7, of which 1 were waited for; matrix products, arithmetic and copies ran while one was open for 8% of the time, Pallas kernels for 25%

profile of v4, /device:TPU:0, one launch (start us, length us, event | category | flops | bytes accessed | tf_op | source)
XLA Modules:
  0.0 652.2 jit_solution(10759217046422597936)
XLA Ops:
  0.7 2.8 select_bitcast_fusion
  3.5 3.0 collective-permute-start
  6.5 1.9 convert_element_type.115.refs_0_
  8.5 0.6 pad.16.refs_1_
  9.1 56.7 %gather_all.1 = (bf16[4,2,2,64,3072]{4,3,2,1,0:T(8,128)(2,1)}, bf16[4,2,2,64,128]{4,3,2,1,0:T(8,128)(2,1)}) custom-call(bf16[64,3072]{1,0:T(8,128)(2,1)} %convert_element_type.115.refs_0_, bf16[64,128]{1,0:T(8,128)(2,1)} %pad.16.refs_1_), custom_call_target="tpu_custom_call" | custom-call | tf_op jit(solution)/shard_map/gather_all/pallas_call | solution.py:568
  65.9 1.0 slice_convert_fusion
  67.3 0.6 add_select_fusion
  67.9 1.7 convert_element_type.121
  69.7 1.0 reduce.4
  70.7 17.2 %add_convert_fusion.q_ref.k_ref.v_ref = bf16[1536,3072]{1,0:T(8,128)(2,1)} fusion(bf16[1024,3072]{1,0:T(8,128)(2,1)} %bitcast.99, f32[3072]{0:T(1024)S(1)} %pad_maximum_fusion.3, bf16[512,1024]{1,0:T(8,128)(2,1)} %collective-permute-done, bf16[1024,1024]{1,0:T(8,128)(2,1)} %bitcast.109, pred[]{:T(512)S(6)} %eq.16), kind=kOutput, calls=%fused_computation | convolution fusion | flops 9687269376 | bytes 18886656 | tf_op jit(solution)/shard_map/dot_general | solution.py:975
  88.3 78.4 %attend.1 = (bf16[1024,1024]{1,0:T(8,128)(2,1)S(1)}, f32[1024,1024]{1,0:T(8,128)}, f32[1024,128]{1,0:T(8,128)S(1)}, bf16[4,2,2,64,1024]{4,3,2,1,0:T(8,128)(2,1)S(1)}, bf16[4,2,2,64,4096]{4,3,2,1,0:T(8,128)(2,1)}) custom-call(s32[1536,128]{1,0:T(8,128)S(1)} %broadcast_in_dim.37.ids_col_ref, s32[8,1536]{1,0:T(8,128)S(1)} %broadcast_in_dim.38.ids_row_ref, ...), custom_call_target="tpu_custom_call" | custom-call | flops 18253611008 | bytes 31457280 | tf_op jit(solution)/shard_map/attend/pallas_call | solution.py:152
  166.7 2.5 fusion.60
  169.3 0.5 multiply_reduce_fusion.3
  169.8 0.7 fusion.7.x_ref
  170.6 2.0 fusion.72
  172.6 59.4 %ffn_up.1 = (bf16[1024,4096]{1,0:T(8,128)(2,1)}, bf16[1024,4096]{1,0:T(8,128)(2,1)}, bf16[4,2,2,64,4096]{4,3,2,1,0:T(8,128)(2,1)}) custom-call(bf16[1024,1024]{1,0:T(8,128)(2,1)S(1)} %fusion.7.x_ref, bf16[1024,4096]{1,0:T(8,128)(2,1)} %bitcast.115, f32[8,4096]{1,0:T(8,128)S(1)} %broadcast_in_dim.40.bias_ref, bf16[64,4096]{1,0:T(8,128)(2,1)S(1)} %get-tuple-element.108.refs_0_), custom_call_target="tpu_custom_call" | custom-call | flops 8589934592 | bytes 41943040 | tf_op jit(solution)/shard_map/ffn_up/pallas_call | solution.py:767
  232.1 14.4 %fusion.61 = (f32[1024]{0:T(1024)S(1)}, f32[1024,1024]{1,0:T(8,128)S(1)}) fusion(f32[1024]{0:T(1024)S(1)} %get-tuple-element.121, bf16[1024,4096]{1,0:T(8,128)(2,1)} %get-tuple-element.55, bf16[1024,4096]{1,0:T(8,128)(2,1)} %bitcast.118, f32[1024]{0:T(1024)S(1)} %get-tuple-element.122, f32[1024]{0:T(1024)S(1)} %get-tuple-element.123, ...), kind=kOutput, calls=%fused_computation.150 | convolution fusion | flops 8597273600 | bytes 25190400 | tf_op jit(solution)/shard_map/dot_general | solution.py:989
  246.6 0.5 multiply_reduce_fusion.2
  247.1 3.0 fusion.3
  250.2 3.8 fusion.55
  254.0 3.9 copy.68.turned_ref
  257.9 3.2 fusion.53
  261.1 15.3 %convolution_convert_fusion = bf16[1024,4096]{1,0:T(8,128)(2,1)} fusion(bf16[1024,1024]{1,0:T(8,128)(2,1)S(1)} %get-tuple-element.92.dz_ref, bf16[1024,4096]{1,0:T(8,128)(2,1)} %get-tuple-element.55), kind=kOutput, calls=%fused_computation.1 | convolution fusion | flops 8594128896 | bytes 18874368 | tf_op jit(solution)/shard_map/dot_general | solution.py:59
  276.4 90.1 %ffn_back.1 = (bf16[1024,4096]{1,0:T(8,128)(2,1)}, f32[8,4096]{1,0:T(8,128)}, f32[1024,1024]{1,0:T(8,128)}, f32[64,4096]{1,0:T(8,128)}) custom-call(bf16[1024,1024]{1,0:T(8,128)(2,1)} %copy-done.28, bf16[1024,4096]{1,0:T(8,128)(2,1)} %bitcast.119, bf16[1024,4096]{1,0:T(8,128)(2,1)} %get-tuple-element.57.slope_ref, bf16[1024,1024]{1,0:T(8,128)(2,1)} %copy.68.turned_ref, ...), custom_call_target="tpu_custom_call" | custom-call | flops 25769803776 | bytes 62914560 | tf_op jit(solution)/shard_map/ffn_back/pallas_call | solution.py:830
  366.6 6.6 %multiply_reduce_fusion = (bf16[1024]{0:T(1024)(128)(2,1)}, f32[1024]{0:T(1024)S(1)}, bf16[1024]{0:T(1024)(128)(2,1)}, f32[1024,1024]{1,0:T(8,128)S(1)}) fusion(f32[1024,1024]{1,0:T(8,128)} %copy-done.10, f32[1024]{0:T(1024)} %copy-done.44, f32[1024]{0:T(1024)} %copy-done.40, f32[1024]{0:T(1024)} %copy-done.42, f32[1024,1024]{1,0:T(8,128)} %get-tuple-element.58, ...), kind=kLoop, calls=%fused_computation.11 | loop fusion | flops 10482688 | bytes 16801792 | tf_op jit(solution)/shard_map/transpose(jvp())/reduce_sum | solution.py:35
  373.2 1.7 fusion.54
  374.9 1.0 convert_reduce_fusion
  375.9 0.6 copy-done.7
  376.5 2.4 convolution_convert_fusion.3.do_ref
  378.9 1.2 slice_select_fusion
  380.2 2.3 fusion.4.inner_ref
  382.5 1.0 fusion.57
  383.5 0.8 fusion.56
  384.3 98.2 %attend_back.1 = (bf16[1024,1024]{1,0:T(8,128)(2,1)}, f32[1024,1024]{1,0:T(8,128)}, f32[1024,1024]{1,0:T(8,128)}, f32[64,4096]{1,0:T(8,128)}) custom-call(s32[1536,128]{1,0:T(8,128)} %copy-done, s32[8,1536]{1,0:T(8,128)} %copy-done.4, bf16[1536,3072]{1,0:T(8,128)(2,1)} %add_convert_fusion.q_ref.k_ref.v_ref, ...), custom_call_target="tpu_custom_call" | custom-call | flops 45634027520 | bytes 41943040 | tf_op jit(solution)/shard_map/attend_back/pallas_call | solution.py:275
  482.6 1.5 collective-permute-start.1
  484.1 1.2 slice_select_fusion.1
  485.4 0.7 collective-permute-start.2
  486.1 6.8 %fusion.21 = (bf16[2,64,4096]{2,1,0:T(8,128)(2,1)}, f32[1,2,64,4096]{3,2,1,0:T(8,128)}) fusion(f32[2,64,4096]{2,1,0:T(8,128)} %param.24, f32[1,2,64,4096]{3,2,1,0:T(8,128)} %param.32, f32[1,2,64,4096]{3,2,1,0:T(8,128)} %param.28, f32[1,64,4096]{2,1,0:T(8,128)} %bitcast.103, f32[1,64,4096]{2,1,0:T(8,128)} %bitcast.105), kind=kLoop, calls=%fused_computation.42 | loop fusion | flops 9437184 | bytes 11534336 | tf_op jit(solution)/shard_map/convert_element_type | solution.py:1070
  493.0 2.9 fusion.14
  496.0 1.2 copy-done.16
  497.3 0.8 copy-done.9
  498.1 3.8 convolution_convert_fusion.2
  501.9 0.9 fusion.34
  502.8 3.6 collective-permute-done.2
  506.6 14.5 %attend_far.1 = (bf16[1024,1024]{1,0:T(8,128)(2,1)S(1)}, bf16[1024,1024]{1,0:T(8,128)(2,1)}) custom-call(s32[1]{0:T(128)} %bitcast.14.side_ref, s32[1536,128]{1,0:T(8,128)S(1)} %copy-done.1, s32[8,1536]{1,0:T(8,128)S(1)} %copy-done.5, bf16[1536,3072]{1,0:T(8,128)(2,1)} %add_convert_fusion.q_ref.k_ref.v_ref, ...), custom_call_target="tpu_custom_call" | custom-call | flops 8589934592 | bytes 20971520 | tf_op jit(solution)/shard_map/attend_far/pallas_call | solution.py:366
  521.2 1.4 copy-done.33
  522.8 2.7 copy-done.12
  525.5 9.0 %convolution_convert_fusion.1 = bf16[3072,1024]{0,1:T(8,128)(2,1)} fusion(bf16[1024,3072]{1,0:T(8,128)(2,1)S(1)} %constant_dynamic-update-slice_fusion.grad_ref, bf16[1,1024,1024]{2,1,0:T(8,128)(2,1)S(1)} %copy-done.31), kind=kOutput, calls=%fused_computation.4 | convolution fusion | flops 6445596672 | bytes 14680064 | tf_op jit(solution)/shard_map/dot_general | solution.py:59
  534.6 3.7 reduce.1
  538.4 0.6 reshape.356
  539.0 0.8 pad.19
  539.8 90.8 %finish.1 = (f32[1024,1024]{1,0:T(8,128)}, f32[64,3072]{1,0:T(8,128)}, f32[64,128]{1,0:T(8,128)}, f32[64,1024]{1,0:T(8,128)}) custom-call(f32[1024,1024]{1,0:T(8,128)} %copy-done.15, bf16[1024,3072]{1,0:T(8,128)(2,1)} %copy-done.12, bf16[1024,3072]{1,0:T(8,128)(2,1)} %bitcast.100, bf16[4,2,2,64,3072]{4,3,2,1,0:T(8,128)(2,1)} %bitcast.101, ...), custom_call_target="tpu_custom_call" | custom-call | flops 6442450944 | bytes 31457280 | tf_op jit(solution)/shard_map/finish/pallas_call | solution.py:886
  630.7 3.7 fusion.26
  634.4 0.9 broadcast_in_dim_reshape.3
  635.3 0.9 reshape.359
  636.3 1.0 fusion.28
  637.7 1.3 multiply_reduce_fusion.5
  639.2 5.7 multiply_subtract_fusion
  644.9 0.6 multiply_subtract_fusion.3
  645.5 1.0 multiply_subtract_fusion.2
  646.5 1.7 multiply_subtract_fusion.1
  648.2 2.0 copy.88
  650.2 0.9 copy.89
  651.1 0.7 copy.90
  (168 shorter events, 2.8 us)
Async XLA Ops:
  0.7 7.7 %copy-start.47 = (f32[768]{0:T(1024)S(1)}, f32[768]{0:T(1024)}, u32[]{:S(2)}) copy-start(f32[768]{0:T(1024)} %param.25) | copy-start | bytes 9220
  0.7 67.2 %copy-start.26 = (f32[64,1024]{1,0:T(8,128)S(1)}, f32[64,1024]{1,0:T(8,128)}, u32[]{:S(2)}) copy-start(f32[64,1024]{1,0:T(8,128)} %param.23) | copy-start | bytes 786436
  0.7 68.9 %copy-start.59 = (s32[1,2048]{1,0:T(1,128)S(1)}, s32[1,2048]{1,0:T(1,128)}, u32[]{:S(2)}) copy-start(s32[1,2048]{1,0:T(1,128)} %param.21) | copy-start | bytes 24580
  0.7 69.0 %copy-start.13 = (bf16[1,1024,1024]{2,1,0:T(8,128)(2,1)S(1)}, bf16[1,1024,1024]{2,1,0:T(8,128)(2,1)}, u32[]{:S(2)}) copy-start(bf16[1,1024,1024]{2,1,0:T(8,128)(2,1)} %param.20) | copy-start | bytes 6291460
  3.5 67.2 %collective-permute-start = (bf16[512,1024]{1,0:T(8,128)(2,1)}, bf16[512,1024]{1,0:T(8,128)(2,1)}, u32[]{:S(2)}, u32[]{:S(2)}) collective-permute-start(bf16[512,1024]{1,0:T(8,128)(2,1)} %select_bitcast_fusion), channel_id=1, source_target_pairs={{0,1},{1,0},{2,3},{3,2},{4,5},{5,4},{6,7},{7,6},{8,9},{9,8},{10,11... | collective-permute-start | bytes 3145736 | tf_op jit(solution)/shard_map/ppermute | solution.py:28
  67.2 20.7 %copy-start.39 = (f32[12288]{0:T(1024)}, f32[12288]{0:T(1024)S(1)}, u32[]{:S(2)}) copy-start(f32[12288]{0:T(1024)S(1)} %reshape.360) | copy-start | bytes 147460
  67.3 164.8 %copy-start.42 = (f32[1024]{0:T(1024)}, f32[1024]{0:T(1024)S(1)}, u32[]{:S(2)}) copy-start(f32[1024]{0:T(1024)S(1)} %get-tuple-element.123) | copy-start | bytes 12292
  88.2 78.4 %copy-start = (s32[1536,128]{1,0:T(8,128)}, s32[1536,128]{1,0:T(8,128)S(1)}, u32[]{:S(2)}) copy-start(s32[1536,128]{1,0:T(8,128)S(1)} %broadcast_in_dim.37.ids_col_ref) | copy-start | bytes 2359300
  88.3 78.4 %copy-start.4 = (s32[8,1536]{1,0:T(8,128)}, s32[8,1536]{1,0:T(8,128)S(1)}, u32[]{:S(2)}) copy-start(s32[8,1536]{1,0:T(8,128)S(1)} %broadcast_in_dim.38.ids_row_ref) | copy-start | bytes 147460
  88.3 78.4 %copy-start.30 = (bf16[1,1024,1024]{2,1,0:T(8,128)(2,1)S(1)}, bf16[1,1024,1024]{2,1,0:T(8,128)(2,1)}, u32[]{:S(2)}) copy-start(bf16[1,1024,1024]{2,1,0:T(8,128)(2,1)} %param.19) | copy-start | bytes 6291460
  166.7 2.5 copy-start.2
  166.7 2.5 copy-start.6
  166.7 2.5 copy-start.8
  169.2 62.9 %copy-start.10 = (f32[1024,1024]{1,0:T(8,128)}, f32[1024,1024]{1,0:T(8,128)S(1)}, u32[]{:S(2)}) copy-start(f32[1024,1024]{1,0:T(8,128)S(1)} %get-tuple-element.132) | copy-start | bytes 12582916
  169.2 62.8 %copy-start.40 = (f32[1024]{0:T(1024)}, f32[1024]{0:T(1024)S(1)}, u32[]{:S(2)}) copy-start(f32[1024]{0:T(1024)S(1)} %broadcast_multiply_fusion.1) | copy-start | bytes 12292
  169.8 2.8 copy-start.49
  169.8 62.3 %copy-start.44 = (f32[1024]{0:T(1024)}, f32[1024]{0:T(1024)S(1)}, u32[]{:S(2)}) copy-start(f32[1024]{0:T(1024)S(1)} %fusion.46) | copy-start | bytes 12292
  254.0 7.1 %copy-start.46 = (f32[1024]{0:T(1024)}, f32[1024]{0:T(1024)S(1)}, u32[]{:S(2)}) copy-start(f32[1024]{0:T(1024)S(1)} %negate_multiply_fusion.1) | copy-start | bytes 12292
  261.1 15.3 %copy-start.28 = (bf16[1024,1024]{1,0:T(8,128)(2,1)}, bf16[1024,1024]{1,0:T(8,128)(2,1)S(1)}, u32[]{:S(2)}) copy-start(bf16[1024,1024]{1,0:T(8,128)(2,1)S(1)} %get-tuple-element.92.dz_ref) | copy-start | bytes 6291460
  366.5 6.6 %copy-start.50 = (f32[1024]{0:T(1024)S(1)}, f32[1024]{0:T(1024)}, u32[]{:S(2)}) copy-start(f32[1024]{0:T(1024)} %copy-done.49) | copy-start | bytes 12292
  366.5 6.6 %copy-start.11 = (f32[1024,1024]{1,0:T(8,128)S(1)}, f32[1024,1024]{1,0:T(8,128)}, u32[]{:S(2)}) copy-start(f32[1024,1024]{1,0:T(8,128)} %copy-done.10) | copy-start | bytes 12582916
  366.5 6.6 %copy-start.41 = (f32[1024]{0:T(1024)S(1)}, f32[1024]{0:T(1024)}, u32[]{:S(2)}) copy-start(f32[1024]{0:T(1024)} %copy-done.40) | copy-start | bytes 12292
  366.5 6.6 %copy-start.43 = (f32[1024]{0:T(1024)S(1)}, f32[1024]{0:T(1024)}, u32[]{:S(2)}) copy-start(f32[1024]{0:T(1024)} %copy-done.42) | copy-start | bytes 12292
  366.5 6.6 %copy-start.45 = (f32[1024]{0:T(1024)S(1)}, f32[1024]{0:T(1024)}, u32[]{:S(2)}) copy-start(f32[1024]{0:T(1024)} %copy-done.44) | copy-start | bytes 12292
  375.9 3.0 copy-start.15
  376.5 3.7 copy-start.21
  376.5 3.7 copy-start.51
  378.9 3.6 copy-start.17
  380.2 3.3 copy-start.3
  482.6 24.0 %collective-permute-start.1 = (bf16[512,1024]{1,0:T(8,128)(2,1)}, bf16[512,1024]{1,0:T(8,128)(2,1)S(1)}, u32[]{:S(2)}, u32[]{:S(2)}) collective-permute-start(bf16[512,1024]{1,0:T(8,128)(2,1)} %slice_select_fusion), channel_id=1, source_target_pairs={{0,1},{1,0},{2,3},{3,2},{4,5},{5,4},{6,7},{7,6},{8,9},{9,8},{10,11... | collective-permute-start | bytes 3145736 | tf_op jit(solution)/shard_map/ppermute | solution.py:28
  485.4 20.9 %collective-permute-start.2 = (f32[512,32]{1,0:T(8,128)S(1)}, f32[512,32]{1,0:T(8,128)S(1)}, u32[]{:S(2)}, u32[]{:S(2)}) collective-permute-start(f32[512,32]{1,0:T(8,128)S(1)} %pad_maximum_fusion.2), channel_id=1, source_target_pairs={{0,1},{1,0},{2,3},{3,2},{4,5},{5,4},{6,7},{7,6},{8,9},{9,8},{10,11... | collective-permute-start | bytes 196616 | tf_op jit(solution)/shard_map/ppermute | solution.py:28
  486.1 6.8 %copy-start.18 = (f32[1,2,64,4096]{3,2,1,0:T(8,128)S(1)}, f32[1,2,64,4096]{3,2,1,0:T(8,128)}, u32[]{:S(2)}) copy-start(f32[1,2,64,4096]{3,2,1,0:T(8,128)} %param.32) | copy-start | bytes 6291460
  486.1 6.8 %copy-start.19 = (f32[1,2,64,4096]{3,2,1,0:T(8,128)S(1)}, f32[1,2,64,4096]{3,2,1,0:T(8,128)}, u32[]{:S(2)}) copy-start(f32[1,2,64,4096]{3,2,1,0:T(8,128)} %param.28) | copy-start | bytes 6291460
  486.1 6.8 %copy-start.23 = (f32[64,4096]{1,0:T(8,128)S(1)}, f32[64,4096]{1,0:T(8,128)}, u32[]{:S(2)}) copy-start(f32[64,4096]{1,0:T(8,128)} %get-tuple-element.72) | copy-start | bytes 3145732
  486.1 6.8 %copy-start.24 = (f32[64,4096]{1,0:T(8,128)S(1)}, f32[64,4096]{1,0:T(8,128)}, u32[]{:S(2)}) copy-start(f32[64,4096]{1,0:T(8,128)} %get-tuple-element.71) | copy-start | bytes 3145732
  492.9 146.3 %collective-permute-start.5 = (bf16[2,64,4096]{2,1,0:T(8,128)(2,1)}, bf16[2,64,4096]{2,1,0:T(8,128)(2,1)}, u32[]{:S(2)}, u32[]{:S(2)}) collective-permute-start(bf16[2,64,4096]{2,1,0:T(8,128)(2,1)} %get-tuple-element.101), channel_id=1, source_target_pairs={{0,16},{16,0},{1,17},{17,1},{2,18},{18,2},{3,19},{19,3},{4,20},{20... | collective-permute-start | bytes 3145736 | tf_op jit(solution)/shard_map/ppermute | solution.py:28
  492.9 2.9 copy-start.32
  492.9 4.3 copy-start.16
  498.1 8.5 %copy-start.1 = (s32[1536,128]{1,0:T(8,128)S(1)}, s32[1536,128]{1,0:T(8,128)}, u32[]{:S(2)}) copy-start(s32[1536,128]{1,0:T(8,128)} %copy-done) | copy-start | bytes 2359300
  498.1 8.5 %copy-start.5 = (s32[8,1536]{1,0:T(8,128)S(1)}, s32[8,1536]{1,0:T(8,128)}, u32[]{:S(2)}) copy-start(s32[8,1536]{1,0:T(8,128)} %copy-done.4) | copy-start | bytes 147460
  521.1 4.4 copy-start.31
  522.8 2.7 copy-start.12
  534.5 3.8 copy-start.57
  534.5 3.8 copy-start.53
  534.5 3.8 copy-start.56
  534.5 3.8 copy-start.55
  534.5 3.9 copy-start.54
  534.5 3.9 copy-start.58
  630.6 5.6 copy-start.27
  630.6 5.6 copy-start.34
  630.6 5.6 copy-start.36
  630.6 5.6 copy-start.37
  630.6 7.1 %copy-start.61 = (f32[1,768]{1,0:T(1,128)S(1)}, f32[1,768]{1,0:T(1,128)}, u32[]{:S(2)}) copy-start(f32[1,768]{1,0:T(1,128)} %param.29) | copy-start | bytes 9220
  630.7 8.4 %copy-start.48 = (f32[768]{0:T(1024)S(1)}, f32[768]{0:T(1024)}, u32[]{:S(2)}) copy-start(f32[768]{0:T(1024)} %param.25) | copy-start | bytes 9220
  630.7 8.5 %copy-start.14 = (f32[2,64,4096]{2,1,0:T(8,128)S(1)}, f32[2,64,4096]{2,1,0:T(8,128)}, u32[]{:S(2)}) copy-start(f32[2,64,4096]{2,1,0:T(8,128)} %param.24) | copy-start | bytes 6291460
  635.3 9.6 %copy-start.52 = (f32[1,768]{1,0:T(1,128)}, f32[1,768]{1,0:T(1,128)S(1)}, u32[]{:S(2)}) copy-start(f32[1,768]{1,0:T(1,128)S(1)} %broadcast_in_dim_reshape.3) | copy-start | bytes 9220
  636.2 10.3 %collective-permute-start.3 = (bf16[64,3072]{1,0:T(8,128)(2,1)S(1)}, bf16[64,3072]{1,0:T(8,128)(2,1)S(1)}, u32[]{:S(2)}, u32[]{:S(2)}) collective-permute-start(bf16[64,3072]{1,0:T(8,128)(2,1)S(1)} %get-tuple-element.105), channel_id=1, source_target_pairs={{0,16},{16,0},{1,17},{17,1},{2,18},{18,2},{3,19},{19,3},{4,20},{20... | collective-permute-start | bytes 1179656 | tf_op jit(solution)/shard_map/ppermute | solution.py:28
  637.3 8.3 %collective-permute-start.4 = (bf16[64,1024]{1,0:T(8,128)(2,1)S(1)}, bf16[64,1024]{1,0:T(8,128)(2,1)S(1)}, u32[]{:S(2)}, u32[]{:S(2)}) collective-permute-start(bf16[64,1024]{1,0:T(8,128)(2,1)S(1)} %get-tuple-element.110), channel_id=1, source_target_pairs={{0,16},{16,0},{1,17},{17,1},{2,18},{18,2},{3,19},{19,3},{4,20},{20... | collective-permute-start | bytes 393224 | tf_op jit(solution)/shard_map/ppermute | solution.py:28
  639.0 5.9 copy-start.60
  639.1 6.5 copy-start.38
  639.1 7.4 %copy-start.20 = (f32[64,3072]{1,0:T(8,128)S(1)}, f32[64,3072]{1,0:T(8,128)}, u32[]{:S(2)}) copy-start(f32[64,3072]{1,0:T(8,128)} %param.22) | copy-start | bytes 2359300
  639.1 7.4 %copy-start.35 = (f32[64,3072]{1,0:T(8,128)S(1)}, f32[64,3072]{1,0:T(8,128)}, u32[]{:S(2)}) copy-start(f32[64,3072]{1,0:T(8,128)} %param.34) | copy-start | bytes 2359300
  639.1 5.8 collective-permute-start.6
  644.9 3.3 copy-start.22
  (6 other events, 11.3 us)

commit v5 on v4

--- a/solution.py
+++ b/solution.py
@@ -398,7 +398,7 @@
 AXES = ("z", "x", "y")
 GATHER_ORDERS = ((("z", "x", "y"), 3), (("z", "y", "x"), 3), (("x", "y", "z"), 2))
 SCATTER_ORDERS = ((("y", "x", "z"), 3), (("x", "y", "z"), 3), (("z", "y", "x"), 2))
-PIECE = 512
+PIECE = 1024
 
 
 def axis_parts():
@@ -795,8 +795,9 @@
     return [*got[:2], *[w.reshape(-1, w.shape[-1]) for w in got[2:]]]
 
 
-def ffn_back_kernel(widths, dz_ref, down_ref, slope_ref, turned_ref, up_ref, *refs):
+def ffn_back_kernel(widths, dz_ref, down_ref, slope_ref, x_ref, up_ref, *refs):
     count = len(widths)
+    turned_ref, *refs = refs[2 * count + 3], *refs[: 2 * count + 3], *refs[2 * count + 4 :]
     up_grad_ref, bias_ref, total_ref = refs[count : count + 3]
     sums = refs[count + 3 : 2 * count + 3]
     work = scatter_steps(widths, refs[:count], sums, *refs[2 * count + 3 :])
@@ -806,6 +807,9 @@
     @pl.when(now == 0)
     def _():
         total_ref[...] = jnp.zeros_like(total_ref)
+        for begin in range(0, x_ref.shape[0], TILE):
+            block = slice(begin, begin + TILE)
+            turned_ref[:, block] = jnp.transpose(x_ref[block, :].astype(jnp.float32)).astype(jnp.bfloat16)
 
     inner = (dot_nn(dz_ref[...], down_ref[...]) * slope_ref[...].astype(jnp.float32)).astype(jnp.bfloat16)
     column = jnp.sum(inner.astype(jnp.float32), axis=0, keepdims=True)
@@ -819,7 +823,7 @@
             step()
 
 
-def ffn_back(dz, weight_down, slope, turned, weight_up, partials):
+def ffn_back(dz, weight_down, slope, x, weight_up, partials):
     rows, depth = dz.shape
     width = weight_up.shape[1]
     tile = width // 16
@@ -835,7 +839,7 @@
             whole,
             pl.BlockSpec((depth, tile), lambda i: (0, i)),
             pl.BlockSpec((rows, tile), lambda i: (0, i)),
-            pl.BlockSpec((depth, rows), lambda i: (0, 0)),
+            whole,
             pl.BlockSpec((depth, tile), lambda i: (0, i)),
             *[pl.BlockSpec(memory_space=pl.ANY) for _ in widths],
         ],
@@ -851,14 +855,14 @@
             jax.ShapeDtypeStruct((rows, depth), jnp.float32),
             *[jax.ShapeDtypeStruct((shard_rows, w), jnp.float32) for w in widths],
         ],
-        scratch_shapes=scatter_scratch(widths, shard_rows),
+        scratch_shapes=[pltpu.VMEM((depth, rows), jnp.bfloat16), *scatter_scratch(widths, shard_rows)],
         compiler_params=pltpu.CompilerParams(
             vmem_limit_bytes=67043328, collective_id=5, has_side_effects=True
         ),
         cost_estimate=pl.CostEstimate(
             flops=6 * rows * depth * width, bytes_accessed=60 << 20, transcendentals=0
         ),
-    )(dz, weight_down, slope, turned, weight_up, *operands)
+    )(dz, weight_down, slope, x, weight_up, *operands)
 
 
 def finish_kernel(widths, base_ref, grad_ref, weight_ref, *refs):
@@ -999,7 +1003,7 @@
     bias_second_grad = jnp.sum(branch_two_low.astype(jnp.float32), axis=0)
     down_grad = dot_tn(branch_two_low, activated_low).astype(jnp.bfloat16)
     up_grad, bias_rows, hidden_total, down_sum = ffn_back(
-        branch_two_low, full_down, slope, jnp.transpose(hidden_low), full_up, [down_grad]
+        branch_two_low, full_down, slope, hidden_low, full_up, [down_grad]
     )
     bias_hidden_grad = bias_rows[0]
     hidden_grad = residue_second_grad + hidden_total

time: 656 us -> 639 us (0.974)
  Pallas kernels: 488 us -> 477 us
    pallas_call x1, Pallas kernels: 90.8 us -> 82.4 us  [finish(): pl.pallas_call(partial(finish_kernel, widths), name='finish', grid=(16,),...]
  transfers between devices with their start and end apart: 7 -> 7, of which waited for: 1 -> 1; matrix products, arithmetic and copies ran while one was open for 8% -> 8% of each run, Pallas kernels for 25% -> 24%
where the time goes in v5:
time: 639 us; the launch traced here: 630 us
  Pallas kernels  477 us (75%)
  matrix products  62.7 us (10%)
  other arithmetic  58.2 us (9%)
  local copies, waits for them, and re-layouts  20.7 us (3%)
    pallas_call x1, Pallas kernels, attend_back(): pl.pallas_call(partial(attend_back_kernel, widths), name='attend_back', g...  99.5 us
    pallas_call x1, Pallas kernels, ffn_back(): pl.pallas_call(partial(ffn_back_kernel, widths), name='ffn_back', grid=(1...  91.5 us
    pallas_call x1, Pallas kernels, finish(): pl.pallas_call(partial(finish_kernel, widths), name='finish', grid=(16,),...  82.4 us
    pallas_call x1, Pallas kernels, attend(): pl.pallas_call(partial(attend_kernel, shared), name='attend', grid_spec=p...  79.2 us
    pallas_call x1, Pallas kernels, ffn_up(): pl.pallas_call(partial(ffn_up_kernel, shared), name='ffn_up', grid=(16,),...  56.1 us
    pallas_call x1, Pallas kernels, gather_all(): pl.pallas_call(partial(gather_kernel, shared), name='gather_all', in_spec...  53.5 us
    dot_general x3, matrix products, dot_tn(): lax.dot_general(a, b, (((0,), (0,)), ((), ())), preferred_element_type=jn...  24 us
    dot_general x1, matrix products, on_device(): jnp.dot(wide_tokens, full_qkv, preferred_element_type=jnp.float32)  17.1 us
  transfers between devices with their start and end apart: 7, of which 1 were waited for; matrix products, arithmetic and copies ran while one was open for 8% of the time, Pallas kernels for 24%

profile of v5, /device:TPU:0, one launch (start us, length us, event | category | flops | bytes accessed | tf_op | source)
XLA Modules:
  0.0 629.7 jit_solution(12727230154990747857)
XLA Ops:
  0.7 2.8 select_bitcast_fusion
  3.5 3.0 collective-permute-start
  6.5 1.9 convert_element_type.115.refs_0_
  8.5 0.6 pad.16.refs_1_
  9.2 53.5 %gather_all.1 = (bf16[4,2,2,64,3072]{4,3,2,1,0:T(8,128)(2,1)}, bf16[4,2,2,64,128]{4,3,2,1,0:T(8,128)(2,1)}) custom-call(bf16[64,3072]{1,0:T(8,128)(2,1)} %convert_element_type.115.refs_0_, bf16[64,128]{1,0:T(8,128)(2,1)} %pad.16.refs_1_), custom_call_target="tpu_custom_call" | custom-call | tf_op jit(solution)/shard_map/gather_all/pallas_call | solution.py:568
  62.7 1.0 slice_convert_fusion
  64.1 0.6 add_select_fusion
  64.7 1.7 convert_element_type.121
  66.5 1.0 reduce.4
  67.5 17.1 %add_convert_fusion.q_ref.k_ref.v_ref = bf16[1536,3072]{1,0:T(8,128)(2,1)} fusion(bf16[1024,3072]{1,0:T(8,128)(2,1)} %bitcast.97, f32[3072]{0:T(1024)S(1)} %pad_maximum_fusion.3, bf16[512,1024]{1,0:T(8,128)(2,1)} %collective-permute-done, bf16[1024,1024]{1,0:T(8,128)(2,1)} %bitcast.107, pred[]{:T(512)S(6)} %eq.16), kind=kOutput, calls=%fused_computation | convolution fusion | flops 9687269376 | bytes 18886656 | tf_op jit(solution)/shard_map/dot_general | solution.py:979
  84.9 79.2 %attend.1 = (bf16[1024,1024]{1,0:T(8,128)(2,1)S(1)}, f32[1024,1024]{1,0:T(8,128)}, f32[1024,128]{1,0:T(8,128)S(1)}, bf16[4,2,2,64,1024]{4,3,2,1,0:T(8,128)(2,1)S(1)}, bf16[4,2,2,64,4096]{4,3,2,1,0:T(8,128)(2,1)}) custom-call(s32[1536,128]{1,0:T(8,128)S(1)} %broadcast_in_dim.37.ids_col_ref, s32[8,1536]{1,0:T(8,128)S(1)} %broadcast_in_dim.38.ids_row_ref, ...), custom_call_target="tpu_custom_call" | custom-call | flops 18253611008 | bytes 31457280 | tf_op jit(solution)/shard_map/attend/pallas_call | solution.py:152
  164.1 2.5 fusion.60
  166.6 0.5 multiply_reduce_fusion.3
  167.2 0.7 fusion.7.x_ref
  168.0 56.1 %ffn_up.1 = (bf16[1024,4096]{1,0:T(8,128)(2,1)}, bf16[1024,4096]{1,0:T(8,128)(2,1)}, bf16[4,2,2,64,4096]{4,3,2,1,0:T(8,128)(2,1)}) custom-call(bf16[1024,1024]{1,0:T(8,128)(2,1)S(1)} %fusion.7.x_ref, bf16[1024,4096]{1,0:T(8,128)(2,1)} %bitcast.113, f32[8,4096]{1,0:T(8,128)S(1)} %broadcast_in_dim.40.bias_ref, bf16[64,4096]{1,0:T(8,128)(2,1)S(1)} %get-tuple-element.108.refs_0_), custom_call_target="tpu_custom_call" | custom-call | flops 8589934592 | bytes 41943040 | tf_op jit(solution)/shard_map/ffn_up/pallas_call | solution.py:767
  224.2 14.4 %fusion.61 = (f32[1024]{0:T(1024)S(1)}, f32[1024,1024]{1,0:T(8,128)S(1)}) fusion(f32[1024]{0:T(1024)S(1)} %get-tuple-element.121, bf16[1024,4096]{1,0:T(8,128)(2,1)} %get-tuple-element.55, bf16[1024,4096]{1,0:T(8,128)(2,1)} %bitcast.116, f32[1024]{0:T(1024)S(1)} %get-tuple-element.122, f32[1024]{0:T(1024)S(1)} %get-tuple-element.123, ...), kind=kOutput, calls=%fused_computation.150 | convolution fusion | flops 8597273600 | bytes 25190400 | tf_op jit(solution)/shard_map/dot_general | solution.py:993
  238.7 0.5 multiply_reduce_fusion.2
  239.2 2.5 fusion.3
  241.8 3.5 fusion.55
  245.4 2.0 copy-done.13
  247.3 1.0 fusion.53
  248.3 11.2 %convolution_convert_fusion = bf16[1024,4096]{1,0:T(8,128)(2,1)} fusion(bf16[1024,1024]{1,0:T(8,128)(2,1)S(1)} %get-tuple-element.92.dz_ref, bf16[1024,4096]{1,0:T(8,128)(2,1)S(1)} %bitcast.120), kind=kOutput, calls=%fused_computation.1 | convolution fusion | flops 8594128896 | bytes 18874368 | tf_op jit(solution)/shard_map/dot_general | solution.py:59
  259.5 91.5 %ffn_back.1 = (bf16[1024,4096]{1,0:T(8,128)(2,1)}, f32[8,4096]{1,0:T(8,128)}, f32[1024,1024]{1,0:T(8,128)}, f32[64,4096]{1,0:T(8,128)}) custom-call(bf16[1024,1024]{1,0:T(8,128)(2,1)} %copy-done.30, bf16[1024,4096]{1,0:T(8,128)(2,1)} %bitcast.117, bf16[1024,4096]{1,0:T(8,128)(2,1)} %get-tuple-element.57.slope_ref, bf16[1024,1024]{1,0:T(8,128)(2,1)} %copy-done.2, ...), custom_call_target="tpu_custom_call" | custom-call | flops 25769803776 | bytes 62914560 | tf_op jit(solution)/shard_map/ffn_back/pallas_call | solution.py:834
  351.1 6.4 %multiply_reduce_fusion = (bf16[1024]{0:T(1024)(128)(2,1)}, f32[1024]{0:T(1024)S(1)}, bf16[1024]{0:T(1024)(128)(2,1)}, f32[1024,1024]{1,0:T(8,128)S(1)}) fusion(f32[1024,1024]{1,0:T(8,128)} %copy-done.11, f32[1024]{0:T(1024)} %copy-done.46, f32[1024]{0:T(1024)} %copy-done.42, f32[1024]{0:T(1024)} %copy-done.44, f32[1024,1024]{1,0:T(8,128)} %get-tuple-element.58, ...), kind=kLoop, calls=%fused_computation.11 | loop fusion | flops 10482688 | bytes 16801792 | tf_op jit(solution)/shard_map/transpose(jvp())/reduce_sum | solution.py:35
  357.6 1.9 fusion.54
  359.5 1.0 convert_reduce_fusion
  360.5 0.6 copy-done.8
  361.1 2.4 convolution_convert_fusion.3.do_ref
  363.5 1.2 slice_select_fusion
  364.7 2.3 fusion.4.inner_ref
  367.1 1.0 fusion.57
  368.1 0.8 fusion.56
  368.9 99.5 %attend_back.1 = (bf16[1024,1024]{1,0:T(8,128)(2,1)}, f32[1024,1024]{1,0:T(8,128)}, f32[1024,1024]{1,0:T(8,128)}, f32[64,4096]{1,0:T(8,128)}) custom-call(s32[1536,128]{1,0:T(8,128)} %copy-done, s32[8,1536]{1,0:T(8,128)} %copy-done.5, bf16[1536,3072]{1,0:T(8,128)(2,1)} %add_convert_fusion.q_ref.k_ref.v_ref, ...), custom_call_target="tpu_custom_call" | custom-call | flops 45634027520 | bytes 41943040 | tf_op jit(solution)/shard_map/attend_back/pallas_call | solution.py:275
  468.4 0.5 collective-permute-start.1
  468.9 1.2 slice_select_fusion.1
  470.2 1.7 collective-permute-start.2
  471.9 6.8 %fusion.21 = (bf16[2,64,4096]{2,1,0:T(8,128)(2,1)}, f32[1,2,64,4096]{3,2,1,0:T(8,128)}) fusion(f32[2,64,4096]{2,1,0:T(8,128)} %param.24, f32[1,2,64,4096]{3,2,1,0:T(8,128)} %param.32, f32[1,2,64,4096]{3,2,1,0:T(8,128)} %param.28, f32[1,64,4096]{2,1,0:T(8,128)} %bitcast.101, f32[1,64,4096]{2,1,0:T(8,128)} %bitcast.103), kind=kLoop, calls=%fused_computation.42 | loop fusion | flops 9437184 | bytes 11534336 | tf_op jit(solution)/shard_map/convert_element_type | solution.py:1074
  478.8 2.9 fusion.14
  481.9 1.2 copy-done.18
  483.1 0.8 copy-done.10
  483.9 3.8 convolution_convert_fusion.2
  487.7 0.9 fusion.34
  488.7 3.5 collective-permute-done.2
  492.4 14.5 %attend_far.1 = (bf16[1024,1024]{1,0:T(8,128)(2,1)S(1)}, bf16[1024,1024]{1,0:T(8,128)(2,1)}) custom-call(s32[1]{0:T(128)} %bitcast.13.side_ref, s32[1536,128]{1,0:T(8,128)S(1)} %copy-done.1, s32[8,1536]{1,0:T(8,128)S(1)} %copy-done.6, bf16[1536,3072]{1,0:T(8,128)(2,1)} %add_convert_fusion.q_ref.k_ref.v_ref, ...), custom_call_target="tpu_custom_call" | custom-call | flops 8589934592 | bytes 20971520 | tf_op jit(solution)/shard_map/attend_far/pallas_call | solution.py:366
  507.1 1.4 copy-done.35
  508.7 2.7 copy-done.14
  511.3 9.0 %convolution_convert_fusion.1 = bf16[3072,1024]{0,1:T(8,128)(2,1)} fusion(bf16[1024,3072]{1,0:T(8,128)(2,1)S(1)} %constant_dynamic-update-slice_fusion.grad_ref, bf16[1,1024,1024]{2,1,0:T(8,128)(2,1)S(1)} %copy-done.33), kind=kOutput, calls=%fused_computation.4 | convolution fusion | flops 6445596672 | bytes 14680064 | tf_op jit(solution)/shard_map/dot_general | solution.py:59
  520.4 3.7 reduce.1
  524.3 0.6 reshape.356
  524.9 0.8 pad.19
  525.7 82.4 %finish.1 = (f32[1024,1024]{1,0:T(8,128)}, f32[64,3072]{1,0:T(8,128)}, f32[64,128]{1,0:T(8,128)}, f32[64,1024]{1,0:T(8,128)}) custom-call(f32[1024,1024]{1,0:T(8,128)} %copy-done.17, bf16[1024,3072]{1,0:T(8,128)(2,1)} %copy-done.14, bf16[1024,3072]{1,0:T(8,128)(2,1)} %bitcast.98, bf16[4,2,2,64,3072]{4,3,2,1,0:T(8,128)(2,1)} %bitcast.99, ...), custom_call_target="tpu_custom_call" | custom-call | flops 6442450944 | bytes 31457280 | tf_op jit(solution)/shard_map/finish/pallas_call | solution.py:890
  608.2 3.7 fusion.26
  611.9 0.9 broadcast_in_dim_reshape.3
  612.8 0.9 reshape.359
  613.8 1.0 fusion.28
  614.8 0.5 collective-permute-start.4
  615.2 1.3 multiply_reduce_fusion.5
  616.7 5.7 multiply_subtract_fusion
  622.4 0.6 multiply_subtract_fusion.3
  623.0 1.0 multiply_subtract_fusion.2
  624.0 1.7 multiply_subtract_fusion.1
  625.7 2.0 copy.84
  627.7 0.9 copy.85
  628.6 0.7 copy.86
  (175 shorter events, 2.4 us)
Async XLA Ops:
  0.7 7.7 %copy-start.49 = (f32[768]{0:T(1024)S(1)}, f32[768]{0:T(1024)}, u32[]{:S(2)}) copy-start(f32[768]{0:T(1024)} %param.25) | copy-start | bytes 9220
  0.7 64.0 %copy-start.28 = (f32[64,1024]{1,0:T(8,128)S(1)}, f32[64,1024]{1,0:T(8,128)}, u32[]{:S(2)}) copy-start(f32[64,1024]{1,0:T(8,128)} %param.23) | copy-start | bytes 786436
  0.7 65.7 %copy-start.61 = (s32[1,2048]{1,0:T(1,128)S(1)}, s32[1,2048]{1,0:T(1,128)}, u32[]{:S(2)}) copy-start(s32[1,2048]{1,0:T(1,128)} %param.21) | copy-start | bytes 24580
  0.7 65.7 %copy-start.15 = (bf16[1,1024,1024]{2,1,0:T(8,128)(2,1)S(1)}, bf16[1,1024,1024]{2,1,0:T(8,128)(2,1)}, u32[]{:S(2)}) copy-start(bf16[1,1024,1024]{2,1,0:T(8,128)(2,1)} %param.20) | copy-start | bytes 6291460
  3.5 64.0 %collective-permute-start = (bf16[512,1024]{1,0:T(8,128)(2,1)}, bf16[512,1024]{1,0:T(8,128)(2,1)}, u32[]{:S(2)}, u32[]{:S(2)}) collective-permute-start(bf16[512,1024]{1,0:T(8,128)(2,1)} %select_bitcast_fusion), channel_id=1, source_target_pairs={{0,1},{1,0},{2,3},{3,2},{4,5},{5,4},{6,7},{7,6},{8,9},{9,8},{10,11... | collective-permute-start | bytes 3145736 | tf_op jit(solution)/shard_map/ppermute | solution.py:28
  64.0 20.5 %copy-start.41 = (f32[12288]{0:T(1024)}, f32[12288]{0:T(1024)S(1)}, u32[]{:S(2)}) copy-start(f32[12288]{0:T(1024)S(1)} %reshape.360) | copy-start | bytes 147460
  64.0 160.1 %copy-start.44 = (f32[1024]{0:T(1024)}, f32[1024]{0:T(1024)S(1)}, u32[]{:S(2)}) copy-start(f32[1024]{0:T(1024)S(1)} %get-tuple-element.123) | copy-start | bytes 12292
  84.8 79.2 %copy-start = (s32[1536,128]{1,0:T(8,128)}, s32[1536,128]{1,0:T(8,128)S(1)}, u32[]{:S(2)}) copy-start(s32[1536,128]{1,0:T(8,128)S(1)} %broadcast_in_dim.37.ids_col_ref) | copy-start | bytes 2359300
  84.8 79.2 %copy-start.5 = (s32[8,1536]{1,0:T(8,128)}, s32[8,1536]{1,0:T(8,128)S(1)}, u32[]{:S(2)}) copy-start(s32[8,1536]{1,0:T(8,128)S(1)} %broadcast_in_dim.38.ids_row_ref) | copy-start | bytes 147460
  84.9 79.2 %copy-start.32 = (bf16[1,1024,1024]{2,1,0:T(8,128)(2,1)S(1)}, bf16[1,1024,1024]{2,1,0:T(8,128)(2,1)}, u32[]{:S(2)}) copy-start(bf16[1,1024,1024]{2,1,0:T(8,128)(2,1)} %param.19) | copy-start | bytes 6291460
  166.6 57.6 %copy-start.11 = (f32[1024,1024]{1,0:T(8,128)}, f32[1024,1024]{1,0:T(8,128)S(1)}, u32[]{:S(2)}) copy-start(f32[1024,1024]{1,0:T(8,128)S(1)} %get-tuple-element.132) | copy-start | bytes 12582916
  166.6 57.6 %copy-start.42 = (f32[1024]{0:T(1024)}, f32[1024]{0:T(1024)S(1)}, u32[]{:S(2)}) copy-start(f32[1024]{0:T(1024)S(1)} %broadcast_multiply_fusion.1) | copy-start | bytes 12292
  167.2 57.0 %copy-start.51 = (f32[1024]{0:T(1024)}, f32[1024]{0:T(1024)S(1)}, u32[]{:S(2)}) copy-start(f32[1024]{0:T(1024)S(1)} %multiply_reduce_fusion.3) | copy-start | bytes 12292
  167.2 57.0 %copy-start.46 = (f32[1024]{0:T(1024)}, f32[1024]{0:T(1024)S(1)}, u32[]{:S(2)}) copy-start(f32[1024]{0:T(1024)S(1)} %fusion.46) | copy-start | bytes 12292
  168.0 56.2 %copy-start.2 = (bf16[1024,1024]{1,0:T(8,128)(2,1)}, bf16[1024,1024]{1,0:T(8,128)(2,1)S(1)}, u32[]{:S(2)}) copy-start(bf16[1024,1024]{1,0:T(8,128)(2,1)S(1)} %fusion.7.x_ref) | copy-start | bytes 6291460
  241.8 6.5 %slice-start.1 = ((s8[8388608]{0:T(1024)(128)(4,1)}), s8[4194304]{0:T(1024)(128)(4,1)S(1)}, s32[]{:S(2)}) async-start(s8[8388608]{0:T(1024)(128)(4,1)} %bitcast.119), calls=%async_computation.1 | async-start | bytes 8388608
  241.8 6.5 %slice-start.2 = ((s8[8388608]{0:T(1024)(128)(4,1)}), s8[4194304]{0:T(1024)(128)(4,1)S(1)}, s32[]{:S(2)}) async-start(s8[8388608]{0:T(1024)(128)(4,1)} %bitcast.119), calls=%async_computation.2 | async-start | bytes 8388608
  245.4 3.0 copy-start.48
  248.3 11.2 %copy-start.30 = (bf16[1024,1024]{1,0:T(8,128)(2,1)}, bf16[1024,1024]{1,0:T(8,128)(2,1)S(1)}, u32[]{:S(2)}) copy-start(bf16[1024,1024]{1,0:T(8,128)(2,1)S(1)} %get-tuple-element.92.dz_ref) | copy-start | bytes 6291460
  351.1 6.5 %copy-start.52 = (f32[1024]{0:T(1024)S(1)}, f32[1024]{0:T(1024)}, u32[]{:S(2)}) copy-start(f32[1024]{0:T(1024)} %copy-done.51) | copy-start | bytes 12292
  351.1 6.5 %copy-start.12 = (f32[1024,1024]{1,0:T(8,128)S(1)}, f32[1024,1024]{1,0:T(8,128)}, u32[]{:S(2)}) copy-start(f32[1024,1024]{1,0:T(8,128)} %copy-done.11) | copy-start | bytes 12582916
  351.1 6.5 %copy-start.43 = (f32[1024]{0:T(1024)S(1)}, f32[1024]{0:T(1024)}, u32[]{:S(2)}) copy-start(f32[1024]{0:T(1024)} %copy-done.42) | copy-start | bytes 12292
  351.1 6.5 %copy-start.45 = (f32[1024]{0:T(1024)S(1)}, f32[1024]{0:T(1024)}, u32[]{:S(2)}) copy-start(f32[1024]{0:T(1024)} %copy-done.44) | copy-start | bytes 12292
  351.1 6.5 %copy-start.47 = (f32[1024]{0:T(1024)S(1)}, f32[1024]{0:T(1024)}, u32[]{:S(2)}) copy-start(f32[1024]{0:T(1024)} %copy-done.46) | copy-start | bytes 12292
  360.5 3.0 copy-start.17
  361.1 3.6 copy-start.23
  361.1 3.6 copy-start.53
  363.5 3.6 copy-start.19
  364.7 3.3 copy-start.4
  468.4 24.0 %collective-permute-start.1 = (bf16[512,1024]{1,0:T(8,128)(2,1)}, bf16[512,1024]{1,0:T(8,128)(2,1)S(1)}, u32[]{:S(2)}, u32[]{:S(2)}) collective-permute-start(bf16[512,1024]{1,0:T(8,128)(2,1)} %slice_select_fusion), channel_id=1, source_target_pairs={{0,1},{1,0},{2,3},{3,2},{4,5},{5,4},{6,7},{7,6},{8,9},{9,8},{10,11... | collective-permute-start | bytes 3145736 | tf_op jit(solution)/shard_map/ppermute | solution.py:28
  470.2 22.0 %collective-permute-start.2 = (f32[512,32]{1,0:T(8,128)S(1)}, f32[512,32]{1,0:T(8,128)S(1)}, u32[]{:S(2)}, u32[]{:S(2)}) collective-permute-start(f32[512,32]{1,0:T(8,128)S(1)} %pad_maximum_fusion.2), channel_id=1, source_target_pairs={{0,1},{1,0},{2,3},{3,2},{4,5},{5,4},{6,7},{7,6},{8,9},{9,8},{10,11... | collective-permute-start | bytes 196616 | tf_op jit(solution)/shard_map/ppermute | solution.py:28
  471.9 6.8 %copy-start.20 = (f32[1,2,64,4096]{3,2,1,0:T(8,128)S(1)}, f32[1,2,64,4096]{3,2,1,0:T(8,128)}, u32[]{:S(2)}) copy-start(f32[1,2,64,4096]{3,2,1,0:T(8,128)} %param.32) | copy-start | bytes 6291460
  471.9 6.8 %copy-start.21 = (f32[1,2,64,4096]{3,2,1,0:T(8,128)S(1)}, f32[1,2,64,4096]{3,2,1,0:T(8,128)}, u32[]{:S(2)}) copy-start(f32[1,2,64,4096]{3,2,1,0:T(8,128)} %param.28) | copy-start | bytes 6291460
  471.9 6.8 %copy-start.25 = (f32[64,4096]{1,0:T(8,128)S(1)}, f32[64,4096]{1,0:T(8,128)}, u32[]{:S(2)}) copy-start(f32[64,4096]{1,0:T(8,128)} %get-tuple-element.72) | copy-start | bytes 3145732
  471.9 6.8 %copy-start.26 = (f32[64,4096]{1,0:T(8,128)S(1)}, f32[64,4096]{1,0:T(8,128)}, u32[]{:S(2)}) copy-start(f32[64,4096]{1,0:T(8,128)} %get-tuple-element.71) | copy-start | bytes 3145732
  478.7 138.0 %collective-permute-start.5 = (bf16[2,64,4096]{2,1,0:T(8,128)(2,1)}, bf16[2,64,4096]{2,1,0:T(8,128)(2,1)}, u32[]{:S(2)}, u32[]{:S(2)}) collective-permute-start(bf16[2,64,4096]{2,1,0:T(8,128)(2,1)} %get-tuple-element.101), channel_id=1, source_target_pairs={{0,16},{16,0},{1,17},{17,1},{2,18},{18,2},{3,19},{19,3},{4,20},{20... | collective-permute-start | bytes 3145736 | tf_op jit(solution)/shard_map/ppermute | solution.py:28
  478.8 2.9 copy-start.34
  478.8 4.3 copy-start.18
  483.9 8.5 %copy-start.1 = (s32[1536,128]{1,0:T(8,128)S(1)}, s32[1536,128]{1,0:T(8,128)}, u32[]{:S(2)}) copy-start(s32[1536,128]{1,0:T(8,128)} %copy-done) | copy-start | bytes 2359300
  483.9 8.5 %copy-start.6 = (s32[8,1536]{1,0:T(8,128)S(1)}, s32[8,1536]{1,0:T(8,128)}, u32[]{:S(2)}) copy-start(s32[8,1536]{1,0:T(8,128)} %copy-done.5) | copy-start | bytes 147460
  506.9 4.5 copy-start.33
  508.7 2.7 copy-start.14
  520.4 3.8 copy-start.59
  520.4 3.8 copy-start.55
  520.4 3.8 copy-start.58
  520.4 3.8 copy-start.57
  520.4 3.9 copy-start.56
  520.4 3.9 copy-start.60
  608.1 5.6 copy-start.29
  608.1 5.6 copy-start.36
  608.1 5.6 copy-start.38
  608.1 5.6 copy-start.39
  608.1 7.1 %copy-start.63 = (f32[1,768]{1,0:T(1,128)S(1)}, f32[1,768]{1,0:T(1,128)}, u32[]{:S(2)}) copy-start(f32[1,768]{1,0:T(1,128)} %param.29) | copy-start | bytes 9220
  608.2 8.4 %copy-start.50 = (f32[768]{0:T(1024)S(1)}, f32[768]{0:T(1024)}, u32[]{:S(2)}) copy-start(f32[768]{0:T(1024)} %param.25) | copy-start | bytes 9220
  608.2 8.5 %copy-start.16 = (f32[2,64,4096]{2,1,0:T(8,128)S(1)}, f32[2,64,4096]{2,1,0:T(8,128)}, u32[]{:S(2)}) copy-start(f32[2,64,4096]{2,1,0:T(8,128)} %param.24) | copy-start | bytes 6291460
  612.8 9.6 %copy-start.54 = (f32[1,768]{1,0:T(1,128)}, f32[1,768]{1,0:T(1,128)S(1)}, u32[]{:S(2)}) copy-start(f32[1,768]{1,0:T(1,128)S(1)} %broadcast_in_dim_reshape.3) | copy-start | bytes 9220
  613.7 10.3 %collective-permute-start.3 = (bf16[64,3072]{1,0:T(8,128)(2,1)S(1)}, bf16[64,3072]{1,0:T(8,128)(2,1)S(1)}, u32[]{:S(2)}, u32[]{:S(2)}) collective-permute-start(bf16[64,3072]{1,0:T(8,128)(2,1)S(1)} %get-tuple-element.105), channel_id=1, source_target_pairs={{0,16},{16,0},{1,17},{17,1},{2,18},{18,2},{3,19},{19,3},{4,20},{20... | collective-permute-start | bytes 1179656 | tf_op jit(solution)/shard_map/ppermute | solution.py:28
  614.8 8.3 %collective-permute-start.4 = (bf16[64,1024]{1,0:T(8,128)(2,1)S(1)}, bf16[64,1024]{1,0:T(8,128)(2,1)S(1)}, u32[]{:S(2)}, u32[]{:S(2)}) collective-permute-start(bf16[64,1024]{1,0:T(8,128)(2,1)S(1)} %get-tuple-element.110), channel_id=1, source_target_pairs={{0,16},{16,0},{1,17},{17,1},{2,18},{18,2},{3,19},{19,3},{4,20},{20... | collective-permute-start | bytes 393224 | tf_op jit(solution)/shard_map/ppermute | solution.py:28
  616.5 5.9 copy-start.62
  616.6 6.5 %copy-start.40 = (f32[64,1024]{1,0:T(8,128)S(1)}, f32[64,1024]{1,0:T(8,128)}, u32[]{:S(2)}) copy-start(f32[64,1024]{1,0:T(8,128)} %param.35) | copy-start | bytes 786436
  616.6 7.4 %copy-start.22 = (f32[64,3072]{1,0:T(8,128)S(1)}, f32[64,3072]{1,0:T(8,128)}, u32[]{:S(2)}) copy-start(f32[64,3072]{1,0:T(8,128)} %param.22) | copy-start | bytes 2359300
  616.6 7.4 %copy-start.37 = (f32[64,3072]{1,0:T(8,128)S(1)}, f32[64,3072]{1,0:T(8,128)}, u32[]{:S(2)}) copy-start(f32[64,3072]{1,0:T(8,128)} %param.34) | copy-start | bytes 2359300
  616.6 5.8 collective-permute-start.6
  622.4 3.3 copy-start.24
  (10 other events, 19.6 us)

commit v6 on v5

--- a/solution.py
+++ b/solution.py
@@ -1042,7 +1042,7 @@
     )
     projected_grad = jnp.concatenate([query_grad, key_grad, value_grad], axis=1)
     qkv_weight_grad = dot_tn(token_rows, projected_grad).astype(jnp.bfloat16)
-    projected_sums = jnp.sum(projected_grad.astype(jnp.float32), axis=0)
+    projected_sums = dot_nn(jnp.ones((16, local_rows), jnp.bfloat16), projected_grad)[0]
     vector_grad = jnp.concatenate(
         [
             projected_sums[:width],

time: 639 us -> 635 us (level)
  no operation moved by 1% of the time
where the time goes in v6:
time: 635 us; the launch traced here: 625 us
  Pallas kernels  476 us (75%)
  matrix products  63.9 us (10%)
  other arithmetic  54.5 us (9%)
  local copies, waits for them, and re-layouts  18.5 us (3%)
    pallas_call x1, Pallas kernels, attend_back(): pl.pallas_call(partial(attend_back_kernel, widths), name='attend_back', g...  99.4 us
    pallas_call x1, Pallas kernels, ffn_back(): pl.pallas_call(partial(ffn_back_kernel, widths), name='ffn_back', grid=(1...  91.5 us
    pallas_call x1, Pallas kernels, finish(): pl.pallas_call(partial(finish_kernel, widths), name='finish', grid=(16,),...  82.3 us
    pallas_call x1, Pallas kernels, attend(): pl.pallas_call(partial(attend_kernel, shared), name='attend', grid_spec=p...  79.1 us
    pallas_call x1, Pallas kernels, ffn_up(): pl.pallas_call(partial(ffn_up_kernel, shared), name='ffn_up', grid=(16,),...  56.2 us
    pallas_call x1, Pallas kernels, gather_all(): pl.pallas_call(partial(gather_kernel, shared), name='gather_all', in_spec...  53.5 us
    dot_general x3, matrix products, dot_tn(): lax.dot_general(a, b, (((0,), (0,)), ((), ())), preferred_element_type=jn...  24 us
    dot_general x1, matrix products, on_device(): jnp.dot(wide_tokens, full_qkv, preferred_element_type=jnp.float32)  17.3 us
  transfers between devices with their start and end apart: 7, of which 1 were waited for; matrix products, arithmetic and copies ran while one was open for 8% of the time, Pallas kernels for 24%

profile of v6, /device:TPU:0, one launch (start us, length us, event | category | flops | bytes accessed | tf_op | source)
XLA Modules:
  0.0 625.3 jit_solution(12958836971610793168)
XLA Ops:
  0.7 2.8 select_bitcast_fusion
  3.5 3.0 collective-permute-start
  6.5 1.9 convert_element_type.112.refs_0_
  8.5 0.6 pad.16.refs_1_
  9.2 53.5 %gather_all.1 = (bf16[4,2,2,64,3072]{4,3,2,1,0:T(8,128)(2,1)}, bf16[4,2,2,64,128]{4,3,2,1,0:T(8,128)(2,1)}) custom-call(bf16[64,3072]{1,0:T(8,128)(2,1)} %convert_element_type.112.refs_0_, bf16[64,128]{1,0:T(8,128)(2,1)} %pad.16.refs_1_), custom_call_target="tpu_custom_call" | custom-call | tf_op jit(solution)/shard_map/gather_all/pallas_call | solution.py:568
  62.7 1.0 slice_convert_fusion
  64.1 0.6 add_select_fusion
  64.7 1.7 convert_element_type.118
  66.5 1.0 reduce.3
  67.5 17.3 %add_convert_fusion.q_ref.k_ref.v_ref = bf16[1536,3072]{1,0:T(8,128)(2,1)} fusion(bf16[1024,3072]{1,0:T(8,128)(2,1)} %bitcast.98, f32[3072]{0:T(1024)S(1)} %pad_maximum_fusion.3, bf16[512,1024]{1,0:T(8,128)(2,1)} %collective-permute-done, bf16[1024,1024]{1,0:T(8,128)(2,1)} %bitcast.108, pred[]{:T(512)S(6)} %eq.16), kind=kOutput, calls=%fused_computation | convolution fusion | flops 9687269376 | bytes 18886656 | tf_op jit(solution)/shard_map/dot_general | solution.py:979
  85.1 79.1 %attend.1 = (bf16[1024,1024]{1,0:T(8,128)(2,1)S(1)}, f32[1024,1024]{1,0:T(8,128)}, f32[1024,128]{1,0:T(8,128)S(1)}, bf16[4,2,2,64,1024]{4,3,2,1,0:T(8,128)(2,1)S(1)}, bf16[4,2,2,64,4096]{4,3,2,1,0:T(8,128)(2,1)}) custom-call(s32[1536,128]{1,0:T(8,128)S(1)} %broadcast_in_dim.39.ids_col_ref, s32[8,1536]{1,0:T(8,128)S(1)} %broadcast_in_dim.40.ids_row_ref, ...), custom_call_target="tpu_custom_call" | custom-call | flops 18253611008 | bytes 31457280 | tf_op jit(solution)/shard_map/attend/pallas_call | solution.py:152
  164.3 2.5 fusion.62
  166.8 0.5 multiply_reduce_fusion.3
  167.4 0.7 fusion.7.x_ref
  168.2 56.2 %ffn_up.1 = (bf16[1024,4096]{1,0:T(8,128)(2,1)}, bf16[1024,4096]{1,0:T(8,128)(2,1)}, bf16[4,2,2,64,4096]{4,3,2,1,0:T(8,128)(2,1)}) custom-call(bf16[1024,1024]{1,0:T(8,128)(2,1)S(1)} %fusion.7.x_ref, bf16[1024,4096]{1,0:T(8,128)(2,1)} %bitcast.114, f32[8,4096]{1,0:T(8,128)S(1)} %broadcast_in_dim.42.bias_ref, bf16[64,4096]{1,0:T(8,128)(2,1)S(1)} %get-tuple-element.110.refs_0_), custom_call_target="tpu_custom_call" | custom-call | flops 8589934592 | bytes 41943040 | tf_op jit(solution)/shard_map/ffn_up/pallas_call | solution.py:767
  224.5 14.5 %fusion.63 = (f32[1024]{0:T(1024)S(1)}, f32[1024,1024]{1,0:T(8,128)S(1)}) fusion(f32[1024]{0:T(1024)S(1)} %get-tuple-element.123, bf16[1024,4096]{1,0:T(8,128)(2,1)} %get-tuple-element.55, bf16[1024,4096]{1,0:T(8,128)(2,1)} %bitcast.117, f32[1024]{0:T(1024)S(1)} %get-tuple-element.124, f32[1024]{0:T(1024)S(1)} %get-tuple-element.125, ...), kind=kOutput, calls=%fused_computation.155 | convolution fusion | flops 8597273600 | bytes 25190400 | tf_op jit(solution)/shard_map/dot_general | solution.py:993
  238.9 0.5 multiply_reduce_fusion.2
  239.5 2.5 fusion.3
  242.1 3.5 fusion.57
  245.6 1.9 copy-done.13
  247.6 1.0 fusion.55
  248.6 11.2 %convolution_convert_fusion = bf16[1024,4096]{1,0:T(8,128)(2,1)} fusion(bf16[1024,1024]{1,0:T(8,128)(2,1)S(1)} %get-tuple-element.94.dz_ref, bf16[1024,4096]{1,0:T(8,128)(2,1)S(1)} %bitcast.121), kind=kOutput, calls=%fused_computation.1 | convolution fusion | flops 8594128896 | bytes 18874368 | tf_op jit(solution)/shard_map/dot_general | solution.py:59
  259.8 91.5 %ffn_back.1 = (bf16[1024,4096]{1,0:T(8,128)(2,1)}, f32[8,4096]{1,0:T(8,128)}, f32[1024,1024]{1,0:T(8,128)}, f32[64,4096]{1,0:T(8,128)}) custom-call(bf16[1024,1024]{1,0:T(8,128)(2,1)} %copy-done.30, bf16[1024,4096]{1,0:T(8,128)(2,1)} %bitcast.118, bf16[1024,4096]{1,0:T(8,128)(2,1)} %get-tuple-element.57.slope_ref, bf16[1024,1024]{1,0:T(8,128)(2,1)} %copy-done.2, ...), custom_call_target="tpu_custom_call" | custom-call | flops 25769803776 | bytes 62914560 | tf_op jit(solution)/shard_map/ffn_back/pallas_call | solution.py:834
  351.4 6.4 %multiply_reduce_fusion = (bf16[1024]{0:T(1024)(128)(2,1)}, f32[1024]{0:T(1024)S(1)}, bf16[1024]{0:T(1024)(128)(2,1)}, f32[1024,1024]{1,0:T(8,128)S(1)}) fusion(f32[1024,1024]{1,0:T(8,128)} %copy-done.11, f32[1024]{0:T(1024)} %copy-done.46, f32[1024]{0:T(1024)} %copy-done.42, f32[1024]{0:T(1024)} %copy-done.44, f32[1024,1024]{1,0:T(8,128)} %get-tuple-element.58, ...), kind=kLoop, calls=%fused_computation.11 | loop fusion | flops 10482688 | bytes 16801792 | tf_op jit(solution)/shard_map/transpose(jvp())/reduce_sum | solution.py:35
  357.8 1.9 fusion.56
  359.7 1.0 convert_reduce_fusion
  360.7 0.6 copy-done.8
  361.3 2.4 convolution_convert_fusion.4.do_ref
  363.7 1.2 slice_select_fusion
  365.0 2.3 fusion.4.inner_ref
  367.3 1.0 fusion.59
  368.3 0.8 fusion.58
  369.1 99.4 %attend_back.1 = (bf16[1024,1024]{1,0:T(8,128)(2,1)}, f32[1024,1024]{1,0:T(8,128)}, f32[1024,1024]{1,0:T(8,128)}, f32[64,4096]{1,0:T(8,128)}) custom-call(s32[1536,128]{1,0:T(8,128)} %copy-done, s32[8,1536]{1,0:T(8,128)} %copy-done.5, bf16[1536,3072]{1,0:T(8,128)(2,1)} %add_convert_fusion.q_ref.k_ref.v_ref, ...), custom_call_target="tpu_custom_call" | custom-call | flops 45634027520 | bytes 41943040 | tf_op jit(solution)/shard_map/attend_back/pallas_call | solution.py:275
  468.5 0.7 collective-permute-start.1
  469.2 1.2 slice_select_fusion.1
  470.6 1.5 collective-permute-start.2
  472.1 6.8 %fusion.21 = (bf16[2,64,4096]{2,1,0:T(8,128)(2,1)}, f32[1,2,64,4096]{3,2,1,0:T(8,128)}) fusion(f32[2,64,4096]{2,1,0:T(8,128)} %param.24, f32[1,2,64,4096]{3,2,1,0:T(8,128)} %param.32, f32[1,2,64,4096]{3,2,1,0:T(8,128)} %param.28, f32[1,64,4096]{2,1,0:T(8,128)} %bitcast.102, f32[1,64,4096]{2,1,0:T(8,128)} %bitcast.104), kind=kLoop, calls=%fused_computation.43 | loop fusion | flops 9437184 | bytes 11534336 | tf_op jit(solution)/shard_map/convert_element_type | solution.py:1074
  479.0 2.9 fusion.14
  482.0 1.2 copy-done.18
  483.3 0.8 copy-done.10
  484.1 3.8 convolution_convert_fusion.3
  487.9 0.9 fusion.34
  488.8 4.0 collective-permute-done.2
  493.1 14.5 %attend_far.1 = (bf16[1024,1024]{1,0:T(8,128)(2,1)S(1)}, bf16[1024,1024]{1,0:T(8,128)(2,1)}) custom-call(s32[1]{0:T(128)} %bitcast.13.side_ref, s32[1536,128]{1,0:T(8,128)S(1)} %copy-done.1, s32[8,1536]{1,0:T(8,128)S(1)} %copy-done.6, bf16[1536,3072]{1,0:T(8,128)(2,1)} %add_convert_fusion.q_ref.k_ref.v_ref, ...), custom_call_target="tpu_custom_call" | custom-call | flops 8589934592 | bytes 20971520 | tf_op jit(solution)/shard_map/attend_far/pallas_call | solution.py:366
  507.7 1.4 copy-done.35
  509.3 0.5 copy-done.33
  509.7 9.0 %convolution_convert_fusion.1 = bf16[3072,1024]{0,1:T(8,128)(2,1)} fusion(bf16[1024,3072]{1,0:T(8,128)(2,1)S(1)} %constant_dynamic-update-slice_fusion.grad_ref, bf16[1,1024,1024]{2,1,0:T(8,128)(2,1)S(1)} %copy-done.33), kind=kOutput, calls=%fused_computation.4 | convolution fusion | flops 6445596672 | bytes 14680064 | tf_op jit(solution)/shard_map/dot_general | solution.py:59
  518.8 0.9 convolution_convert_fusion.2
  520.0 0.6 reshape.360
  520.6 0.8 pad.19
  521.3 82.3 %finish.1 = (f32[1024,1024]{1,0:T(8,128)}, f32[64,3072]{1,0:T(8,128)}, f32[64,128]{1,0:T(8,128)}, f32[64,1024]{1,0:T(8,128)}) custom-call(f32[1024,1024]{1,0:T(8,128)} %copy-done.17, bf16[1024,3072]{1,0:T(8,128)(2,1)} %copy-done.14, bf16[1024,3072]{1,0:T(8,128)(2,1)} %bitcast.99, bf16[4,2,2,64,3072]{4,3,2,1,0:T(8,128)(2,1)} %bitcast.100, ...), custom_call_target="tpu_custom_call" | custom-call | flops 6442450944 | bytes 31457280 | tf_op jit(solution)/shard_map/finish/pallas_call | solution.py:890
  603.7 3.7 fusion.26
  607.5 0.9 broadcast_in_dim_reshape.3
  608.4 0.9 reshape.363
  609.3 1.0 fusion.28
  610.3 0.5 collective-permute-start.4
  610.8 1.3 multiply_reduce_fusion.5
  612.3 5.7 multiply_subtract_fusion
  618.0 0.6 multiply_subtract_fusion.3
  618.6 1.0 multiply_subtract_fusion.2
  619.6 1.7 multiply_subtract_fusion.1
  621.2 2.0 copy.84
  623.3 0.9 copy.85
  624.1 0.7 copy.86
  (176 shorter events, 2.4 us)
Async XLA Ops:
  0.7 7.7 %copy-start.49 = (f32[768]{0:T(1024)S(1)}, f32[768]{0:T(1024)}, u32[]{:S(2)}) copy-start(f32[768]{0:T(1024)} %param.25) | copy-start | bytes 9220
  0.7 64.0 %copy-start.28 = (f32[64,1024]{1,0:T(8,128)S(1)}, f32[64,1024]{1,0:T(8,128)}, u32[]{:S(2)}) copy-start(f32[64,1024]{1,0:T(8,128)} %param.23) | copy-start | bytes 786436
  0.7 65.7 %copy-start.61 = (s32[1,2048]{1,0:T(1,128)S(1)}, s32[1,2048]{1,0:T(1,128)}, u32[]{:S(2)}) copy-start(s32[1,2048]{1,0:T(1,128)} %param.21) | copy-start | bytes 24580
  0.7 65.7 %copy-start.15 = (bf16[1,1024,1024]{2,1,0:T(8,128)(2,1)S(1)}, bf16[1,1024,1024]{2,1,0:T(8,128)(2,1)}, u32[]{:S(2)}) copy-start(bf16[1,1024,1024]{2,1,0:T(8,128)(2,1)} %param.20) | copy-start | bytes 6291460
  3.5 64.0 %collective-permute-start = (bf16[512,1024]{1,0:T(8,128)(2,1)}, bf16[512,1024]{1,0:T(8,128)(2,1)}, u32[]{:S(2)}, u32[]{:S(2)}) collective-permute-start(bf16[512,1024]{1,0:T(8,128)(2,1)} %select_bitcast_fusion), channel_id=1, source_target_pairs={{0,1},{1,0},{2,3},{3,2},{4,5},{5,4},{6,7},{7,6},{8,9},{9,8},{10,11... | collective-permute-start | bytes 3145736 | tf_op jit(solution)/shard_map/ppermute | solution.py:28
  64.0 20.8 %copy-start.41 = (f32[12288]{0:T(1024)}, f32[12288]{0:T(1024)S(1)}, u32[]{:S(2)}) copy-start(f32[12288]{0:T(1024)S(1)} %reshape.364) | copy-start | bytes 147460
  64.0 160.4 %copy-start.44 = (f32[1024]{0:T(1024)}, f32[1024]{0:T(1024)S(1)}, u32[]{:S(2)}) copy-start(f32[1024]{0:T(1024)S(1)} %get-tuple-element.125) | copy-start | bytes 12292
  85.1 79.2 %copy-start = (s32[1536,128]{1,0:T(8,128)}, s32[1536,128]{1,0:T(8,128)S(1)}, u32[]{:S(2)}) copy-start(s32[1536,128]{1,0:T(8,128)S(1)} %broadcast_in_dim.39.ids_col_ref) | copy-start | bytes 2359300
  85.1 79.2 %copy-start.5 = (s32[8,1536]{1,0:T(8,128)}, s32[8,1536]{1,0:T(8,128)S(1)}, u32[]{:S(2)}) copy-start(s32[8,1536]{1,0:T(8,128)S(1)} %broadcast_in_dim.40.ids_row_ref) | copy-start | bytes 147460
  85.1 79.2 %copy-start.32 = (bf16[1,1024,1024]{2,1,0:T(8,128)(2,1)S(1)}, bf16[1,1024,1024]{2,1,0:T(8,128)(2,1)}, u32[]{:S(2)}) copy-start(bf16[1,1024,1024]{2,1,0:T(8,128)(2,1)} %param.19) | copy-start | bytes 6291460
  164.3 2.5 copy-start.3
  164.3 2.5 copy-start.7
  164.3 2.5 copy-start.9
  166.8 57.6 %copy-start.11 = (f32[1024,1024]{1,0:T(8,128)}, f32[1024,1024]{1,0:T(8,128)S(1)}, u32[]{:S(2)}) copy-start(f32[1024,1024]{1,0:T(8,128)S(1)} %get-tuple-element.134) | copy-start | bytes 12582916
  166.8 57.6 %copy-start.42 = (f32[1024]{0:T(1024)}, f32[1024]{0:T(1024)S(1)}, u32[]{:S(2)}) copy-start(f32[1024]{0:T(1024)S(1)} %broadcast_multiply_fusion.1) | copy-start | bytes 12292
  167.4 57.0 %copy-start.51 = (f32[1024]{0:T(1024)}, f32[1024]{0:T(1024)S(1)}, u32[]{:S(2)}) copy-start(f32[1024]{0:T(1024)S(1)} %multiply_reduce_fusion.3) | copy-start | bytes 12292
  167.4 57.0 %copy-start.46 = (f32[1024]{0:T(1024)}, f32[1024]{0:T(1024)S(1)}, u32[]{:S(2)}) copy-start(f32[1024]{0:T(1024)S(1)} %fusion.47) | copy-start | bytes 12292
  168.2 56.2 %copy-start.2 = (bf16[1024,1024]{1,0:T(8,128)(2,1)}, bf16[1024,1024]{1,0:T(8,128)(2,1)S(1)}, u32[]{:S(2)}) copy-start(bf16[1024,1024]{1,0:T(8,128)(2,1)S(1)} %fusion.7.x_ref) | copy-start | bytes 6291460
  242.1 6.5 %slice-start.1 = ((s8[8388608]{0:T(1024)(128)(4,1)}), s8[4194304]{0:T(1024)(128)(4,1)S(1)}, s32[]{:S(2)}) async-start(s8[8388608]{0:T(1024)(128)(4,1)} %bitcast.120), calls=%async_computation.1 | async-start | bytes 8388608
  242.1 6.5 %slice-start.2 = ((s8[8388608]{0:T(1024)(128)(4,1)}), s8[4194304]{0:T(1024)(128)(4,1)S(1)}, s32[]{:S(2)}) async-start(s8[8388608]{0:T(1024)(128)(4,1)} %bitcast.120), calls=%async_computation.2 | async-start | bytes 8388608
  245.6 2.0 copy-start.13
  245.6 3.0 copy-start.48
  248.6 11.3 %copy-start.30 = (bf16[1024,1024]{1,0:T(8,128)(2,1)}, bf16[1024,1024]{1,0:T(8,128)(2,1)S(1)}, u32[]{:S(2)}) copy-start(bf16[1024,1024]{1,0:T(8,128)(2,1)S(1)} %get-tuple-element.94.dz_ref) | copy-start | bytes 6291460
  351.3 6.5 %copy-start.52 = (f32[1024]{0:T(1024)S(1)}, f32[1024]{0:T(1024)}, u32[]{:S(2)}) copy-start(f32[1024]{0:T(1024)} %copy-done.51) | copy-start | bytes 12292
  351.3 6.5 %copy-start.12 = (f32[1024,1024]{1,0:T(8,128)S(1)}, f32[1024,1024]{1,0:T(8,128)}, u32[]{:S(2)}) copy-start(f32[1024,1024]{1,0:T(8,128)} %copy-done.11) | copy-start | bytes 12582916
  351.3 6.5 %copy-start.43 = (f32[1024]{0:T(1024)S(1)}, f32[1024]{0:T(1024)}, u32[]{:S(2)}) copy-start(f32[1024]{0:T(1024)} %copy-done.42) | copy-start | bytes 12292
  351.3 6.5 %copy-start.45 = (f32[1024]{0:T(1024)S(1)}, f32[1024]{0:T(1024)}, u32[]{:S(2)}) copy-start(f32[1024]{0:T(1024)} %copy-done.44) | copy-start | bytes 12292
  351.4 6.5 %copy-start.47 = (f32[1024]{0:T(1024)S(1)}, f32[1024]{0:T(1024)}, u32[]{:S(2)}) copy-start(f32[1024]{0:T(1024)} %copy-done.46) | copy-start | bytes 12292
  360.7 3.0 copy-start.17
  361.3 3.7 copy-start.23
  361.3 3.7 copy-start.53
  363.7 3.6 copy-start.19
  365.0 3.3 copy-start.4
  468.5 24.5 %collective-permute-start.1 = (bf16[512,1024]{1,0:T(8,128)(2,1)}, bf16[512,1024]{1,0:T(8,128)(2,1)S(1)}, u32[]{:S(2)}, u32[]{:S(2)}) collective-permute-start(bf16[512,1024]{1,0:T(8,128)(2,1)} %slice_select_fusion), channel_id=1, source_target_pairs={{0,1},{1,0},{2,3},{3,2},{4,5},{5,4},{6,7},{7,6},{8,9},{9,8},{10,11... | collective-permute-start | bytes 3145736 | tf_op jit(solution)/shard_map/ppermute | solution.py:28
  470.6 22.2 %collective-permute-start.2 = (f32[512,32]{1,0:T(8,128)S(1)}, f32[512,32]{1,0:T(8,128)S(1)}, u32[]{:S(2)}, u32[]{:S(2)}) collective-permute-start(f32[512,32]{1,0:T(8,128)S(1)} %pad_maximum_fusion.2), channel_id=1, source_target_pairs={{0,1},{1,0},{2,3},{3,2},{4,5},{5,4},{6,7},{7,6},{8,9},{9,8},{10,11... | collective-permute-start | bytes 196616 | tf_op jit(solution)/shard_map/ppermute | solution.py:28
  472.1 6.8 %copy-start.20 = (f32[1,2,64,4096]{3,2,1,0:T(8,128)S(1)}, f32[1,2,64,4096]{3,2,1,0:T(8,128)}, u32[]{:S(2)}) copy-start(f32[1,2,64,4096]{3,2,1,0:T(8,128)} %param.32) | copy-start | bytes 6291460
  472.1 6.8 %copy-start.21 = (f32[1,2,64,4096]{3,2,1,0:T(8,128)S(1)}, f32[1,2,64,4096]{3,2,1,0:T(8,128)}, u32[]{:S(2)}) copy-start(f32[1,2,64,4096]{3,2,1,0:T(8,128)} %param.28) | copy-start | bytes 6291460
  472.1 6.8 %copy-start.25 = (f32[64,4096]{1,0:T(8,128)S(1)}, f32[64,4096]{1,0:T(8,128)}, u32[]{:S(2)}) copy-start(f32[64,4096]{1,0:T(8,128)} %get-tuple-element.72) | copy-start | bytes 3145732
  472.1 6.8 %copy-start.26 = (f32[64,4096]{1,0:T(8,128)S(1)}, f32[64,4096]{1,0:T(8,128)}, u32[]{:S(2)}) copy-start(f32[64,4096]{1,0:T(8,128)} %get-tuple-element.71) | copy-start | bytes 3145732
  478.9 133.4 %collective-permute-start.5 = (bf16[2,64,4096]{2,1,0:T(8,128)(2,1)}, bf16[2,64,4096]{2,1,0:T(8,128)(2,1)}, u32[]{:S(2)}, u32[]{:S(2)}) collective-permute-start(bf16[2,64,4096]{2,1,0:T(8,128)(2,1)} %get-tuple-element.103), channel_id=1, source_target_pairs={{0,16},{16,0},{1,17},{17,1},{2,18},{18,2},{3,19},{19,3},{4,20},{20... | collective-permute-start | bytes 3145736 | tf_op jit(solution)/shard_map/ppermute | solution.py:28
  478.9 2.9 copy-start.34
  479.0 4.3 copy-start.18
  481.9 2.2 copy-start.10
  484.1 9.0 %copy-start.1 = (s32[1536,128]{1,0:T(8,128)S(1)}, s32[1536,128]{1,0:T(8,128)}, u32[]{:S(2)}) copy-start(s32[1536,128]{1,0:T(8,128)} %copy-done) | copy-start | bytes 2359300
  484.1 9.0 %copy-start.6 = (s32[8,1536]{1,0:T(8,128)S(1)}, s32[8,1536]{1,0:T(8,128)}, u32[]{:S(2)}) copy-start(s32[8,1536]{1,0:T(8,128)} %copy-done.5) | copy-start | bytes 147460
  507.5 2.2 copy-start.33
  509.7 9.0 %copy-start.14 = (bf16[1024,3072]{1,0:T(8,128)(2,1)}, bf16[1024,3072]{1,0:T(8,128)(2,1)S(1)}, u32[]{:S(2)}) copy-start(bf16[1024,3072]{1,0:T(8,128)(2,1)S(1)} %constant_dynamic-update-slice_fusion.grad_ref) | copy-start | bytes 18874372
  603.7 5.6 copy-start.29
  603.7 5.6 copy-start.36
  603.7 5.6 copy-start.38
  603.7 5.6 copy-start.39
  603.7 7.1 %copy-start.63 = (f32[1,768]{1,0:T(1,128)S(1)}, f32[1,768]{1,0:T(1,128)}, u32[]{:S(2)}) copy-start(f32[1,768]{1,0:T(1,128)} %param.29) | copy-start | bytes 9220
  603.7 8.4 %copy-start.50 = (f32[768]{0:T(1024)S(1)}, f32[768]{0:T(1024)}, u32[]{:S(2)}) copy-start(f32[768]{0:T(1024)} %param.25) | copy-start | bytes 9220
  603.7 8.5 %copy-start.16 = (f32[2,64,4096]{2,1,0:T(8,128)S(1)}, f32[2,64,4096]{2,1,0:T(8,128)}, u32[]{:S(2)}) copy-start(f32[2,64,4096]{2,1,0:T(8,128)} %param.24) | copy-start | bytes 6291460
  608.4 9.6 %copy-start.54 = (f32[1,768]{1,0:T(1,128)}, f32[1,768]{1,0:T(1,128)S(1)}, u32[]{:S(2)}) copy-start(f32[1,768]{1,0:T(1,128)S(1)} %broadcast_in_dim_reshape.3) | copy-start | bytes 9220
  609.2 10.3 %collective-permute-start.3 = (bf16[64,3072]{1,0:T(8,128)(2,1)S(1)}, bf16[64,3072]{1,0:T(8,128)(2,1)S(1)}, u32[]{:S(2)}, u32[]{:S(2)}) collective-permute-start(bf16[64,3072]{1,0:T(8,128)(2,1)S(1)} %get-tuple-element.107), channel_id=1, source_target_pairs={{0,16},{16,0},{1,17},{17,1},{2,18},{18,2},{3,19},{19,3},{4,20},{20... | collective-permute-start | bytes 1179656 | tf_op jit(solution)/shard_map/ppermute | solution.py:28
  610.3 8.3 %collective-permute-start.4 = (bf16[64,1024]{1,0:T(8,128)(2,1)S(1)}, bf16[64,1024]{1,0:T(8,128)(2,1)S(1)}, u32[]{:S(2)}, u32[]{:S(2)}) collective-permute-start(bf16[64,1024]{1,0:T(8,128)(2,1)S(1)} %get-tuple-element.112), channel_id=1, source_target_pairs={{0,16},{16,0},{1,17},{17,1},{2,18},{18,2},{3,19},{19,3},{4,20},{20... | collective-permute-start | bytes 393224 | tf_op jit(solution)/shard_map/ppermute | solution.py:28
  612.1 5.9 copy-start.62
  612.1 6.5 %copy-start.40 = (f32[64,1024]{1,0:T(8,128)S(1)}, f32[64,1024]{1,0:T(8,128)}, u32[]{:S(2)}) copy-start(f32[64,1024]{1,0:T(8,128)} %param.35) | copy-start | bytes 786436
  612.1 7.4 %copy-start.22 = (f32[64,3072]{1,0:T(8,128)S(1)}, f32[64,3072]{1,0:T(8,128)}, u32[]{:S(2)}) copy-start(f32[64,3072]{1,0:T(8,128)} %param.22) | copy-start | bytes 2359300
  612.1 7.4 %copy-start.37 = (f32[64,3072]{1,0:T(8,128)S(1)}, f32[64,3072]{1,0:T(8,128)}, u32[]{:S(2)}) copy-start(f32[64,3072]{1,0:T(8,128)} %param.34) | copy-start | bytes 2359300
  612.2 5.8 collective-permute-start.6
  618.0 3.3 copy-start.24
  621.2 2.0 copy-start.27
  (10 other events, 12.4 us)
